TPU v7x, 32 devices: a whole 2x2x4 slice. The times are simulated.
32 devices in a mesh: groups: 2 (over y), seq: 4 (over z), hid: 2 (over x), sub: 2 (over core).
Axes of the slice: x: 2, y: 2, z: 4, core: 2. Of those that a mesh axis runs over, the one named last changes fastest.
Arguments:
- z_mix: bfloat16 [16384, 768], P(('groups', 'seq', 'sub')), parts along dimension 0, may hold values from -6 to 6
- z_ffn: bfloat16 [16384, 768], P(('groups', 'seq', 'sub')), parts along dimension 0, may hold values from -6 to 6
- pre_act: bfloat16 [16384, 3072], P(('groups', 'seq', 'sub'), 'hid'), parts along dimension 0, may hold values from -6 to 6
- grad_out: bfloat16 [16384, 768], P(('groups', 'seq', 'sub')), parts along dimension 0, may hold values from -6 to 6
- gain_mix: float32 [768], replicated, may hold values from 0.1 to 1.9
- gain_ffn: float32 [768], replicated, may hold values from 0.1 to 1.9
- w_in: bfloat16 [768, 3072], P(('seq', 'sub'), 'hid'), may hold values from -0.21875 to 0.21875
- w_out: bfloat16 [768, 3072], P(('seq', 'sub'), 'hid'), may hold values from -0.109375 to 0.109375
Outputs:
- grad_in: float32 [16384, 768], P(('groups', 'seq', 'sub'), 'hid'), parts along dimension 0
- grad_w_in: float32 [1536, 3072], P(('groups', 'seq', 'sub'), 'hid'), parts along dimension 0
- grad_w_out: float32 [1536, 3072], P(('groups', 'seq', 'sub'), 'hid'), parts along dimension 0
There are 2 independent parts, one for each index of `groups`. A program takes and returns all parts, laid end to end along the dimension named above; an argument that names none is the same for every part. Nothing has to cross between parts.
All inputs are finite; a program needn't handle non-finite values.
Results may differ from a plain program's by a relative error of at most 0.014.
Values may be sent and summed in bfloat16 or wider, within the bound.
No kernel may reach another device: no remote copies, remote signals or barrier semaphores. Data moves between devices by JAX's collectives and lax.ppermute only.
A program may use at most 64 MiB of HBM per device.

v0:
```python
import math

import jax
import jax.numpy as jnp
from jax import lax
from jax.sharding import PartitionSpec as P

epsilon = 1e-05


def norm_parts(values):
    values = values.astype(jnp.float32)
    row_mean = jnp.mean(values, axis=-1, keepdims=True)
    centred = values - row_mean
    inv_std = lax.rsqrt(jnp.mean(centred * centred, axis=-1, keepdims=True) + epsilon)
    return (centred * inv_std, inv_std)


def norm_backward(values, gain_vec, upstream):
    unit_rows, inv_std = norm_parts(values)
    scaled = upstream * gain_vec
    return inv_std * (
        scaled
        - jnp.mean(scaled, axis=-1, keepdims=True)
        - unit_rows * jnp.mean(scaled * unit_rows, axis=-1, keepdims=True)
    )


def gelu_tanh(values):
    return jax.nn.gelu(values, approximate=True)


def exact_dot(left, right):
    return jnp.dot(left, right, precision=lax.Precision.HIGHEST, preferred_element_type=jnp.float32)


def angle_table(row_ids, col_ids, period):
    products = row_ids[:, None] * col_ids[None, :] % period
    angles = 2.0 * math.pi / period * products.astype(jnp.float32)
    return (jnp.cos(angles), jnp.sin(angles))


def local(z_mix, z_ffn, pre_act, grad_out, gain_mix, gain_ffn, w_in, w_out):
    tok_rows = z_mix.shape[0]
    feat_width = z_mix.shape[1]
    unit_count = pre_act.shape[1]
    hid_count = lax.axis_size("hid")
    hid_index = lax.axis_index("hid")
    span_count = lax.axis_size(("seq", "sub"))
    place_idx = lax.axis_index(("seq", "sub"))
    col_count = feat_width // hid_count
    seq_length = tok_rows * span_count
    quota = tok_rows // span_count
    normed = (norm_parts(z_mix)[0] * gain_mix).astype(jnp.bfloat16)
    ffn_grad = norm_backward(z_ffn, gain_ffn, grad_out.astype(jnp.float32))
    ffn_low = ffn_grad.astype(jnp.bfloat16)
    pre_wide = pre_act.astype(jnp.float32)
    activation = gelu_tanh(pre_wide).astype(jnp.bfloat16)
    _, pull_back = jax.vjp(gelu_tanh, pre_wide)
    contract_units = (((1,), (1,)), ((), ()))
    contract_rows = (((0,), (0,)), ((), ()))
    act_grad = jnp.dot(
        ffn_low,
        lax.all_gather(w_out, ("seq", "sub"), axis=0, tiled=True),
        preferred_element_type=jnp.float32,
    )
    pre_grad = pull_back(act_grad)[0].astype(jnp.bfloat16)
    partial_sum = lax.dot_general(
        pre_grad,
        lax.all_gather(w_in, ("seq", "sub"), axis=0, tiled=True),
        contract_units,
        preferred_element_type=jnp.float32,
    )
    both_grads = lax.psum_scatter(
        jnp.concatenate(
            [
                lax.dot_general(
                    normed, pre_grad, contract_rows, preferred_element_type=jnp.float32
                ),
                lax.dot_general(
                    ffn_low, activation, contract_rows, preferred_element_type=jnp.float32
                ),
            ],
            axis=1,
        ).astype(jnp.bfloat16),
        ("seq", "sub"),
        scatter_dimension=0,
        tiled=True,
    ).astype(jnp.float32)
    grad_w_in = both_grads[:, :unit_count]
    grad_w_out = both_grads[:, unit_count:]
    feat_ids = jnp.arange(feat_width, dtype=jnp.int32)
    summed = lax.psum(partial_sum.astype(jnp.bfloat16), "hid").astype(jnp.float32)
    mix_grad = norm_backward(z_mix, gain_mix, ffn_grad + summed)
    own_ids = hid_index * col_count + jnp.arange(col_count, dtype=jnp.int32)
    cos_hid, sin_hid = angle_table(feat_ids, own_ids, feat_width)
    own_cols = lax.dynamic_slice_in_dim(mix_grad, hid_index * col_count, col_count, 1)
    spectral = jnp.stack([exact_dot(mix_grad, cos_hid), exact_dot(mix_grad, sin_hid)])
    gathered = lax.all_to_all(
        spectral.astype(jnp.bfloat16), ("seq", "sub"), split_axis=1, concat_axis=1, tiled=True
    ).astype(spectral.dtype)
    gathered = gathered.reshape(2, span_count, quota, col_count)
    span_ids = jnp.arange(span_count, dtype=jnp.int32)
    cos_span, sin_span = angle_table(span_ids, span_ids, span_count)
    exact = lax.Precision.HIGHEST
    first_real = jnp.einsum("kr,rqc->kqc", cos_span, gathered[0], precision=exact) - jnp.einsum(
        "kr,rqc->kqc", sin_span, gathered[1], precision=exact
    )
    first_imag = jnp.einsum("kr,rqc->kqc", sin_span, gathered[0], precision=exact) + jnp.einsum(
        "kr,rqc->kqc", cos_span, gathered[1], precision=exact
    )
    local_pos = place_idx * quota + jnp.arange(quota, dtype=jnp.int32)
    cos_twist, sin_twist = angle_table(span_ids, local_pos, seq_length)
    cos_twist = cos_twist[:, :, None]
    sin_twist = sin_twist[:, :, None]
    twisted = jnp.stack(
        [
            first_real * cos_twist - first_imag * sin_twist,
            first_real * sin_twist + first_imag * cos_twist,
        ]
    )
    spread = lax.all_to_all(
        twisted.astype(jnp.bfloat16), ("seq", "sub"), split_axis=1, concat_axis=2, tiled=True
    ).astype(twisted.dtype)
    spread = spread.reshape(2, tok_rows, col_count)
    out_order = jnp.arange(tok_rows, dtype=jnp.int32)
    freq_ids = quota * (out_order % span_count) + out_order // span_count
    cos_seq, sin_seq = angle_table(freq_ids, out_order, tok_rows)
    real_out = exact_dot(cos_seq, spread[0]) - exact_dot(sin_seq, spread[1])
    returned = lax.all_to_all(
        real_out.reshape(quota, span_count, col_count).astype(jnp.bfloat16),
        ("seq", "sub"),
        split_axis=1,
        concat_axis=1,
        tiled=True,
    ).astype(jnp.float32)
    returned = returned.reshape(tok_rows, col_count)
    grad_in = own_cols + returned * (1.0 / math.sqrt(seq_length * feat_width))
    return (grad_in, grad_w_in, grad_w_out)


def solution(mesh):
    in_specs = (
        P(("groups", "seq", "sub"), None),
        P(("groups", "seq", "sub"), None),
        P(("groups", "seq", "sub"), "hid"),
        P(("groups", "seq", "sub"), None),
        P(),
        P(),
        P(("seq", "sub"), "hid"),
        P(("seq", "sub"), "hid"),
    )
    out_specs = (
        P(("groups", "seq", "sub"), "hid"),
        P(("groups", "seq", "sub"), "hid"),
        P(("groups", "seq", "sub"), "hid"),
    )
    return jax.shard_map(local, mesh=mesh, in_specs=in_specs, out_specs=out_specs, check_vma=False)
```

profile of v0, /device:TPU:1, one launch (start us, length us, event | category | flops | bytes accessed | tf_op | source)
XLA Modules:
  0.0 367.2 jit_solution(12904754999118727706)
XLA Ops:
  7.2 0.7 all-gather.3.cloned.1.call-update
  8.0 0.7 all-gather.5.cloned.1.call-update
  8.7 0.0 all-reduce.2.cloned.1.call-start
  8.7 1.7 convert_reduce_fusion
  10.4 0.6 fusion.32
  11.1 1.2 fusion.42
  12.2 31.6 %all-gather.3.cloned.1.call-done = bf16[768,1536]{1,0:T(8,128)(2,1)} async-done(((bf16[96,1536]{1,0:T(8,128)(2,1)}), bf16[768,1536]{1,0:T(8,128)(2,1)}) %all-gather.3.cloned.1.call-update) | async-done | bytes 2359312 | tf_op jit(solution)/shard_map/all_gather | solution.py:64
  43.8 9.5 %fusion.3 = bf16[1024,1536]{1,0:T(8,128)(2,1)} fusion(bf16[1024,1536]{1,0:T(8,128)(2,1)} %param.10, bf16[768,1536]{1,0:T(8,128)(2,1)} %all-gather.3.cloned.1.call-done, bf16[1024,768]{1,0:T(8,128)(2,1)S(1)} %copy-done, bf16[1024,768]{1,0:T(8,128)(2,1)S(1)} %copy-done.4, f32[1024]{0:T(1024)S(1)} %get-tuple-element.18, f32[1024]{0:T(1024)S(1)} %get-tuple-element.19, ...), kind=kOutput, calls=%fused_computation.8 | convolution fusion | flops 2456813568 | bytes 11815936 | tf_op jit(solution)/shard_map/dot_general | solution.py:62
  53.3 23.0 %all-gather.5.cloned.1.call-done = bf16[768,1536]{1,0:T(8,128)(2,1)} async-done(((bf16[96,1536]{1,0:T(8,128)(2,1)}), bf16[768,1536]{1,0:T(8,128)(2,1)}) %all-gather.5.cloned.1.call-update) | async-done | bytes 2359312 | tf_op jit(solution)/shard_map/all_gather | solution.py:70
  76.2 6.4 %convolution_convert_fusion.2 = bf16[1024,768]{1,0:T(8,128)(2,1)} fusion(bf16[1024,1536]{1,0:T(8,128)(2,1)} %fusion.3, bf16[768,1536]{1,0:T(8,128)(2,1)} %all-gather.5.cloned.1.call-done), kind=kOutput, calls=%fused_computation.61 | convolution fusion | flops 2416705536 | bytes 7077888 | tf_op jit(solution)/shard_map/dot_general | solution.py:68
  82.7 0.3 convert_reduce_fusion.1
  83.0 0.6 fusion.37
  83.6 49.4 %all-reduce.2.cloned.1.call-done = bf16[1024,768]{1,0:T(8,128)(2,1)} async-done(((bf16[1024,768]{1,0:T(8,128)(2,1)}), bf16[1024,768]{1,0:T(8,128)(2,1)}) %all-reduce.2.cloned.1.call-update) | async-done | bytes 1572880 | tf_op jit(solution)/shard_map/psum | solution.py:93
  133.0 3.8 %fusion.154 = (f32[1024]{0:T(1024)S(1)}, f32[1024]{0:T(1024)S(1)}, f32[1024,768]{1,0:T(8,128)S(1)}) fusion(f32[1024]{0:T(1024)S(1)} %add_rsqrt_fusion.1, f32[1024]{0:T(1024)S(1)} %broadcast_multiply_fusion.5, bf16[1024,768]{1,0:T(8,128)(2,1)S(1)} %copy-done.1, f32[768]{0:T(1024)S(1)} %copy-done.6, bf16[1024,768]{1,0:T(8,128)(2,1)} %all-reduce.2.cloned.1.call-done, ...), kind=kLoop, calls=%fused_computation.185 | loop fusion | flops 14153728 | bytes 9476096 | tf_op jit(solution)/shard_map/reduce_sum | solution.py:24
  136.8 1.3 fusion.35
  138.1 9.5 %fusion.56 = bf16[1,1024,384]{2,1,0:T(8,128)(2,1)S(1)} fusion(f32[1024,768]{1,0:T(8,128)S(1)} %fusion.35, s32[384]{0:T(512)S(1)} %iota_add_fusion), kind=kOutput, calls=%fused_computation.78 | convolution fusion | flops 3626926080 | bytes 3933696 | tf_op jit(solution)/shard_map/dot_general | solution.py:34
  147.6 10.0 %fusion.55 = bf16[1,1024,384]{2,1,0:T(8,128)(2,1)S(1)} fusion(f32[1024,768]{1,0:T(8,128)S(1)} %fusion.35, s32[384]{0:T(512)S(1)} %iota_add_fusion), kind=kOutput, calls=%fused_computation.77 | convolution fusion | flops 3626926080 | bytes 3933696 | tf_op jit(solution)/shard_map/dot_general | solution.py:34
  157.6 0.2 pad_maximum_fusion.1
  157.8 2.8 copy.39
  160.5 5.3 %all-to-all-start = ((bf16[2,1024,384]{2,0,1:T(2,128)(2,1)}), bf16[2,1024,384]{2,0,1:T(2,128)(2,1)}, u32[]{:S(2)}, u32[]{:S(2)}) async-start(bf16[2,1024,384]{2,0,1:T(2,128)(2,1)} %copy.39), calls=%async_computation | async-start | bytes 3145728 | tf_op jit(solution)/shard_map/all_to_all | solution.py:99
  165.8 0.2 reduce-scatter.2.cloned.1.call-start
  166.0 6.7 %convolution_convert_fusion = bf16[768,1536]{1,0:T(8,128)(2,1)S(1)} fusion(bf16[1024,1536]{1,0:T(8,128)(2,1)} %param.10, bf16[1024,768]{1,0:T(8,128)(2,1)S(1)} %copy-done, bf16[1024,768]{1,0:T(8,128)(2,1)} %param.11, f32[1024]{0:T(1024)S(1)} %get-tuple-element.18, f32[1024]{0:T(1024)S(1)} %get-tuple-element.19, f32[768]{0:T(1024)S(1)} %copy-done.5, ...), kind=kOutput, calls=%fused_computation.42 | convolution fusion | flops 2440691712 | bytes 8670208 | tf_op jit(solution)/shard_map/dot_general | solution.py:80
  172.7 3.2 convolution_convert_fusion.1
  175.9 2.7 pad_maximum_fusion
  178.7 0.1 fusion.108
  178.7 0.1 copy.44
  178.8 0.1 copy.47
  178.9 37.7 %all-to-all-done = bf16[2,1024,384]{2,0,1:T(2,128)(2,1)} async-done(((bf16[2,1024,384]{2,0,1:T(2,128)(2,1)}), bf16[2,1024,384]{2,0,1:T(2,128)(2,1)}, u32[]{:S(2)}, u32[]{:S(2)}) %all-to-all-start) | async-done | bytes 1572896 | tf_op jit(solution)/shard_map/all_to_all | solution.py:99
  216.6 4.3 %fusion.156 = (bf16[1,1024,384]{2,0,1:T(2,128)(2,1)S(1)}, bf16[1,1024,384]{2,0,1:T(2,128)(2,1)S(1)}) fusion(bf16[2,1024,384]{2,0,1:T(2,128)(2,1)} %all-to-all-done), kind=kLoop, calls=%fused_computation.187 | loop fusion | bytes 3145728 | tf_op jit(solution)/shard_map/slice | solution.py:107
  220.9 0.1 copy.54
  221.1 0.1 copy.53
  221.2 1.0 fusion.70
  222.2 1.1 fusion.72
  223.3 1.1 convolution_add_fusion
  224.4 1.5 fusion.66
  226.0 0.2 pad_maximum_fusion.2
  226.1 1.4 copy.48
  227.5 8.6 %all-to-all-start.1 = ((bf16[2,8,128,384]{3,2,0,1:T(8,128)(2,1)}), bf16[2,8,128,384]{3,2,0,1:T(8,128)(2,1)S(1)}, u32[]{:S(2)}, u32[]{:S(2)}) async-start(bf16[2,8,128,384]{3,2,0,1:T(8,128)(2,1)} %copy.48), calls=%async_computation.1 | async-start | bytes 3145728 | tf_op jit(solution)/shard_map/all_to_all | solution.py:122
  236.1 45.0 %all-to-all-done.1 = bf16[2,8,128,384]{3,2,0,1:T(8,128)(2,1)S(1)} async-done(((bf16[2,8,128,384]{3,2,0,1:T(8,128)(2,1)}), bf16[2,8,128,384]{3,2,0,1:T(8,128)(2,1)S(1)}, u32[]{:S(2)}, u32[]{:S(2)}) %all-to-all-start.1) | async-done | bytes 1572896 | tf_op jit(solution)/shard_map/all_to_all | solution.py:122
  281.1 0.2 fusion.155
  281.3 23.8 %fusion.13 = f32[1024,384]{1,0:T(8,128)S(1)} fusion(bf16[1024,384]{1,0:T(8,128)(2,1)S(1)} %bitcast.45, s32[1024]{0:T(1024)S(1)} %fusion.88), kind=kOutput, calls=%fused_computation.22 | convolution fusion | flops 4846518272 | bytes 2363392 | tf_op jit(solution)/shard_map/dot_general | solution.py:34
  305.1 23.7 %fusion.52 = bf16[128,8,384]{2,1,0:T(8,128)(2,1)S(1)} fusion(f32[1024,384]{1,0:T(8,128)S(1)} %fusion.13, bf16[1024,384]{1,0:T(8,128)(2,1)S(1)} %bitcast.44, s32[1024]{0:T(1024)S(1)} %fusion.88), kind=kOutput, calls=%fused_computation.76 | convolution fusion | flops 4847304704 | bytes 3149824 | tf_op jit(solution)/shard_map/dot_general | solution.py:34
  328.9 1.0 copy.51
  329.9 4.7 %all-to-all-start.2 = ((bf16[128,8,384]{2,0,1:T(8,128)(2,1)}), bf16[128,8,384]{2,0,1:T(8,128)(2,1)}, u32[]{:S(2)}, u32[]{:S(2)}) async-start(bf16[128,8,384]{2,0,1:T(8,128)(2,1)} %copy.51), calls=%async_computation.2 | async-start | bytes 1572864 | tf_op jit(solution)/shard_map/all_to_all | solution.py:130
  334.6 20.2 %all-to-all-done.2 = bf16[128,8,384]{2,0,1:T(8,128)(2,1)} async-done(((bf16[128,8,384]{2,0,1:T(8,128)(2,1)}), bf16[128,8,384]{2,0,1:T(8,128)(2,1)}, u32[]{:S(2)}, u32[]{:S(2)}) %all-to-all-start.2) | async-done | bytes 786464 | tf_op jit(solution)/shard_map/all_to_all | solution.py:130
  354.8 1.3 convert_multiply_fusion.5
  356.1 2.1 bitcast_add_fusion
  358.3 2.2 fusion.157
  (31 shorter events, 0.2 us)
Async XLA Ops:
  7.2 3.3 copy-start
  7.2 3.9 %copy-start.5 = (f32[768]{0:T(1024)S(1)}, f32[768]{0:T(1024)}, u32[]{:S(2)}) copy-start(f32[768]{0:T(1024)} %param.13) | copy-start | bytes 9220
  7.2 3.9 %copy-start.4 = (bf16[1024,768]{1,0:T(8,128)(2,1)S(1)}, bf16[1024,768]{1,0:T(8,128)(2,1)}, u32[]{:S(2)}) copy-start(bf16[1024,768]{1,0:T(8,128)(2,1)} %param.11) | copy-start | bytes 4718596
  7.2 36.6 %all-gather.3.cloned.1.call-start = ((), (), s32[]{:S(2)}) async-start(), calls=%async_computation.4 | async-start | bytes 2654208 | tf_op jit(solution)/shard_map/all_gather | solution.py:64
  7.9 68.3 %all-gather.5.cloned.1.call-start = ((), (), s32[]{:S(2)}) async-start(), calls=%async_computation.5 | async-start | bytes 2654208 | tf_op jit(solution)/shard_map/all_gather | solution.py:70
  8.7 124.3 %all-reduce.2.cloned.1.call-start = ((), (), s32[]{:S(2)}) async-start(), calls=%async_computation.6 | async-start | bytes 3145728 | tf_op jit(solution)/shard_map/psum | solution.py:93
  53.3 29.4 %copy-start.1 = (bf16[1024,768]{1,0:T(8,128)(2,1)S(1)}, bf16[1024,768]{1,0:T(8,128)(2,1)}, u32[]{:S(2)}) copy-start(bf16[1024,768]{1,0:T(8,128)(2,1)} %param.8) | copy-start | bytes 4718596
  82.6 50.4 %copy-start.6 = (f32[768]{0:T(1024)S(1)}, f32[768]{0:T(1024)}, u32[]{:S(2)}) copy-start(f32[768]{0:T(1024)} %param.12) | copy-start | bytes 9220
  138.1 19.4 %copy-start.2 = (f32[1024,768]{1,0:T(8,128)}, f32[1024,768]{1,0:T(8,128)S(1)}, u32[]{:S(2)}) copy-start(f32[1024,768]{1,0:T(8,128)S(1)} %fusion.35) | copy-start | bytes 9437188
  160.5 56.1 %all-to-all-start = ((bf16[2,1024,384]{2,0,1:T(2,128)(2,1)}), bf16[2,1024,384]{2,0,1:T(2,128)(2,1)}, u32[]{:S(2)}, u32[]{:S(2)}) async-start(bf16[2,1024,384]{2,0,1:T(2,128)(2,1)} %copy.39), calls=%async_computation | async-start | bytes 3145728 | tf_op jit(solution)/shard_map/all_to_all | solution.py:99
  165.8 192.5 %reduce-scatter.2.cloned.1.call-start = ((), (), s32[]{:S(2)}) async-start(), calls=%async_computation.7 | async-start | bytes 5308416 | tf_op jit(solution)/shard_map/reduce_scatter | solution.py:74
  166.0 6.7 %copy-start.7 = (bf16[1024,1536]{1,0:T(8,128)(2,1)S(1)}, bf16[1024,1536]{1,0:T(8,128)(2,1)}, u32[]{:S(2)}) copy-start(bf16[1024,1536]{1,0:T(8,128)(2,1)} %fusion.3) | copy-start | bytes 9437188
  227.5 53.6 %all-to-all-start.1 = ((bf16[2,8,128,384]{3,2,0,1:T(8,128)(2,1)}), bf16[2,8,128,384]{3,2,0,1:T(8,128)(2,1)S(1)}, u32[]{:S(2)}, u32[]{:S(2)}) async-start(bf16[2,8,128,384]{3,2,0,1:T(8,128)(2,1)} %copy.48), calls=%async_computation.1 | async-start | bytes 3145728 | tf_op jit(solution)/shard_map/all_to_all | solution.py:122
  328.9 27.2 %copy-start.3 = (f32[1024,768]{1,0:T(8,128)S(1)}, f32[1024,768]{1,0:T(8,128)}, u32[]{:S(2)}) copy-start(f32[1024,768]{1,0:T(8,128)} %copy-done.2) | copy-start | bytes 9437188
  329.9 25.0 %all-to-all-start.2 = ((bf16[128,8,384]{2,0,1:T(8,128)(2,1)}), bf16[128,8,384]{2,0,1:T(8,128)(2,1)}, u32[]{:S(2)}, u32[]{:S(2)}) async-start(bf16[128,8,384]{2,0,1:T(8,128)(2,1)} %copy.51), calls=%async_computation.2 | async-start | bytes 1572864 | tf_op jit(solution)/shard_map/all_to_all | solution.py:130
Sparse Core Ops, SparseCore 0:
  9.7 34.0 all-gather.2
  45.4 30.7 all-gather.4
  82.8 50.1 all-reduce.1
  178.8 84.8 reduce-scatter.1
where the time goes:
time: 374 us; the launch traced here: 367 us
  waiting for transfers between devices  208 us (56%)
  matrix products  97.5 us (26%)
  starting transfers between devices  18.8 us (5%)
  other arithmetic  16 us (4%)
  between operations  14.3 us (4%)
  local copies, waits for them, and re-layouts  12.3 us (3%)
    dot_general x4, matrix products, exact_dot(): jnp.dot(left, right, precision=lax.Precision.HIGHEST, preferred_element_t...  67 us
    psum x1, waiting for transfers between devices, local(): lax.psum(partial_sum.astype(jnp.bfloat16), 'hid').astype(jnp.float32)  49.4 us
    all_to_all x1, waiting for transfers between devices, local(): lax.all_to_all(twisted.astype(jnp.bfloat16), ('seq', 'sub'), split_axis=1...  45 us
    all_to_all x1, waiting for transfers between devices, local(): lax.all_to_all(spectral.astype(jnp.bfloat16), ('seq', 'sub'), split_axis=...  37.7 us
    all_gather x1, waiting for transfers between devices, local(): lax.all_gather(w_out, ('seq', 'sub'), axis=0, tiled=True)  31.6 us
    all_gather x1, waiting for transfers between devices, local(): lax.all_gather(w_in, ('seq', 'sub'), axis=0, tiled=True)  23 us
    all_to_all x1, waiting for transfers between devices, local(): lax.all_to_all(real_out.reshape(quota, span_count, col_count).astype(jnp....  20.2 us
    dot_general x1, matrix products, local(): jnp.dot(ffn_low, lax.all_gather(w_out, ('seq', 'sub'), axis=0, tiled=True...  9.45 us
  transfers between devices with their start and end apart: 7, of which 6 were waited for; matrix products, arithmetic and copies ran while one was open for 24% of the time, Pallas kernels for 0%

commit v1 on v0

v1 whole, which is shorter than its diff:
```python
import functools
import math

import jax
import jax.numpy as jnp
from jax import lax
from jax.experimental import pallas as pl
from jax.experimental.pallas import tpu as pltpu
from jax.sharding import PartitionSpec as P

epsilon = 1e-05
SPANS = ("seq", "sub")
TEAM = ("seq", "sub", "hid")
LANES = 128


def norm_parts(values):
    values = values.astype(jnp.float32)
    row_mean = jnp.mean(values, axis=-1, keepdims=True)
    centred = values - row_mean
    inv_std = lax.rsqrt(jnp.mean(centred * centred, axis=-1, keepdims=True) + epsilon)
    return (centred * inv_std, inv_std)


def norm_backward(values, gain_vec, upstream):
    unit_rows, inv_std = norm_parts(values)
    scaled = upstream * gain_vec
    return inv_std * (
        scaled
        - jnp.mean(scaled, axis=-1, keepdims=True)
        - unit_rows * jnp.mean(scaled * unit_rows, axis=-1, keepdims=True)
    )


def gelu_tanh(values):
    return jax.nn.gelu(values, approximate=True)


def shift_pairs(size, step):
    return [(i, (i + step) % size) for i in range(size)]


def turn(products, period):
    angles = (2.0 * math.pi / period) * (products % period).astype(jnp.float32)
    return (jnp.cos(angles), jnp.sin(angles))


def feature_table(width, slots, team):
    half = width // 2
    device = lax.broadcasted_iota(jnp.int32, (team, 2 * slots, width), 0)
    place = lax.broadcasted_iota(jnp.int32, (team, 2 * slots, width), 1)
    feat = lax.broadcasted_iota(jnp.int32, (team, 2 * slots, width), 2)
    feat = lax.optimization_barrier(feat)
    is_sin = place >= slots
    slot = device * slots + place % slots
    top = is_sin & (slot == 0)
    freq = jnp.where(top, half, slot)
    lag = jnp.where(is_sin & ~top, width - width // 4, 0)
    angles = (2.0 * math.pi / width) * ((freq * feat + lag) % width).astype(jnp.float32)
    table = jnp.where(slot < half, jnp.cos(angles), 0.0)
    return table.astype(jnp.bfloat16).reshape(team * 2 * slots, width)


def position_table(count):
    fine = 32
    coarse = count // fine
    col = lax.optimization_barrier(jnp.arange(count, dtype=jnp.int32))
    cos_a, sin_a = turn(fine * jnp.arange(coarse, dtype=jnp.int32)[:, None] * col[None], count)
    cos_b, sin_b = turn(jnp.arange(fine, dtype=jnp.int32)[:, None] * col[None], count)
    cos_a, sin_a = cos_a[:, None], sin_a[:, None]
    cos_b, sin_b = cos_b[None], sin_b[None]
    both = jnp.stack([cos_a * cos_b - sin_a * sin_b, -sin_a * cos_b - cos_a * sin_b])
    return both.astype(jnp.bfloat16).reshape(2 * count, count)


def combine(terms):
    total = None
    for factor, value in terms:
        if abs(factor) < 1e-12:
            continue
        if abs(factor - 1.0) < 1e-12:
            total = value if total is None else total + value
        elif abs(factor + 1.0) < 1e-12:
            total = -value if total is None else total - value
        else:
            part = factor * value
            total = part if total is None else total + part
    return total


def span_transform(parts, freq, spans):
    angles = [2.0 * math.pi * (r * freq % spans) / spans for r in range(spans)]
    real = combine([(math.cos(a), p) for a, p in zip(angles, parts)])
    imag = combine([(math.sin(a), p) for a, p in zip(angles, parts)])
    return (real, imag)


def position_kernel(spans, hids, slots, x_ref, mark_ref, twist_ref, tab_ref, o_ref, v_ref):
    rows_in = x_ref.shape[2]
    count = rows_in * hids
    own_rows = spans * slots

    @pl.when(pl.program_id(0) == 0)
    def _():
        mark = jnp.broadcast_to(mark_ref[...], (slots, LANES)) > 0.5
        for hid in range(hids):
            for piece in range(rows_in // LANES):
                lanes = slice(piece * LANES, (piece + 1) * LANES)
                at = hid * rows_in + piece * LANES
                blocks = [x_ref[r * hids + hid, :, lanes].astype(jnp.float32) for r in range(spans)]
                cos_parts = [b[:slots] for b in blocks]
                sin_parts = [b[slots:] for b in blocks]
                cos_half, sin_half = [], []
                for freq in range(spans // 2 + 1):
                    cos_half.append(span_transform(cos_parts, freq, spans))
                    sin_half.append(span_transform(sin_parts, freq, spans))
                held = []
                for freq in range(spans):
                    low = min(freq, spans - freq)
                    c_re, c_im = cos_half[low]
                    s_re, s_im = sin_half[low]
                    if c_im is None:
                        c_im, s_im = jnp.zeros_like(c_re), jnp.zeros_like(s_re)
                    elif low != freq:
                        c_im, s_im = -c_im, -s_im
                    t_re = jnp.broadcast_to(twist_ref[0, freq : freq + 1, at : at + LANES], c_re.shape)
                    t_im = jnp.broadcast_to(twist_ref[1, freq : freq + 1, at : at + LANES], c_re.shape)
                    pairs = (
                        (jnp.where(mark, c_re, c_re - s_im), jnp.where(mark, c_im, c_im + s_re)),
                        (jnp.where(mark, s_re, c_re + s_im), jnp.where(mark, s_im, c_im - s_re)),
                    )
                    held.append(
                        [(re * t_re - im * t_im, re * t_im + im * t_re) for re, im in pairs]
                    )
                    if freq % 2 == 1:
                        row = (freq - 1) * slots
                        for side in range(2):
                            for part in range(2):
                                v_ref[
                                    side * own_rows + row : side * own_rows + row + 2 * slots,
                                    part * count + at : part * count + at + LANES,
                                ] = jnp.concatenate(
                                    [held[0][side][part], held[1][side][part]], axis=0
                                ).astype(v_ref.dtype)
                        held = []

    res = jnp.dot(v_ref[...], tab_ref[...], preferred_element_type=jnp.float32)
    res = res.astype(o_ref.dtype)
    for dest in range(o_ref.shape[0]):
        for side in range(2):
            o_ref[dest, side] = res[
                side * own_rows : (side + 1) * own_rows, dest * LANES : (dest + 1) * LANES
            ]


def position_transform(got, mark, twist, table, spans, hids, slots):
    count = table.shape[1]
    share = count // spans
    team = spans * hids
    rows = spans * slots
    if hids == 2 and share == LANES and slots % 8 == 0 and spans % 2 == 0:
        dests = 2
        out = pl.pallas_call(
            functools.partial(position_kernel, spans, hids, slots),
            grid=(spans // dests,),
            in_specs=[
                pl.BlockSpec(got.shape, lambda i: (0, 0, 0)),
                pl.BlockSpec(mark.shape, lambda i: (0, 0)),
                pl.BlockSpec(twist.shape, lambda i: (0, 0, 0)),
                pl.BlockSpec((2 * count, dests * LANES), lambda i: (0, i)),
            ],
            out_specs=pl.BlockSpec((dests, hids, rows, LANES), lambda i: (i, 0, 0, 0)),
            out_shape=jax.ShapeDtypeStruct((spans, hids, rows, LANES), jnp.bfloat16),
            scratch_shapes=[pltpu.VMEM((2 * rows, 2 * count), jnp.bfloat16)],
            compiler_params=pltpu.CompilerParams(vmem_limit_bytes=32 << 20),
            cost_estimate=pl.CostEstimate(
                flops=2 * 2 * rows * 2 * count * count, bytes_accessed=6 << 20, transcendentals=0
            ),
            name="position_transform",
        )(got, mark, twist, table)
        return out.reshape(team, rows, share)
    wide = got.astype(jnp.float32).reshape(spans, hids, 2, slots, count // hids)
    wide = wide.transpose(2, 0, 3, 1, 4).reshape(2, spans, slots, count)
    ids = jnp.arange(spans, dtype=jnp.int32)
    cos_s, sin_s = turn(ids[:, None] * ids[None], spans)
    exact = lax.Precision.HIGHEST
    re = jnp.einsum("kr,crsn->cksn", cos_s, wide, precision=exact)
    im = jnp.einsum("kr,crsn->cksn", sin_s, wide, precision=exact)
    special = mark > 0.5
    v_re = jnp.stack([jnp.where(special, re[0], re[0] - im[1]), jnp.where(special, re[1], re[0] + im[1])])
    v_im = jnp.stack([jnp.where(special, im[0], im[0] + re[1]), jnp.where(special, im[1], im[0] - re[1])])
    t_re, t_im = twist[0][:, None], twist[1][:, None]
    both = jnp.concatenate([v_re * t_re - v_im * t_im, v_re * t_im + v_im * t_re], axis=-1)
    res = jnp.dot(
        both.astype(jnp.bfloat16).reshape(2 * rows, 2 * count), table, preferred_element_type=jnp.float32
    ).astype(jnp.bfloat16)
    res = res.reshape(2, rows, spans, share).transpose(2, 0, 1, 3)
    res = jnp.repeat(res, hids // 2, axis=1)
    return res.reshape(team, rows, share)


def finish_kernel(spans, slots, back_ref, pick_ref, own_ref, o_ref, held_ref):
    team = back_ref.shape[0]
    groups = held_ref.shape[0]
    for freq in range(spans):
        rows = slice(freq * slots, (freq + 1) * slots)
        block = jnp.concatenate(
            [back_ref[s].astype(jnp.float32)[rows] for s in range(team)], axis=0
        ).astype(jnp.bfloat16)
        value = lax.dot_general(
            block, pick_ref[...], (((0,), (0,)), ((), ())), preferred_element_type=jnp.float32
        )
        for g in range(groups):
            held_ref[g, pl.ds(freq, LANES, stride=spans), :] = value[:, g * LANES : (g + 1) * LANES]
    for g in range(groups):
        lanes = slice(g * LANES, (g + 1) * LANES)
        o_ref[:, lanes] = own_ref[:, lanes] + held_ref[g]


def finish(back, pick, own, spans, slots):
    team, rows, share = back.shape
    if share == LANES and slots % 8 == 0 and own.shape[1] % LANES == 0:
        return pl.pallas_call(
            functools.partial(finish_kernel, spans, slots),
            out_shape=jax.ShapeDtypeStruct(own.shape, jnp.float32),
            scratch_shapes=[pltpu.VMEM((own.shape[1] // LANES, own.shape[0], LANES), jnp.float32)],
            compiler_params=pltpu.CompilerParams(vmem_limit_bytes=32 << 20),
            cost_estimate=pl.CostEstimate(
                flops=2 * own.shape[0] * pick.size, bytes_accessed=5 << 20, transcendentals=0
            ),
            name="finish",
        )(back, pick, own)
    value = jnp.einsum(
        "skjn,sjm->nkm",
        back.reshape(team, spans, slots, share),
        pick.reshape(team, slots, pick.shape[1]),
        preferred_element_type=jnp.float32,
    )
    return own + value.reshape(own.shape)


def local(z_mix, z_ffn, pre_act, grad_out, gain_mix, gain_ffn, w_in, w_out):
    tok_rows, width = z_mix.shape
    unit_count = pre_act.shape[1]
    hids = lax.axis_size("hid")
    hid_index = lax.axis_index("hid")
    spans = lax.axis_size(SPANS)
    team = spans * hids
    half = width // 2
    slots = -(-half // team)
    rows = tok_rows // hids
    col_count = width // hids
    seq_length = tok_rows * spans
    bf16 = jnp.bfloat16

    def row_part(values, index):
        return lax.dynamic_slice_in_dim(values, index * rows, rows, 0)

    feat_tab = feature_table(width, slots, team)
    pos_tab = position_table(tok_rows)
    t_cos, t_sin = turn(
        jnp.arange(spans, dtype=jnp.int32)[:, None] * jnp.arange(tok_rows, dtype=jnp.int32)[None], seq_length
    )
    twist = jnp.stack([t_cos, t_sin]) * (1.0 / math.sqrt(seq_length * width))
    team_index = lax.axis_index(TEAM)
    mark = ((team_index * slots + jnp.arange(slots, dtype=jnp.int32)) == 0).astype(jnp.float32)[:, None]
    own_ids = hid_index * col_count + jnp.arange(col_count, dtype=jnp.int32)
    own_slot = jnp.where(own_ids < half, own_ids, jnp.where(own_ids == half, 0, width - own_ids))
    pick = (jnp.arange(team * slots, dtype=jnp.int32)[:, None] == own_slot[None]).astype(bf16)

    normed = (norm_parts(z_mix)[0] * gain_mix).astype(bf16)
    ffn_grad = norm_backward(z_ffn, gain_ffn, grad_out.astype(jnp.float32))
    ffn_low = ffn_grad.astype(bf16)
    pre_wide = pre_act.astype(jnp.float32)
    activation = gelu_tanh(pre_wide).astype(bf16)
    _, pull_back = jax.vjp(gelu_tanh, pre_wide)
    contract_units = (((1,), (1,)), ((), ()))
    contract_rows = (((0,), (0,)), ((), ()))
    act_grad = jnp.dot(
        ffn_low, lax.all_gather(w_out, SPANS, axis=0, tiled=True), preferred_element_type=jnp.float32
    )
    pre_grad = pull_back(act_grad)[0].astype(bf16)
    partial_sum = lax.dot_general(
        pre_grad,
        lax.all_gather(w_in, SPANS, axis=0, tiled=True),
        contract_units,
        preferred_element_type=jnp.float32,
    ).astype(bf16)
    both_grads = lax.psum_scatter(
        jnp.concatenate(
            [
                lax.dot_general(normed, pre_grad, contract_rows, preferred_element_type=jnp.float32),
                lax.dot_general(ffn_low, activation, contract_rows, preferred_element_type=jnp.float32),
            ],
            axis=1,
        ).astype(bf16),
        SPANS,
        scatter_dimension=0,
        tiled=True,
    ).astype(jnp.float32)
    grad_w_in = both_grads[:, :unit_count]
    grad_w_out = both_grads[:, unit_count:]

    summed = row_part(partial_sum, hid_index).astype(jnp.float32)
    for step in range(1, hids):
        sent = row_part(partial_sum, (hid_index + step) % hids)
        summed += lax.ppermute(sent, "hid", shift_pairs(hids, step)).astype(jnp.float32)
    mix_grad = norm_backward(
        row_part(z_mix, hid_index), gain_mix, row_part(ffn_grad, hid_index) + summed
    )
    mix_low = mix_grad.astype(bf16)

    spectral = lax.dot_general(
        feat_tab, mix_low, contract_units, preferred_element_type=jnp.float32
    ).astype(bf16)
    got = lax.all_to_all(
        spectral.reshape(team, 2 * slots, rows), TEAM, split_axis=0, concat_axis=0, tiled=True
    )
    sent_back = position_transform(got, mark, twist, pos_tab, spans, hids, slots)
    back = lax.all_to_all(sent_back, TEAM, split_axis=0, concat_axis=0, tiled=True)

    def col_part(values, index):
        return lax.dynamic_slice_in_dim(values, index * col_count, col_count, 1)

    own = jnp.zeros((tok_rows, col_count), jnp.float32)
    own = lax.dynamic_update_slice_in_dim(own, col_part(mix_grad, hid_index), hid_index * rows, 0)
    for step in range(1, hids):
        sent = col_part(mix_low, (hid_index + step) % hids)
        came = lax.ppermute(sent, "hid", shift_pairs(hids, step)).astype(jnp.float32)
        own = lax.dynamic_update_slice_in_dim(own, came, (hid_index - step) % hids * rows, 0)
    grad_in = finish(back, pick, own, spans, slots)
    return (grad_in, grad_w_in, grad_w_out)


def solution(mesh):
    in_specs = (
        P(("groups", "seq", "sub"), None),
        P(("groups", "seq", "sub"), None),
        P(("groups", "seq", "sub"), "hid"),
        P(("groups", "seq", "sub"), None),
        P(),
        P(),
        P(("seq", "sub"), "hid"),
        P(("seq", "sub"), "hid"),
    )
    out_specs = (
        P(("groups", "seq", "sub"), "hid"),
        P(("groups", "seq", "sub"), "hid"),
        P(("groups", "seq", "sub"), "hid"),
    )
    return jax.shard_map(local, mesh=mesh, in_specs=in_specs, out_specs=out_specs, check_vma=False)
```

time: 374 us -> 185 us (0.49); the launches traced: 367 us -> 184 us
  waiting for transfers between devices: 208 us -> 88.3 us
  matrix products: 97.5 us -> 23 us
  other arithmetic: 16 us -> 26.4 us
  Pallas kernels: 0 us -> 6.99 us
    all_to_all x3 -> x2, waiting for transfers between devices: 103 us -> 25.5 us  [the longest x1 23.4 us: local(): lax.all_to_all(spectral.reshape(team, 2 * slots, rows), TEAM, split_axis=...]
    dot_general x10 -> x3, matrix products: 87.6 us -> 15.5 us  [the longest x1 8.5 us: local(): jnp.dot(ffn_low, lax.all_gather(w_out, SPANS, axis=0, tiled=True), prefer...]
    psum x1 -> x0, waiting for transfers between devices: 49.4 us -> none  [local(): lax.psum(partial_sum.astype(jnp.bfloat16), 'hid').astype(jnp.float32)]
    ppermute x0 -> x2, waiting for transfers between devices: none -> 22.5 us  [local(): lax.ppermute(sent, 'hid', shift_pairs(hids, step)).astype(jnp.float32)]
    all_gather x2, waiting for transfers between devices: 54.5 us -> 38.9 us  [the longest x1 23.3 us: local(): lax.all_gather(w_out, SPANS, axis=0, tiled=True)]
    convert_element_type x0 -> x4, other arithmetic: none -> 11.4 us  [the longest x1 9.66 us: feature_table(): return table.astype(jnp.bfloat16).reshape(team * 2 * slots, width)]
    pallas_call x0 -> x2, Pallas kernels: none -> 6.99 us  [the longest x1 4.8 us: position_transform(): pl.pallas_call(functools.partial(position_kernel, spans, hids, slots), gr...]
    unnamed x18 -> x22, local copies, waits for them, and re-layouts: 0.29 us -> 5.67 us
  transfers between devices with their start and end apart: 7 -> 7, of which waited for: 6 -> 6; matrix products, arithmetic and copies ran while one was open for 24% -> 28% of each run, Pallas kernels for 0% -> 4%
where the time goes in v1:
time: 185 us; the launch traced here: 184 us
  waiting for transfers between devices  88.3 us (48%)
  other arithmetic  26.4 us (14%)
  matrix products  23 us (12%)
  starting transfers between devices  16.2 us (9%)
  between operations  14.1 us (8%)
  local copies, waits for them, and re-layouts  9.48 us (5%)
  Pallas kernels  6.99 us (4%)
    all_to_all x1, waiting for transfers between devices, local(): lax.all_to_all(spectral.reshape(team, 2 * slots, rows), TEAM, split_axis=...  23.4 us
    all_gather x1, waiting for transfers between devices, local(): lax.all_gather(w_out, SPANS, axis=0, tiled=True)  23.3 us
    ppermute x2, waiting for transfers between devices, local(): lax.ppermute(sent, 'hid', shift_pairs(hids, step)).astype(jnp.float32)  22.5 us
    all_gather x1, waiting for transfers between devices, local(): lax.all_gather(w_in, SPANS, axis=0, tiled=True)  15.7 us
    convert_element_type x1, other arithmetic, feature_table(): return table.astype(jnp.bfloat16).reshape(team * 2 * slots, width)  9.66 us
    all_to_all x1, starting transfers between devices, local(): lax.all_to_all(sent_back, TEAM, split_axis=0, concat_axis=0, tiled=True)  8.69 us
    dot_general x1, matrix products, local(): jnp.dot(ffn_low, lax.all_gather(w_out, SPANS, axis=0, tiled=True), prefer...  8.5 us
    unnamed x22, local copies, waits for them, and re-layouts  5.67 us
  transfers between devices with their start and end apart: 7, of which 6 were waited for; matrix products, arithmetic and copies ran while one was open for 28% of the time, Pallas kernels for 4%

profile of v1, /device:TPU:1, one launch (start us, length us, event | category | flops | bytes accessed | tf_op | source)
XLA Modules:
  0.0 184.4 jit_solution(6859664246844594250)
XLA Ops:
  7.2 0.0 all-gather.3.cloned.1.call-start
  7.2 0.7 all-gather.3.cloned.1.call-update
  7.9 0.0 all-gather.5.cloned.1.call-start
  8.0 0.7 all-gather.5.cloned.1.call-update
  8.7 0.0 reduce-scatter.2.cloned.1.call-start
  8.7 1.8 convert_reduce_fusion.1
  10.6 0.6 fusion.22
  11.2 0.3 convert_reduce_fusion
  11.5 0.6 fusion.19
  12.1 1.2 fusion.27
  13.3 1.2 fusion.18
  14.5 1.7 copy-done.3
  16.2 4.4 %convolution_convert_fusion = bf16[768,1536]{1,0:T(8,128)(2,1)} fusion(bf16[1024,1536]{1,0:T(8,128)(2,1)S(1)} %copy-done.9, f32[1024,768]{1,0:T(8,128)S(1)} %fusion.18), kind=kOutput, calls=%fused_computation.30 | convolution fusion | flops 2433613824 | bytes 8650752 | tf_op jit(solution)/shard_map/dot_general | solution.py:293
  20.5 23.3 %all-gather.3.cloned.1.call-done = bf16[768,1536]{1,0:T(8,128)(2,1)} async-done(((bf16[96,1536]{1,0:T(8,128)(2,1)}), bf16[768,1536]{1,0:T(8,128)(2,1)}) %all-gather.3.cloned.1.call-update) | async-done | bytes 2359312 | tf_op jit(solution)/shard_map/all_gather | solution.py:280
  43.8 8.5 %fusion.3 = bf16[1024,1536]{1,0:T(8,128)(2,1)S(1)} fusion(bf16[1024,1536]{1,0:T(8,128)(2,1)} %param.10, bf16[768,1536]{1,0:T(8,128)(2,1)} %all-gather.3.cloned.1.call-done, f32[1024,768]{1,0:T(8,128)} %copy-done.3), kind=kOutput, calls=%fused_computation.8 | convolution fusion | flops 2449735680 | bytes 11796480 | tf_op jit(solution)/shard_map/dot_general | solution.py:279
  52.3 1.7 copy-done.10
  54.1 3.1 %convolution_convert_fusion.1 = bf16[768,1536]{1,0:T(8,128)(2,1)S(1)} fusion(bf16[1024,1536]{1,0:T(8,128)(2,1)S(1)} %fusion.3, bf16[1024,768]{1,0:T(8,128)(2,1)S(1)} %copy-done.2, f32[768]{0:T(1024)S(1)} %copy-done.8, f32[1024]{0:T(1024)S(1)} %add_rsqrt_fusion, f32[1024]{0:T(1024)S(1)} %broadcast_multiply_fusion), kind=kOutput, calls=%fused_computation.31 | convolution fusion | flops 2421030912 | bytes 7089152 | tf_op jit(solution)/shard_map/dot_general | solution.py:292
  57.2 2.7 %pad_maximum_fusion = bf16[768,3072]{1,0:T(8,128)(2,1)} fusion(bf16[768,1536]{1,0:T(8,128)(2,1)S(1)} %copy-done.6, bf16[768,1536]{1,0:T(8,128)(2,1)S(1)} %convolution_convert_fusion.1), kind=kLoop, calls=%fused_computation.15 | loop fusion | flops 9437184 | bytes 9437184 | tf_op jit(solution)/shard_map/concatenate | solution.py:290
  59.9 0.2 convert_reduce_fusion.2
  60.2 0.4 fusion.43
  60.5 15.7 %all-gather.5.cloned.1.call-done = bf16[768,1536]{1,0:T(8,128)(2,1)} async-done(((bf16[96,1536]{1,0:T(8,128)(2,1)}), bf16[768,1536]{1,0:T(8,128)(2,1)}) %all-gather.5.cloned.1.call-update) | async-done | bytes 2359312 | tf_op jit(solution)/shard_map/all_gather | solution.py:285
  76.2 5.2 %convolution_convert_fusion.2 = bf16[1024,768]{1,0:T(8,128)(2,1)S(1)} fusion(bf16[1024,1536]{1,0:T(8,128)(2,1)} %copy-done.10, bf16[768,1536]{1,0:T(8,128)(2,1)} %all-gather.5.cloned.1.call-done), kind=kOutput, calls=%fused_computation.60 | convolution fusion | flops 2416705536 | bytes 7077888 | tf_op jit(solution)/shard_map/dot_general | solution.py:283
  81.5 0.1 constant_dynamic-slice_fusion.1
  81.5 1.2 collective-permute-start
  82.8 0.2 iota.108
  83.0 9.7 %fusion.32 = bf16[16,48,768]{2,1,0:T(8,128)(2,1)S(1)} fusion(s32[16,48,768]{2,1,0:T(8,128)S(1)} %iota.108, s32[48]{0:T(128)S(1)} %get-tuple-element.21, s32[48]{0:T(128)S(1)} %get-tuple-element.22, s32[16]{0:T(128)S(1)} %iota_multiply_fusion.1, pred[48]{0:T(512)(128)(4,1)S(1)} %get-tuple-element.20, pred[48]{0:T(512)(128)(4,1)S(1)} %get-tuple-element.19), kind=kLoop, calls=%fused_computation.48 | loop fusion | flops 12386304 | bytes 3539488 | tf_op jit(solution)/shard_map/convert_element_type | solution.py:61
  92.7 7.9 %collective-permute-done = bf16[512,768]{1,0:T(8,128)(2,1)S(1)} collective-permute-done((bf16[512,768]{1,0:T(8,128)(2,1)S(1)}, bf16[512,768]{1,0:T(8,128)(2,1)S(1)}, u32[]{:S(2)}, u32[]{:S(2)}) %collective-permute-start) | collective-permute-done | bytes 786464 | tf_op jit(solution)/shard_map/ppermute | solution.py:307
  100.6 0.8 fusion.82
  101.4 1.6 fusion.83
  103.0 1.7 convolution_convert_fusion.3
  104.8 4.7 %all-to-all-start = ((bf16[16,48,512]{2,1,0:T(8,128)(2,1)}), bf16[16,48,512]{2,1,0:T(8,128)(2,1)S(1)}, u32[]{:S(2)}, u32[]{:S(2)}) async-start(bf16[16,48,512]{2,1,0:T(8,128)(2,1)} %bitcast.1), calls=%async_computation | async-start | bytes 1572864 | tf_op jit(solution)/shard_map/all_to_all | solution.py:316
  109.5 0.1 fusion.74
  109.7 1.1 fusion.65
  110.7 1.6 subtract_convert_fusion.1
  112.3 2.4 %pad_maximum_fusion.1 = bf16[2,32,32,1024]{3,2,1,0:T(8,128)(2,1)} fusion(bf16[1,32,32,1024]{3,2,1,0:T(8,128)(2,1)S(1)} %get-tuple-element.13, bf16[1,32,32,1024]{3,2,1,0:T(8,128)(2,1)S(1)} %get-tuple-element.12), kind=kLoop, calls=%fused_computation.16 | loop fusion | flops 2097152 | bytes 8388608 | tf_op jit(solution)/shard_map/stack | solution.py:72
  114.7 23.4 %all-to-all-done.x_ref = bf16[16,48,512]{2,1,0:T(8,128)(2,1)S(1)} async-done(((bf16[16,48,512]{2,1,0:T(8,128)(2,1)}), bf16[16,48,512]{2,1,0:T(8,128)(2,1)S(1)}, u32[]{:S(2)}, u32[]{:S(2)}) %all-to-all-start) | async-done | bytes 786464 | tf_op jit(solution)/shard_map/all_to_all | solution.py:316
  138.1 2.2 %copy-done = bf16[2,32,32,1024]{3,2,1,0:T(8,128)(2,1)S(1)} copy-done((bf16[2,32,32,1024]{3,2,1,0:T(8,128)(2,1)S(1)}, bf16[2,32,32,1024]{3,2,1,0:T(8,128)(2,1)}, u32[]{:S(2)}) %copy-start) | copy-done | bytes 4194328
  140.4 4.8 %position_transform.1 = bf16[8,2,192,128]{3,2,1,0:T(8,128)(2,1)} custom-call(bf16[16,48,512]{2,1,0:T(8,128)(2,1)S(1)} %all-to-all-done.x_ref, f32[24,1]{1,0:T(8,128)S(1)} %fusion.76.mark_ref, f32[2,8,1024]{2,1,0:T(8,128)S(1)} %maximum_multiply_fusion.twist_ref, bf16[2048,1024]{1,0:T(8,128)(2,1)S(1)} %bitcast.10), custom_call_target="tpu_custom_call" | custom-call | flops 1610612736 | bytes 6291456 | tf_op jit(solution)/shard_map/position_transform/pallas_call | solution.py:163
  145.2 8.7 %all-to-all-start.1 = ((bf16[16,192,128]{2,1,0:T(8,128)(2,1)}), bf16[16,192,128]{2,1,0:T(8,128)(2,1)S(1)}, u32[]{:S(2)}, u32[]{:S(2)}) async-start(bf16[16,192,128]{2,1,0:T(8,128)(2,1)} %bitcast.3), calls=%async_computation.1 | async-start | bytes 1572864 | tf_op jit(solution)/shard_map/all_to_all | solution.py:320
  153.9 1.4 collective-permute-start.1
  155.4 0.1 fusion.53.pick_ref
  155.5 0.1 broadcast_in_dim.20
  155.6 1.2 dynamic-slice_dynamic-update-slice_fusion
  156.8 14.6 %collective-permute-done.1 = bf16[512,384]{1,0:T(8,128)(2,1)S(1)} collective-permute-done((bf16[512,384]{1,0:T(8,128)(2,1)S(1)}, bf16[512,384]{1,0:T(8,128)(2,1)S(1)}, u32[]{:S(2)}, u32[]{:S(2)}) %collective-permute-start.1) | collective-permute-done | bytes 393248 | tf_op jit(solution)/shard_map/ppermute | solution.py:329
  171.4 0.1 convert_dynamic-update-slice_fusion.own_ref
  171.4 2.0 %all-to-all-done.1.back_ref = bf16[16,192,128]{2,1,0:T(8,128)(2,1)S(1)} async-done(((bf16[16,192,128]{2,1,0:T(8,128)(2,1)}), bf16[16,192,128]{2,1,0:T(8,128)(2,1)S(1)}, u32[]{:S(2)}, u32[]{:S(2)}) %all-to-all-start.1) | async-done | bytes 786464 | tf_op jit(solution)/shard_map/all_to_all | solution.py:320
  173.5 2.2 %finish.1 = f32[1024,384]{1,0:T(8,128)} custom-call(bf16[16,192,128]{2,1,0:T(8,128)(2,1)S(1)} %all-to-all-done.1.back_ref, bf16[384,384]{1,0:T(8,128)(2,1)S(1)} %fusion.53.pick_ref, f32[1024,384]{1,0:T(8,128)S(1)} %convert_dynamic-update-slice_fusion.own_ref), custom_call_target="tpu_custom_call" | custom-call | flops 301989888 | bytes 5242880 | tf_op jit(solution)/shard_map/finish/pallas_call | solution.py:223
  175.7 2.2 %fusion.85 = (f32[96,1536]{1,0:T(8,128)}, f32[96,1536]{1,0:T(8,128)}) fusion(bf16[96,3072]{1,0:T(8,128)(2,1)} %reduce-scatter.2.cloned.1.call-done), kind=kLoop, calls=%fused_computation.140 | loop fusion | bytes 2359296 | tf_op jit(solution)/shard_map/slice | solution.py:302
  (39 shorter events, 0.2 us)
Async XLA Ops:
  7.2 3.4 %copy-start.1 = (bf16[1024,768]{1,0:T(8,128)(2,1)S(1)}, bf16[1024,768]{1,0:T(8,128)(2,1)}, u32[]{:S(2)}) copy-start(bf16[1024,768]{1,0:T(8,128)(2,1)} %param.9) | copy-start | bytes 4718596
  7.2 4.0 %copy-start.2 = (bf16[1024,768]{1,0:T(8,128)(2,1)S(1)}, bf16[1024,768]{1,0:T(8,128)(2,1)}, u32[]{:S(2)}) copy-start(bf16[1024,768]{1,0:T(8,128)(2,1)} %param.8) | copy-start | bytes 4718596
  7.2 36.6 %all-gather.3.cloned.1.call-start = ((), (), s32[]{:S(2)}) async-start(), calls=%async_computation.3 | async-start | bytes 2654208 | tf_op jit(solution)/shard_map/all_gather | solution.py:280
  7.9 68.3 %all-gather.5.cloned.1.call-start = ((), (), s32[]{:S(2)}) async-start(), calls=%async_computation.4 | async-start | bytes 2654208 | tf_op jit(solution)/shard_map/all_gather | solution.py:285
  8.7 3.4 %copy-start.7 = (f32[768]{0:T(1024)S(1)}, f32[768]{0:T(1024)}, u32[]{:S(2)}) copy-start(f32[768]{0:T(1024)} %param.13) | copy-start | bytes 9220
  8.7 167.0 %reduce-scatter.2.cloned.1.call-start = ((), (), s32[]{:S(2)}) async-start(), calls=%async_computation.5 | async-start | bytes 5308416 | tf_op jit(solution)/shard_map/reduce_scatter | solution.py:289
  8.7 3.4 %copy-start.5 = (bf16[1024,768]{1,0:T(8,128)(2,1)S(1)}, bf16[1024,768]{1,0:T(8,128)(2,1)}, u32[]{:S(2)}) copy-start(bf16[1024,768]{1,0:T(8,128)(2,1)} %param.11) | copy-start | bytes 4718596
  13.3 2.9 %copy-start.9 = (bf16[1024,1536]{1,0:T(8,128)(2,1)S(1)}, bf16[1024,1536]{1,0:T(8,128)(2,1)}, u32[]{:S(2)}) copy-start(bf16[1024,1536]{1,0:T(8,128)(2,1)} %param.10) | copy-start | bytes 9437188
  14.5 1.7 copy-start.3
  20.5 33.5 %copy-start.8 = (f32[768]{0:T(1024)S(1)}, f32[768]{0:T(1024)}, u32[]{:S(2)}) copy-start(f32[768]{0:T(1024)} %param.12) | copy-start | bytes 9220
  52.3 1.7 copy-start.10
  54.0 3.1 %copy-start.6 = (bf16[768,1536]{1,0:T(8,128)(2,1)S(1)}, bf16[768,1536]{1,0:T(8,128)(2,1)}, u32[]{:S(2)}) copy-start(bf16[768,1536]{1,0:T(8,128)(2,1)} %convolution_convert_fusion) | copy-start | bytes 7077892
  81.5 19.0 %copy-start.4 = (f32[1024,768]{1,0:T(8,128)S(1)}, f32[1024,768]{1,0:T(8,128)}, u32[]{:S(2)}) copy-start(f32[1024,768]{1,0:T(8,128)} %copy-done.3) | copy-start | bytes 9437188
  81.5 19.0 %collective-permute-start = (bf16[512,768]{1,0:T(8,128)(2,1)S(1)}, bf16[512,768]{1,0:T(8,128)(2,1)S(1)}, u32[]{:S(2)}, u32[]{:S(2)}) collective-permute-start(bf16[512,768]{1,0:T(8,128)(2,1)S(1)} %constant_dynamic-slice_fusion.1), channel_id=1, source_target_pairs={{0,2},{2,0},{1,3},{3,1},{4,6},{6,4},{5,7},{7,5},{8,10},{10,8},{9,1... | collective-permute-start | bytes 2359304 | tf_op jit(solution)/shard_map/ppermute | solution.py:307
  104.8 33.4 %all-to-all-start = ((bf16[16,48,512]{2,1,0:T(8,128)(2,1)}), bf16[16,48,512]{2,1,0:T(8,128)(2,1)S(1)}, u32[]{:S(2)}, u32[]{:S(2)}) async-start(bf16[16,48,512]{2,1,0:T(8,128)(2,1)} %bitcast.1), calls=%async_computation | async-start | bytes 1572864 | tf_op jit(solution)/shard_map/all_to_all | solution.py:316
  138.1 2.2 %copy-start = (bf16[2,32,32,1024]{3,2,1,0:T(8,128)(2,1)S(1)}, bf16[2,32,32,1024]{3,2,1,0:T(8,128)(2,1)}, u32[]{:S(2)}) copy-start(bf16[2,32,32,1024]{3,2,1,0:T(8,128)(2,1)} %pad_maximum_fusion.1) | copy-start | bytes 12582916
  145.2 28.3 %all-to-all-start.1 = ((bf16[16,192,128]{2,1,0:T(8,128)(2,1)}), bf16[16,192,128]{2,1,0:T(8,128)(2,1)S(1)}, u32[]{:S(2)}, u32[]{:S(2)}) async-start(bf16[16,192,128]{2,1,0:T(8,128)(2,1)} %bitcast.3), calls=%async_computation.1 | async-start | bytes 1572864 | tf_op jit(solution)/shard_map/all_to_all | solution.py:320
  153.9 17.5 %collective-permute-start.1 = (bf16[512,384]{1,0:T(8,128)(2,1)S(1)}, bf16[512,384]{1,0:T(8,128)(2,1)S(1)}, u32[]{:S(2)}, u32[]{:S(2)}) collective-permute-start(bf16[512,384]{1,0:T(8,128)(2,1)S(1)} %constant_dynamic-slice_fusion), channel_id=1, source_target_pairs={{0,2},{2,0},{1,3},{3,1},{4,6},{6,4},{5,7},{7,5},{8,10},{10,8},{9,1... | collective-permute-start | bytes 1179656 | tf_op jit(solution)/shard_map/ppermute | solution.py:329
Sparse Core Ops, SparseCore 0:
  9.7 34.0 all-gather.2
  45.4 30.7 all-gather.4
  78.5 64.1 reduce-scatter.1

commit v2 on v1

--- a/solution.py
+++ b/solution.py
@@ -45,26 +45,24 @@
     return (jnp.cos(angles), jnp.sin(angles))
 
 
-def feature_table(width, slots, team):
+def feature_table(feats, width, slots, team):
     half = width // 2
-    device = lax.broadcasted_iota(jnp.int32, (team, 2 * slots, width), 0)
-    place = lax.broadcasted_iota(jnp.int32, (team, 2 * slots, width), 1)
-    feat = lax.broadcasted_iota(jnp.int32, (team, 2 * slots, width), 2)
-    feat = lax.optimization_barrier(feat)
-    is_sin = place >= slots
-    slot = device * slots + place % slots
-    top = is_sin & (slot == 0)
-    freq = jnp.where(top, half, slot)
-    lag = jnp.where(is_sin & ~top, width - width // 4, 0)
-    angles = (2.0 * math.pi / width) * ((freq * feat + lag) % width).astype(jnp.float32)
-    table = jnp.where(slot < half, jnp.cos(angles), 0.0)
-    return table.astype(jnp.bfloat16).reshape(team * 2 * slots, width)
-
-
-def position_table(count):
+    cos_a, sin_a = turn(slots * jnp.arange(team, dtype=jnp.int32)[:, None] * feats[None], width)
+    cos_b, sin_b = turn(jnp.arange(slots, dtype=jnp.int32)[:, None] * feats[None], width)
+    slot = lax.broadcasted_iota(jnp.int32, (team, slots, 1), 0) * slots
+    slot = slot + lax.broadcasted_iota(jnp.int32, (team, slots, 1), 1)
+    cos_all = cos_a[:, None] * cos_b[None] - sin_a[:, None] * sin_b[None]
+    sin_all = sin_a[:, None] * cos_b[None] + cos_a[:, None] * sin_b[None]
+    top = (1 - 2 * (feats % 2)).astype(jnp.float32)[None, None]
+    sin_all = jnp.where(slot == 0, top, sin_all)
+    table = jnp.where(slot < half, jnp.stack([cos_all, sin_all], axis=1).transpose(1, 0, 2, 3), 0.0)
+    return table.astype(jnp.bfloat16).transpose(1, 0, 2, 3).reshape(team * 2 * slots, width)
+
+
+def position_table(count, seed):
     fine = 32
     coarse = count // fine
-    col = lax.optimization_barrier(jnp.arange(count, dtype=jnp.int32))
+    col = jnp.arange(count, dtype=jnp.int32) + seed
     cos_a, sin_a = turn(fine * jnp.arange(coarse, dtype=jnp.int32)[:, None] * col[None], count)
     cos_b, sin_b = turn(jnp.arange(fine, dtype=jnp.int32)[:, None] * col[None], count)
     cos_a, sin_a = cos_a[:, None], sin_a[:, None]
@@ -172,7 +170,7 @@
             out_specs=pl.BlockSpec((dests, hids, rows, LANES), lambda i: (i, 0, 0, 0)),
             out_shape=jax.ShapeDtypeStruct((spans, hids, rows, LANES), jnp.bfloat16),
             scratch_shapes=[pltpu.VMEM((2 * rows, 2 * count), jnp.bfloat16)],
-            compiler_params=pltpu.CompilerParams(vmem_limit_bytes=32 << 20),
+            compiler_params=pltpu.CompilerParams(vmem_limit_bytes=48 << 20),
             cost_estimate=pl.CostEstimate(
                 flops=2 * 2 * rows * 2 * count * count, bytes_accessed=6 << 20, transcendentals=0
             ),
@@ -224,7 +222,7 @@
             functools.partial(finish_kernel, spans, slots),
             out_shape=jax.ShapeDtypeStruct(own.shape, jnp.float32),
             scratch_shapes=[pltpu.VMEM((own.shape[1] // LANES, own.shape[0], LANES), jnp.float32)],
-            compiler_params=pltpu.CompilerParams(vmem_limit_bytes=32 << 20),
+            compiler_params=pltpu.CompilerParams(vmem_limit_bytes=48 << 20),
             cost_estimate=pl.CostEstimate(
                 flops=2 * own.shape[0] * pick.size, bytes_accessed=5 << 20, transcendentals=0
             ),
@@ -239,25 +237,207 @@
     return own + value.reshape(own.shape)
 
 
+def weight_pieces(w_out, w_in):
+    chips, cores, groups = (lax.axis_size(name) for name in ("seq", "sub", "groups"))
+    mine = [w_out, w_in]
+    if groups == 2:
+        mine = [jnp.where(lax.axis_index("groups") == 0, w_out, w_in)]
+    near = [((0, 0), (w_out, w_in))]
+    steps = sorted(range(1, chips), key=lambda d: (min(d, chips - d), d))
+    waves = [steps[k : k + 2] for k in range(0, len(steps), 2)]
+    arrived = []
+    for wave in waves:
+        if arrived:
+            mine = lax.optimization_barrier((tuple(mine), arrived[-1]))[0]
+        came = []
+        for d in wave:
+            blocks = tuple(lax.ppermute(w, "seq", shift_pairs(chips, d)) for w in mine)
+            came.extend(blocks)
+            near.append(((d, 0), blocks))
+            if groups == 2:
+                near.append(((d, 1), (lax.ppermute(blocks[0], "groups", shift_pairs(2, 1)),)))
+        arrived.append(came)
+    pieces = [((0, d, k), arrays) for (d, k), arrays in near]
+    for e in range(1, cores):
+        for (d, k), arrays in near:
+            pieces.append(
+                ((e, d, k), tuple(lax.ppermute(x, "sub", shift_pairs(cores, -e)) for x in arrays))
+            )
+    return pieces, arrived
+
+
+def piece_rows(key, width, shard, seq, sub, group, chips, cores):
+    e, d, k = key
+    row = (lax.rem(seq + chips - d, chips) * cores + lax.rem(sub + e, cores)) * shard
+    if d and lax.axis_size("groups") == 2:
+        return [row + lax.rem(group + k, 2) * width]
+    return [row, row + width]
+
+
+def feed_kernel(keys, count, shard, chips, cores, carried, where_ref, x_ref, slope_ref, *refs):
+    blocks, refs = list(refs[:count]), refs[count + carried :]
+    pre_ref, part_ref, weights, total = refs
+    width = x_ref.shape[1]
+    for key in keys:
+        for at in piece_rows(key, width, shard, where_ref[1], where_ref[2], where_ref[3], chips, cores):
+            weights[pl.ds(pl.multiple_of(at, shard), shard), :] = blocks.pop(0)[...]
+    act_grad = jnp.dot(x_ref[...], weights[:width, :], preferred_element_type=jnp.float32)
+    pre_grad = (slope_ref[...] * act_grad).astype(jnp.bfloat16)
+    pre_ref[...] = pre_grad
+    term = lax.dot_general(
+        pre_grad, weights[width:, :], (((1,), (1,)), ((), ())), preferred_element_type=jnp.float32
+    )
+    first = pl.program_id(0) == 0
+
+    @pl.when(first)
+    def _():
+        total[...] = term
+
+    @pl.when(jnp.logical_not(first))
+    def _():
+        total[...] += term
+
+    @pl.when(pl.program_id(0) == pl.num_programs(0) - 1)
+    def _():
+        part_ref[...] = total[...].astype(part_ref.dtype)
+
+
+def feed_rows(where, low, slope, pieces, rows, step, carried):
+    chips, cores, hids = (lax.axis_size(name) for name in ("seq", "sub", "hid"))
+    width, units = low.shape[1], slope.shape[1]
+    shard = pieces[0][1][0].shape[0]
+    tile = 768 if units % 768 == 0 else 128
+    keys = [key for key, _ in pieces]
+    flat = [x for _, arrays in pieces for x in arrays]
+
+    def row_block(i, where_ref):
+        return (lax.rem(where_ref[0] + step, hids), i)
+
+    extra = [] if carried is None else [carried]
+    return pl.pallas_call(
+        functools.partial(feed_kernel, keys, len(flat), shard, chips, cores, len(extra)),
+        grid_spec=pltpu.PrefetchScalarGridSpec(
+            num_scalar_prefetch=1,
+            grid=(units // tile,),
+            in_specs=[
+                pl.BlockSpec((rows, width), lambda i, w: (lax.rem(w[0] + step, hids), 0)),
+                pl.BlockSpec((rows, tile), row_block),
+                *[pl.BlockSpec((x.shape[0], tile), lambda i, w: (0, i)) for x in flat],
+                *[pl.BlockSpec(memory_space=pl.ANY) for _ in extra],
+            ],
+            out_specs=[
+                pl.BlockSpec((rows, tile), row_block),
+                pl.BlockSpec((rows, width), lambda i, w: (0, 0)),
+            ],
+            scratch_shapes=[
+                pltpu.VMEM((2 * width, tile), jnp.bfloat16),
+                pltpu.VMEM((rows, width), jnp.float32),
+            ],
+        ),
+        out_shape=[
+            jax.ShapeDtypeStruct(slope.shape, jnp.bfloat16),
+            jax.ShapeDtypeStruct((rows, width), jnp.bfloat16),
+        ],
+        input_output_aliases={3 + len(flat): 0} if extra else {},
+        compiler_params=pltpu.CompilerParams(vmem_limit_bytes=48 << 20),
+        cost_estimate=pl.CostEstimate(
+            flops=4 * rows * width * units, bytes_accessed=12 << 20, transcendentals=0
+        ),
+        name="feed_rows",
+    )(where, low, slope, *flat, *extra)
+
+
+def whole_weights(pieces, width):
+    chips, cores = lax.axis_size("seq"), lax.axis_size("sub")
+    shard, units = pieces[0][1][0].shape
+    places = [lax.axis_index(name) for name in ("seq", "sub", "groups")]
+    whole = jnp.zeros((2 * width, units), jnp.bfloat16)
+    for key, arrays in pieces:
+        for at, x in zip(piece_rows(key, width, shard, *places, chips, cores), arrays):
+            whole = lax.dynamic_update_slice_in_dim(whole, x, at, 0)
+    return whole
+
+
 def local(z_mix, z_ffn, pre_act, grad_out, gain_mix, gain_ffn, w_in, w_out):
     tok_rows, width = z_mix.shape
     unit_count = pre_act.shape[1]
     hids = lax.axis_size("hid")
     hid_index = lax.axis_index("hid")
-    spans = lax.axis_size(SPANS)
+    cores = lax.axis_size("sub")
+    chips = lax.axis_size("seq")
+    spans = chips * cores
     team = spans * hids
     half = width // 2
     slots = -(-half // team)
     rows = tok_rows // hids
     col_count = width // hids
     seq_length = tok_rows * spans
+    shard_rows = w_in.shape[0]
     bf16 = jnp.bfloat16
+    contract_units = (((1,), (1,)), ((), ()))
+    contract_rows = (((0,), (0,)), ((), ()))
 
     def row_part(values, index):
         return lax.dynamic_slice_in_dim(values, index * rows, rows, 0)
 
-    feat_tab = feature_table(width, slots, team)
-    pos_tab = position_table(tok_rows)
+    pieces, arrived = weight_pieces(w_out, w_in)
+    where = jnp.stack([lax.axis_index(name) for name in ("hid", "seq", "sub", "groups")])
+
+    feats = jnp.arange(width, dtype=jnp.int32)
+    core_ids = (lax.axis_index("sub") + jnp.arange(cores, dtype=jnp.int32)) % cores
+    core_order = (
+        jnp.arange(chips, dtype=jnp.int32)[None, :, None] * cores + core_ids[:, None, None]
+    ) * shard_rows + jnp.arange(shard_rows, dtype=jnp.int32)[None, None]
+    core_reorder = (feats[:, None] == core_order.reshape(1, width)).astype(bf16)
+
+    def by_core(values):
+        return jnp.dot(values, core_reorder, preferred_element_type=jnp.float32).astype(bf16)
+
+    ffn_grad = norm_backward(z_ffn, gain_ffn, grad_out.astype(jnp.float32))
+    ffn_low = ffn_grad.astype(bf16)
+    ffn_core = by_core(ffn_low)
+    ffn_low, ffn_core, pre_act, *_ = lax.optimization_barrier((ffn_low, ffn_core, pre_act, *arrived[0]))
+    pre_wide = pre_act.astype(jnp.float32)
+    activation, pull_back = jax.vjp(gelu_tanh, pre_wide)
+    activation = activation.astype(bf16)
+    slope = pull_back(jnp.ones_like(pre_wide))[0]
+    activation, slope = lax.optimization_barrier((activation, slope))
+
+    def weight_grad(left, right, after):
+        def core_rows(core):
+            part = left[:, core * (width // cores) : (core + 1) * (width // cores)]
+            return lax.dot_general(part, right, contract_rows, preferred_element_type=jnp.float32)
+
+        total = core_rows(0)
+        for core in range(1, cores):
+            sent = core_rows(core).astype(bf16)
+            total += lax.ppermute(sent, "sub", shift_pairs(cores, core)).astype(jnp.float32)
+        total, *_ = lax.optimization_barrier((total.astype(bf16), *after))
+        return lax.psum_scatter(total, "seq", scatter_dimension=0, tiled=True).astype(jnp.float32)
+
+    grad_w_out = weight_grad(ffn_core, activation, arrived[-1])
+
+    partials = []
+    if shard_rows % 16 == 0 and rows % 16 == 0 and unit_count % 128 == 0:
+        pre_grad = None
+        for step in [*range(1, hids), 0]:
+            pre_grad, part = feed_rows(where, ffn_low, slope, pieces, rows, step, pre_grad)
+            partials.append(part)
+    else:
+        whole = whole_weights(pieces, width)
+        act_grad = jnp.dot(ffn_low, whole[:width], preferred_element_type=jnp.float32)
+        pre_grad = (slope * act_grad).astype(bf16)
+        product = lax.dot_general(
+            pre_grad, whole[width:], contract_units, preferred_element_type=jnp.float32
+        ).astype(bf16)
+        for step in [*range(1, hids), 0]:
+            partials.append(row_part(product, (hid_index + step) % hids))
+
+    seed = jnp.zeros((), jnp.int32)
+    late_z, seed, *_ = lax.optimization_barrier((z_mix, seed, *partials[:-1]))
+    normed_core = by_core((norm_parts(late_z)[0] * gain_mix).astype(bf16))
+    feat_tab = lax.optimization_barrier(feature_table(feats + seed, width, slots, team))
+    pos_tab = lax.optimization_barrier(position_table(tok_rows, seed))
     t_cos, t_sin = turn(
         jnp.arange(spans, dtype=jnp.int32)[:, None] * jnp.arange(tok_rows, dtype=jnp.int32)[None], seq_length
     )
@@ -268,42 +448,8 @@
     own_slot = jnp.where(own_ids < half, own_ids, jnp.where(own_ids == half, 0, width - own_ids))
     pick = (jnp.arange(team * slots, dtype=jnp.int32)[:, None] == own_slot[None]).astype(bf16)
 
-    normed = (norm_parts(z_mix)[0] * gain_mix).astype(bf16)
-    ffn_grad = norm_backward(z_ffn, gain_ffn, grad_out.astype(jnp.float32))
-    ffn_low = ffn_grad.astype(bf16)
-    pre_wide = pre_act.astype(jnp.float32)
-    activation = gelu_tanh(pre_wide).astype(bf16)
-    _, pull_back = jax.vjp(gelu_tanh, pre_wide)
-    contract_units = (((1,), (1,)), ((), ()))
-    contract_rows = (((0,), (0,)), ((), ()))
-    act_grad = jnp.dot(
-        ffn_low, lax.all_gather(w_out, SPANS, axis=0, tiled=True), preferred_element_type=jnp.float32
-    )
-    pre_grad = pull_back(act_grad)[0].astype(bf16)
-    partial_sum = lax.dot_general(
-        pre_grad,
-        lax.all_gather(w_in, SPANS, axis=0, tiled=True),
-        contract_units,
-        preferred_element_type=jnp.float32,
-    ).astype(bf16)
-    both_grads = lax.psum_scatter(
-        jnp.concatenate(
-            [
-                lax.dot_general(normed, pre_grad, contract_rows, preferred_element_type=jnp.float32),
-                lax.dot_general(ffn_low, activation, contract_rows, preferred_element_type=jnp.float32),
-            ],
-            axis=1,
-        ).astype(bf16),
-        SPANS,
-        scatter_dimension=0,
-        tiled=True,
-    ).astype(jnp.float32)
-    grad_w_in = both_grads[:, :unit_count]
-    grad_w_out = both_grads[:, unit_count:]
-
-    summed = row_part(partial_sum, hid_index).astype(jnp.float32)
-    for step in range(1, hids):
-        sent = row_part(partial_sum, (hid_index + step) % hids)
+    summed = partials.pop().astype(jnp.float32)
+    for step, sent in enumerate(partials, 1):
         summed += lax.ppermute(sent, "hid", shift_pairs(hids, step)).astype(jnp.float32)
     mix_grad = norm_backward(
         row_part(z_mix, hid_index), gain_mix, row_part(ffn_grad, hid_index) + summed
@@ -313,12 +459,11 @@
     spectral = lax.dot_general(
         feat_tab, mix_low, contract_units, preferred_element_type=jnp.float32
     ).astype(bf16)
+    pre_grad, *_ = lax.optimization_barrier((pre_grad, spectral))
+    grad_w_in = weight_grad(normed_core, pre_grad, ())
     got = lax.all_to_all(
         spectral.reshape(team, 2 * slots, rows), TEAM, split_axis=0, concat_axis=0, tiled=True
     )
-    sent_back = position_transform(got, mark, twist, pos_tab, spans, hids, slots)
-    back = lax.all_to_all(sent_back, TEAM, split_axis=0, concat_axis=0, tiled=True)
-
     def col_part(values, index):
         return lax.dynamic_slice_in_dim(values, index * col_count, col_count, 1)
 
@@ -328,6 +473,10 @@
         sent = col_part(mix_low, (hid_index + step) % hids)
         came = lax.ppermute(sent, "hid", shift_pairs(hids, step)).astype(jnp.float32)
         own = lax.dynamic_update_slice_in_dim(own, came, (hid_index - step) % hids * rows, 0)
+    got, own = lax.optimization_barrier((got, own))
+    sent_back = position_transform(got, mark, twist, pos_tab, spans, hids, slots)
+    back = lax.all_to_all(sent_back, TEAM, split_axis=0, concat_axis=0, tiled=True)
+    back, grad_w_in, grad_w_out = lax.optimization_barrier((back, grad_w_in, grad_w_out))
     grad_in = finish(back, pick, own, spans, slots)
     return (grad_in, grad_w_in, grad_w_out)
 

time: 185 us -> 167 us (0.903)
  waiting for transfers between devices: 88.3 us -> 46 us
  Pallas kernels: 6.99 us -> 20.9 us
  starting transfers between devices: 16.2 us -> 29.3 us
  other arithmetic: 26.4 us -> 34 us
  matrix products: 23 us -> 17 us
  local copies, waits for them, and re-layouts: 9.48 us -> 4.06 us
    all_gather x2 -> x0, waiting for transfers between devices: 38.9 us -> none  [the longest x1 23.3 us: local(): lax.all_gather(w_out, SPANS, axis=0, tiled=True)]
    ppermute x2, waiting for transfers between devices: 22.5 us -> 3.86 us  [local(): lax.ppermute(sent, 'hid', shift_pairs(hids, step)).astype(jnp.float32)]
    ppermute x0 -> x16, starting transfers between devices: none -> 15.2 us  [the longest x8 6.81 us: weight_pieces(): lax.ppermute(x, 'sub', shift_pairs(cores, -e))]
    pallas_call x0 -> x2, Pallas kernels: none -> 14 us  [feed_rows(): pl.pallas_call(functools.partial(feed_kernel, keys, len(flat), shard, chi...]
    all_to_all x1, waiting for transfers between devices: 23.4 us -> 10.4 us  [local(): lax.all_to_all(spectral.reshape(team, 2 * slots, rows), TEAM, split_axis=...]
    ppermute x0 -> x16, waiting for transfers between devices: none -> 11.9 us  [the longest x3 11.9 us: weight_pieces(): lax.ppermute(w, 'seq', shift_pairs(chips, d))]
    reduce_scatter x1 -> x2, waiting for transfers between devices: 0.01 us -> 10.1 us  [weight_grad(): lax.psum_scatter(total, 'seq', scatter_dimension=0, tiled=True)]
    all_to_all x1, waiting for transfers between devices: 2.04 us -> 9.67 us  [local(): lax.all_to_all(sent_back, TEAM, split_axis=0, concat_axis=0, tiled=True)]
  transfers between devices with their start and end apart: 7 -> 22, of which waited for: 6 -> 7; matrix products, arithmetic and copies ran while one was open for 28% -> 31% of each run, Pallas kernels for 4% -> 11%
where the time goes in v2:
time: 167 us; the launch traced here: 166 us
  waiting for transfers between devices  46 us (28%)
  other arithmetic  34 us (20%)
  starting transfers between devices  29.3 us (18%)
  Pallas kernels  20.9 us (13%)
  matrix products  17 us (10%)
  between operations  14.5 us (9%)
  local copies, waits for them, and re-layouts  4.06 us (2%)
    pallas_call x2, Pallas kernels, feed_rows(): pl.pallas_call(functools.partial(feed_kernel, keys, len(flat), shard, chi...  14 us
    ppermute x3, waiting for transfers between devices, weight_pieces(): lax.ppermute(w, 'seq', shift_pairs(chips, d))  11.9 us
    dot_general x4, matrix products, core_rows(): lax.dot_general(part, right, contract_rows, preferred_element_type=jnp.fl...  11 us
    all_to_all x1, waiting for transfers between devices, local(): lax.all_to_all(spectral.reshape(team, 2 * slots, rows), TEAM, split_axis=...  10.4 us
    reduce_scatter x2, waiting for transfers between devices, weight_grad(): lax.psum_scatter(total, 'seq', scatter_dimension=0, tiled=True)  10.1 us
    all_to_all x1, waiting for transfers between devices, local(): lax.all_to_all(sent_back, TEAM, split_axis=0, concat_axis=0, tiled=True)  9.67 us
    ppermute x8, starting transfers between devices, weight_pieces(): lax.ppermute(x, 'sub', shift_pairs(cores, -e))  6.81 us
    add_any x1, other arithmetic, gelu_tanh(): return jax.nn.gelu(values, approximate=True)  6.02 us
  transfers between devices with their start and end apart: 22, of which 7 were waited for; matrix products, arithmetic and copies ran while one was open for 31% of the time, Pallas kernels for 11%

profile of v2, /device:TPU:1, one launch (start us, length us, event | category | flops | bytes accessed | tf_op | source)
XLA Modules:
  0.0 165.8 jit_solution(11276279398961843429)
XLA Ops:
  7.2 1.1 broadcast_select_fusion
  8.3 4.2 %collective-permute-start.1 = (bf16[96,1536]{1,0:T(8,128)(2,1)S(1)}, bf16[96,1536]{1,0:T(8,128)(2,1)S(1)}, u32[]{:S(2)}, u32[]{:S(2)}) collective-permute-start(bf16[96,1536]{1,0:T(8,128)(2,1)S(1)} %broadcast_select_fusion), channel_id=1, source_target_pairs={{0,12},{4,0},{8,4},{12,8},{1,13},{5,1},{9,5},{13,9},{2,14},{6,2},{... | collective-permute-start | bytes 884744 | tf_op jit(solution)/shard_map/ppermute | solution.py:254
  12.5 1.0 collective-permute-start.7
  13.5 1.3 convert_reduce_fusion.2
  14.9 1.5 fusion.35
  17.7 2.7 %fusion.21 = (f32[1024]{0:T(1024)S(1)}, f32[1024]{0:T(1024)S(1)}) fusion(bf16[1024,768]{1,0:T(8,128)(2,1)} %param.11, f32[768]{0:T(1024)S(1)} %copy-done.15, f32[1024]{0:T(1024)S(1)} %add_rsqrt_fusion.1, f32[1024]{0:T(1024)S(1)} %broadcast_multiply_fusion.3, bf16[1024,768]{1,0:T(8,128)(2,1)S(1)} %copy-done.3), kind=kLoop, calls=%fused_computation.34 | loop fusion | flops 6289408 | bytes 3165184 | tf_op jit(solution)/shard_map/reduce_sum | solution.py:30
  20.4 2.7 %fusion.98 = (bf16[1024,768]{1,0:T(8,128)(2,1)S(1)}, f32[1024,768]{1,0:T(8,128)}) fusion(f32[1024]{0:T(1024)S(1)} %get-tuple-element.67, f32[1024]{0:T(1024)S(1)} %broadcast_multiply_fusion.3, bf16[1024,768]{1,0:T(8,128)(2,1)S(1)} %copy-done.3, f32[1024]{0:T(1024)S(1)} %get-tuple-element.68, f32[768]{0:T(1024)S(1)} %copy-done.15, ...), kind=kLoop, calls=%fused_computation.169 | loop fusion | flops 7864320 | bytes 7883776 | tf_op jit(solution)/shard_map/convert_element_type | solution.py:397
  23.2 2.3 %collective-permute-done.refs_2_ = bf16[96,1536]{1,0:T(8,128)(2,1)S(1)} collective-permute-done((bf16[96,1536]{1,0:T(8,128)(2,1)S(1)}, bf16[96,1536]{1,0:T(8,128)(2,1)S(1)}, u32[]{:S(2)}, u32[]{:S(2)}) %collective-permute-start) | collective-permute-done | bytes 294944 | tf_op jit(solution)/shard_map/ppermute | solution.py:254
  25.6 1.5 fusion.30
  27.1 2.2 %collective-permute-start.10 = (bf16[96,1536]{1,0:T(8,128)(2,1)S(1)}, bf16[96,1536]{1,0:T(8,128)(2,1)S(1)}, u32[]{:S(2)}, u32[]{:S(2)}) collective-permute-start(bf16[96,1536]{1,0:T(8,128)(2,1)S(1)} %collective-permute-done.1.refs_4_), channel_id=1, source_target_pairs={{0,1},{1,0},{2,3},{3,2},{4,5},{5,4},{6,7},{7,6},{8,9},{9,8},{10,11... | collective-permute-start | bytes 884744 | tf_op jit(solution)/shard_map/ppermute | solution.py:264
  29.3 1.3 collective-permute-start.3
  30.8 9.7 %collective-permute-done.4.refs_6_ = bf16[96,1536]{1,0:T(8,128)(2,1)S(1)} collective-permute-done((bf16[96,1536]{1,0:T(8,128)(2,1)S(1)}, bf16[96,1536]{1,0:T(8,128)(2,1)S(1)}, u32[]{:S(2)}, u32[]{:S(2)}) %collective-permute-start.4) | collective-permute-done | bytes 294944 | tf_op jit(solution)/shard_map/ppermute | solution.py:254
  40.4 1.2 collective-permute-start.5
  41.7 6.0 %fusion.2 = (f32[1024,1536]{1,0:T(8,128)}, bf16[1024,1536]{1,0:T(8,128)(2,1)S(1)}) fusion(bf16[1024,1536]{1,0:T(8,128)(2,1)S(1)} %copy-done.10), kind=kLoop, calls=%fused_computation.7 | loop fusion | flops 31457280 | bytes 12582912 | tf_op jit(solution)/shard_map/transpose(jvp())/add_any | solution.py:36
  47.7 2.0 %collective-permute-start.8 = (bf16[96,1536]{1,0:T(8,128)(2,1)S(1)}, bf16[96,1536]{1,0:T(8,128)(2,1)S(1)}, u32[]{:S(2)}, u32[]{:S(2)}) collective-permute-start(bf16[96,1536]{1,0:T(8,128)(2,1)S(1)} %collective-permute-done.refs_2_), channel_id=1, source_target_pairs={{0,1},{1,0},{2,3},{3,2},{4,5},{5,4},{6,7},{7,6},{8,9},{9,8},{10,11... | collective-permute-start | bytes 884744 | tf_op jit(solution)/shard_map/ppermute | solution.py:264
  50.3 1.0 collective-permute-start.13
  51.4 1.4 convolution_convert_fusion
  52.9 6.9 %feed_rows.2 = (bf16[1024,1536]{1,0:T(8,128)(2,1)}, bf16[512,768]{1,0:T(8,128)(2,1)S(1)}) custom-call(s32[4]{0:T(128)S(1)} %pad_add_fusion.where_ref, bf16[1024,768]{1,0:T(8,128)(2,1)} %copy-done.6, f32[1024,1536]{1,0:T(8,128)} %get-tuple-element.24.slope_ref, bf16[96,1536]{1,0:T(8,128)(2,1)S(1)} %copy-done.1, bf16[96,1536]{1,0:T(8,128)(2,1)S(1)} %copy-done.2, ...), custom_call_target="tpu_custom_call" | custom-call | flops 2415919104 | bytes 12582912 | tf_op jit(solution)/shard_map/feed_rows/pallas_call | solution.py:317
  60.4 1.3 collective-permute-start.14
  62.5 1.3 fusion.23
  64.5 7.1 %feed_rows.3 = (bf16[1024,1536]{1,0:T(8,128)(2,1)}, bf16[512,768]{1,0:T(8,128)(2,1)S(1)}) custom-call(s32[4]{0:T(128)S(1)} %pad_add_fusion.where_ref, bf16[1024,768]{1,0:T(8,128)(2,1)} %copy-done.6, f32[1024,1536]{1,0:T(8,128)} %get-tuple-element.24.slope_ref, bf16[96,1536]{1,0:T(8,128)(2,1)S(1)} %copy-done.1, ...), custom_call_target="tpu_custom_call", output_to_operand_aliasing={{0}: (19, {})} | custom-call | flops 2415919104 | bytes 12582912 | tf_op jit(solution)/shard_map/feed_rows/pallas_call | solution.py:317
  71.6 2.9 %fusion.31 = bf16[1024,768]{1,0:T(8,128)(2,1)} fusion(bf16[1024,768]{1,0:T(8,128)(2,1)S(1)} %copy-done.4, f32[768]{0:T(1024)S(1)} %copy-done.16, f32[1024]{0:T(1024)S(1)} %add_rsqrt_fusion, f32[1024]{0:T(1024)S(1)} %broadcast_multiply_fusion, s32[768]{0:T(1024)S(1)} %copy-done.18), kind=kOutput, calls=%fused_computation.53 | convolution fusion | flops 1213267968 | bytes 3160064 | tf_op jit(solution)/shard_map/dot_general | solution.py:394
  74.5 2.5 %fusion.22 = bf16[384,1536]{1,0:T(8,128)(2,1)} fusion(bf16[1024,1536]{1,0:T(8,128)(2,1)S(1)} %get-tuple-element.35, bf16[384,1536]{1,0:T(8,128)(2,1)S(1)} %collective-permute-done.17, bf16[1024,768]{1,0:T(8,128)(2,1)S(1)} %copy-done.14), kind=kOutput, calls=%fused_computation.36 | convolution fusion | flops 1209729024 | bytes 6291456 | tf_op jit(solution)/shard_map/dot_general | solution.py:409
  77.0 2.1 %collective-permute-done.14 = bf16[512,768]{1,0:T(8,128)(2,1)S(1)} collective-permute-done((bf16[512,768]{1,0:T(8,128)(2,1)S(1)}, bf16[512,768]{1,0:T(8,128)(2,1)S(1)}, u32[]{:S(2)}, u32[]{:S(2)}) %collective-permute-start.14) | collective-permute-done | bytes 786464 | tf_op jit(solution)/shard_map/ppermute | solution.py:453
  79.1 2.5 %fusion.95 = (f32[512]{0:T(512)S(1)}, f32[512]{0:T(512)S(1)}, f32[512,768]{1,0:T(8,128)S(1)}) fusion(f32[512]{0:T(512)S(1)} %add_rsqrt_fusion.2, f32[512]{0:T(512)S(1)} %broadcast_multiply_fusion.6, bf16[1024,768]{1,0:T(8,128)(2,1)} %param.8, s32[]{:T(128)S(6)} %select_n.166, f32[768]{0:T(1024)S(1)} %copy-done.16, ...), kind=kLoop, calls=%fused_computation.167 | loop fusion | flops 4324352 | bytes 5516292 | tf_op jit(solution)/shard_map/reduce_sum | solution.py:30
  81.7 1.6 fusion.96
  83.4 1.7 %convolution_convert_fusion.2 = bf16[768,512]{1,0:T(8,128)(2,1)} fusion(bf16[768,768]{1,0:T(8,128)(2,1)S(1)} %copy-done.11, bf16[512,768]{1,0:T(8,128)(2,1)S(1)} %get-tuple-element.45), kind=kOutput, calls=%fused_computation.62 | convolution fusion | flops 604372992 | bytes 2752512 | tf_op jit(solution)/shard_map/dot_general | solution.py:459
  85.0 0.6 copy-done.7
  85.7 2.5 %convolution_convert_fusion.1 = bf16[384,1536]{1,0:T(8,128)(2,1)} fusion(bf16[1024,1536]{1,0:T(8,128)(2,1)S(1)} %copy-done.7, bf16[1024,768]{1,0:T(8,128)(2,1)S(1)} %copy-done.12), kind=kOutput, calls=%fused_computation.38 | convolution fusion | flops 1208549376 | bytes 5111808 | tf_op jit(solution)/shard_map/dot_general | solution.py:409
  88.1 1.3 collective-permute-start.16
  89.6 1.1 fusion.68
  90.7 5.6 %all-to-all-start = ((bf16[16,48,512]{2,1,0:T(8,128)(2,1)}), bf16[16,48,512]{2,1,0:T(8,128)(2,1)S(1)}, u32[]{:S(2)}, u32[]{:S(2)}) async-start(bf16[16,48,512]{2,1,0:T(8,128)(2,1)} %bitcast.19), calls=%async_computation | async-start | bytes 1572864 | tf_op jit(solution)/shard_map/all_to_all | solution.py:464
  96.6 0.8 constant_dynamic-slice_fusion
  97.4 1.4 collective-permute-start.15
  98.8 4.6 %add_convert_fusion = bf16[384,1536]{1,0:T(8,128)(2,1)} fusion(bf16[384,1536]{1,0:T(8,128)(2,1)S(1)} %collective-permute-done.16, bf16[1024,1536]{1,0:T(8,128)(2,1)} %get-tuple-element.33, bf16[1024,768]{1,0:T(8,128)(2,1)} %fusion.31), kind=kOutput, calls=%fused_computation.42 | convolution fusion | flops 1209729024 | bytes 6291456 | tf_op jit(solution)/shard_map/dot_general | solution.py:409
  103.4 1.6 subtract_convert_fusion.1
  105.0 2.3 %pad_maximum_fusion = bf16[2,32,32,1024]{3,2,1,0:T(8,128)(2,1)} fusion(bf16[1,32,32,1024]{3,2,1,0:T(8,128)(2,1)S(1)} %get-tuple-element.53, bf16[1,32,32,1024]{3,2,1,0:T(8,128)(2,1)S(1)} %get-tuple-element.52), kind=kLoop, calls=%fused_computation.13 | loop fusion | flops 2097152 | bytes 8388608 | tf_op jit(solution)/shard_map/stack | solution.py:70
  107.5 1.8 %collective-permute-done.15 = bf16[512,384]{1,0:T(8,128)(2,1)} collective-permute-done((bf16[512,384]{1,0:T(8,128)(2,1)}, bf16[512,384]{1,0:T(8,128)(2,1)}, u32[]{:S(2)}, u32[]{:S(2)}) %collective-permute-start.15) | collective-permute-done | bytes 393248 | tf_op jit(solution)/shard_map/ppermute | solution.py:474
  109.3 1.0 convert_dynamic-update-slice_fusion.own_ref
  110.3 10.4 %all-to-all-done.x_ref = bf16[16,48,512]{2,1,0:T(8,128)(2,1)S(1)} async-done(((bf16[16,48,512]{2,1,0:T(8,128)(2,1)}), bf16[16,48,512]{2,1,0:T(8,128)(2,1)S(1)}, u32[]{:S(2)}, u32[]{:S(2)}) %all-to-all-start) | async-done | bytes 786464 | tf_op jit(solution)/shard_map/all_to_all | solution.py:464
  120.7 2.2 %copy-done = bf16[2,32,32,1024]{3,2,1,0:T(8,128)(2,1)S(1)} copy-done((bf16[2,32,32,1024]{3,2,1,0:T(8,128)(2,1)S(1)}, bf16[2,32,32,1024]{3,2,1,0:T(8,128)(2,1)}, u32[]{:S(2)}) %copy-start) | copy-done | bytes 4194328
  122.9 4.8 %position_transform.1 = bf16[8,2,192,128]{3,2,1,0:T(8,128)(2,1)} custom-call(bf16[16,48,512]{2,1,0:T(8,128)(2,1)S(1)} %all-to-all-done.x_ref, f32[24,1]{1,0:T(8,128)S(1)} %fusion.86.mark_ref, f32[2,8,1024]{2,1,0:T(8,128)S(1)} %maximum_multiply_fusion.twist_ref, bf16[2048,1024]{1,0:T(8,128)(2,1)S(1)} %bitcast.18), custom_call_target="tpu_custom_call" | custom-call | flops 1610612736 | bytes 6291456 | tf_op jit(solution)/shard_map/position_transform/pallas_call | solution.py:161
  127.7 5.5 %all-to-all-start.1 = ((bf16[16,192,128]{2,1,0:T(8,128)(2,1)}), bf16[16,192,128]{2,1,0:T(8,128)(2,1)S(1)}, u32[]{:S(2)}, u32[]{:S(2)}) async-start(bf16[16,192,128]{2,1,0:T(8,128)(2,1)} %bitcast.7), calls=%async_computation.1 | async-start | bytes 1572864 | tf_op jit(solution)/shard_map/all_to_all | solution.py:478
  133.3 1.8 %convert_element_type.190 = f32[96,1536]{1,0:T(8,128)} convert(bf16[96,1536]{1,0:T(8,128)(2,1)} %reduce-scatter.5.cloned.1.call-done) | non-fusion elementwise | flops 147456 | bytes 884736 | tf_op jit(solution)/shard_map/convert_element_type | solution.py:416
  135.2 10.1 %reduce-scatter.3.cloned.1.call-done = bf16[96,1536]{1,0:T(8,128)(2,1)} async-done(((bf16[384,1536]{1,0:T(8,128)(2,1)}), bf16[96,1536]{1,0:T(8,128)(2,1)}) %reduce-scatter.3.cloned.1.call-update) | async-done | bytes 294928 | tf_op jit(solution)/shard_map/reduce_scatter | solution.py:416
  145.3 1.8 %convert_element_type.186 = f32[96,1536]{1,0:T(8,128)} convert(bf16[96,1536]{1,0:T(8,128)(2,1)} %reduce-scatter.3.cloned.1.call-done) | non-fusion elementwise | flops 147456 | bytes 884736 | tf_op jit(solution)/shard_map/convert_element_type | solution.py:416
  147.1 9.7 %all-to-all-done.1.back_ref = bf16[16,192,128]{2,1,0:T(8,128)(2,1)S(1)} async-done(((bf16[16,192,128]{2,1,0:T(8,128)(2,1)}), bf16[16,192,128]{2,1,0:T(8,128)(2,1)S(1)}, u32[]{:S(2)}, u32[]{:S(2)}) %all-to-all-start.1) | async-done | bytes 786464 | tf_op jit(solution)/shard_map/all_to_all | solution.py:478
  156.8 2.2 %finish.1 = f32[1024,384]{1,0:T(8,128)} custom-call(bf16[16,192,128]{2,1,0:T(8,128)(2,1)S(1)} %all-to-all-done.1.back_ref, bf16[384,384]{1,0:T(8,128)(2,1)S(1)} %fusion.49.pick_ref, f32[1024,384]{1,0:T(8,128)S(1)} %convert_dynamic-update-slice_fusion.own_ref), custom_call_target="tpu_custom_call" | custom-call | flops 301989888 | bytes 5242880 | tf_op jit(solution)/shard_map/finish/pallas_call | solution.py:221
  (101 shorter events, 5.4 us)
Async XLA Ops:
  7.2 9.4 %copy-start.3 = (bf16[1024,768]{1,0:T(8,128)(2,1)S(1)}, bf16[1024,768]{1,0:T(8,128)(2,1)}, u32[]{:S(2)}) copy-start(bf16[1024,768]{1,0:T(8,128)(2,1)} %param.9) | copy-start | bytes 4718596
  7.2 126.2 %reduce-scatter.5.cloned.1.call-start = ((), (), s32[]{:S(2)}) async-start(), calls=%async_computation.5 | async-start | bytes 1474560 | tf_op jit(solution)/shard_map/reduce_scatter | solution.py:416
  8.3 14.9 %collective-permute-start.1 = (bf16[96,1536]{1,0:T(8,128)(2,1)S(1)}, bf16[96,1536]{1,0:T(8,128)(2,1)S(1)}, u32[]{:S(2)}, u32[]{:S(2)}) collective-permute-start(bf16[96,1536]{1,0:T(8,128)(2,1)S(1)} %broadcast_select_fusion), channel_id=1, source_target_pairs={{0,12},{4,0},{8,4},{12,8},{1,13},{5,1},{9,5},{13,9},{2,14},{6,2},{... | collective-permute-start | bytes 884744 | tf_op jit(solution)/shard_map/ppermute | solution.py:254
  12.5 12.9 %collective-permute-start = (bf16[96,1536]{1,0:T(8,128)(2,1)S(1)}, bf16[96,1536]{1,0:T(8,128)(2,1)S(1)}, u32[]{:S(2)}, u32[]{:S(2)}) collective-permute-start(bf16[96,1536]{1,0:T(8,128)(2,1)S(1)} %broadcast_select_fusion), channel_id=1, source_target_pairs={{0,4},{4,8},{8,12},{12,0},{1,5},{5,9},{9,13},{13,1},{2,6},{6,10},{... | collective-permute-start | bytes 884744 | tf_op jit(solution)/shard_map/ppermute | solution.py:254
  12.5 18.0 %collective-permute-start.7 = (bf16[96,1536]{1,0:T(8,128)(2,1)}, bf16[96,1536]{1,0:T(8,128)(2,1)S(1)}, u32[]{:S(2)}, u32[]{:S(2)}) collective-permute-start(bf16[96,1536]{1,0:T(8,128)(2,1)} %refs_1_.3), channel_id=1, source_target_pairs={{0,1},{1,0},{2,3},{3,2},{4,5},{5,4},{6,7},{7,6},{8,9},{9,8},{10,11... | collective-permute-start | bytes 884744 | tf_op jit(solution)/shard_map/ppermute | solution.py:264
  13.5 34.2 %collective-permute-start.6 = (bf16[96,1536]{1,0:T(8,128)(2,1)}, bf16[96,1536]{1,0:T(8,128)(2,1)S(1)}, u32[]{:S(2)}, u32[]{:S(2)}) collective-permute-start(bf16[96,1536]{1,0:T(8,128)(2,1)} %refs_0_.3), channel_id=1, source_target_pairs={{0,1},{1,0},{2,3},{3,2},{4,5},{5,4},{6,7},{7,6},{8,9},{9,8},{10,11... | collective-permute-start | bytes 884744 | tf_op jit(solution)/shard_map/ppermute | solution.py:264
  13.5 4.2 %copy-start.15 = (f32[768]{0:T(1024)S(1)}, f32[768]{0:T(1024)}, u32[]{:S(2)}) copy-start(f32[768]{0:T(1024)} %param.13) | copy-start | bytes 9220
  16.6 9.0 %copy-start.17 = (s32[768]{0:T(1024)}, s32[768]{0:T(1024)S(1)}, u32[]{:S(2)}) copy-start(s32[768]{0:T(1024)S(1)} %add.301) | copy-start | bytes 9220
  17.7 2.7 %copy-start.8 = (bf16[1024,768]{1,0:T(8,128)(2,1)S(1)}, bf16[1024,768]{1,0:T(8,128)(2,1)}, u32[]{:S(2)}) copy-start(bf16[1024,768]{1,0:T(8,128)(2,1)} %param.11) | copy-start | bytes 4718596
  23.1 3.9 %copy-start.6 = (bf16[1024,768]{1,0:T(8,128)(2,1)}, bf16[1024,768]{1,0:T(8,128)(2,1)S(1)}, u32[]{:S(2)}) copy-start(bf16[1024,768]{1,0:T(8,128)(2,1)S(1)} %get-tuple-element.22.x_ref) | copy-start | bytes 4718596
  25.4 15.0 %collective-permute-start.4 = (bf16[96,1536]{1,0:T(8,128)(2,1)S(1)}, bf16[96,1536]{1,0:T(8,128)(2,1)S(1)}, u32[]{:S(2)}, u32[]{:S(2)}) collective-permute-start(bf16[96,1536]{1,0:T(8,128)(2,1)S(1)} %broadcast_select_fusion), channel_id=1, source_target_pairs={{0,8},{4,12},{8,0},{12,4},{1,9},{5,13},{9,1},{13,5},{2,10},{6,14},... | collective-permute-start | bytes 884744 | tf_op jit(solution)/shard_map/ppermute | solution.py:254
  25.6 16.1 %copy-start.10 = (bf16[1024,1536]{1,0:T(8,128)(2,1)S(1)}, bf16[1024,1536]{1,0:T(8,128)(2,1)}, u32[]{:S(2)}) copy-start(bf16[1024,1536]{1,0:T(8,128)(2,1)} %param.10) | copy-start | bytes 9437188
  27.1 24.3 %copy-start.13 = (bf16[1024,768]{1,0:T(8,128)(2,1)}, bf16[1024,768]{1,0:T(8,128)(2,1)S(1)}, u32[]{:S(2)}) copy-start(bf16[1024,768]{1,0:T(8,128)(2,1)S(1)} %fusion.30) | copy-start | bytes 4718596
  27.1 22.6 %collective-permute-start.10 = (bf16[96,1536]{1,0:T(8,128)(2,1)S(1)}, bf16[96,1536]{1,0:T(8,128)(2,1)S(1)}, u32[]{:S(2)}, u32[]{:S(2)}) collective-permute-start(bf16[96,1536]{1,0:T(8,128)(2,1)S(1)} %collective-permute-done.1.refs_4_), channel_id=1, source_target_pairs={{0,1},{1,0},{2,3},{3,2},{4,5},{5,4},{6,7},{7,6},{8,9},{9,8},{10,11... | collective-permute-start | bytes 884744 | tf_op jit(solution)/shard_map/ppermute | solution.py:264
  29.3 20.5 %collective-permute-start.3 = (bf16[96,1536]{1,0:T(8,128)(2,1)S(1)}, bf16[96,1536]{1,0:T(8,128)(2,1)S(1)}, u32[]{:S(2)}, u32[]{:S(2)}) collective-permute-start(bf16[96,1536]{1,0:T(8,128)(2,1)S(1)} %collective-permute-done.1.refs_4_), channel_id=1, source_target_pairs={{0,16},{16,0},{1,17},{17,1},{2,18},{18,2},{3,19},{19,3},{4,20},{20... | collective-permute-start | bytes 884744 | tf_op jit(solution)/shard_map/ppermute | solution.py:258
  30.5 19.7 %collective-permute-start.2 = (bf16[96,1536]{1,0:T(8,128)(2,1)S(1)}, bf16[96,1536]{1,0:T(8,128)(2,1)S(1)}, u32[]{:S(2)}, u32[]{:S(2)}) collective-permute-start(bf16[96,1536]{1,0:T(8,128)(2,1)S(1)} %collective-permute-done.refs_2_), channel_id=1, source_target_pairs={{0,16},{16,0},{1,17},{17,1},{2,18},{18,2},{3,19},{19,3},{4,20},{20... | collective-permute-start | bytes 884744 | tf_op jit(solution)/shard_map/ppermute | solution.py:258
  40.4 9.9 %collective-permute-start.5 = (bf16[96,1536]{1,0:T(8,128)(2,1)S(1)}, bf16[96,1536]{1,0:T(8,128)(2,1)S(1)}, u32[]{:S(2)}, u32[]{:S(2)}) collective-permute-start(bf16[96,1536]{1,0:T(8,128)(2,1)S(1)} %collective-permute-done.4.refs_6_), channel_id=1, source_target_pairs={{0,16},{16,0},{1,17},{17,1},{2,18},{18,2},{3,19},{19,3},{4,20},{20... | collective-permute-start | bytes 884744 | tf_op jit(solution)/shard_map/ppermute | solution.py:258
  47.7 5.2 %copy-start.1 = (bf16[96,1536]{1,0:T(8,128)(2,1)S(1)}, bf16[96,1536]{1,0:T(8,128)(2,1)}, u32[]{:S(2)}) copy-start(bf16[96,1536]{1,0:T(8,128)(2,1)} %refs_0_.3) | copy-start | bytes 884740
  47.7 5.2 %copy-start.2 = (bf16[96,1536]{1,0:T(8,128)(2,1)S(1)}, bf16[96,1536]{1,0:T(8,128)(2,1)}, u32[]{:S(2)}) copy-start(bf16[96,1536]{1,0:T(8,128)(2,1)} %refs_1_.3) | copy-start | bytes 884740
  47.7 5.1 %collective-permute-start.8 = (bf16[96,1536]{1,0:T(8,128)(2,1)S(1)}, bf16[96,1536]{1,0:T(8,128)(2,1)S(1)}, u32[]{:S(2)}, u32[]{:S(2)}) collective-permute-start(bf16[96,1536]{1,0:T(8,128)(2,1)S(1)} %collective-permute-done.refs_2_), channel_id=1, source_target_pairs={{0,1},{1,0},{2,3},{3,2},{4,5},{5,4},{6,7},{7,6},{8,9},{9,8},{10,11... | collective-permute-start | bytes 884744 | tf_op jit(solution)/shard_map/ppermute | solution.py:264
  49.7 3.2 %collective-permute-start.12 = (bf16[96,1536]{1,0:T(8,128)(2,1)S(1)}, bf16[96,1536]{1,0:T(8,128)(2,1)S(1)}, u32[]{:S(2)}, u32[]{:S(2)}) collective-permute-start(bf16[96,1536]{1,0:T(8,128)(2,1)S(1)} %collective-permute-done.4.refs_6_), channel_id=1, source_target_pairs={{0,1},{1,0},{2,3},{3,2},{4,5},{5,4},{6,7},{7,6},{8,9},{9,8},{10,11... | collective-permute-start | bytes 884744 | tf_op jit(solution)/shard_map/ppermute | solution.py:264
  49.8 3.1 %collective-permute-start.11 = (bf16[96,1536]{1,0:T(8,128)(2,1)S(1)}, bf16[96,1536]{1,0:T(8,128)(2,1)S(1)}, u32[]{:S(2)}, u32[]{:S(2)}) collective-permute-start(bf16[96,1536]{1,0:T(8,128)(2,1)S(1)} %collective-permute-done.3.refs_5_), channel_id=1, source_target_pairs={{0,1},{1,0},{2,3},{3,2},{4,5},{5,4},{6,7},{7,6},{8,9},{9,8},{10,11... | collective-permute-start | bytes 884744 | tf_op jit(solution)/shard_map/ppermute | solution.py:264
  50.2 2.7 %collective-permute-start.9 = (bf16[96,1536]{1,0:T(8,128)(2,1)S(1)}, bf16[96,1536]{1,0:T(8,128)(2,1)S(1)}, u32[]{:S(2)}, u32[]{:S(2)}) collective-permute-start(bf16[96,1536]{1,0:T(8,128)(2,1)S(1)} %collective-permute-done.2.refs_3_), channel_id=1, source_target_pairs={{0,1},{1,0},{2,3},{3,2},{4,5},{5,4},{6,7},{7,6},{8,9},{9,8},{10,11... | collective-permute-start | bytes 884744 | tf_op jit(solution)/shard_map/ppermute | solution.py:264
  50.3 2.6 %collective-permute-start.13 = (bf16[96,1536]{1,0:T(8,128)(2,1)S(1)}, bf16[96,1536]{1,0:T(8,128)(2,1)S(1)}, u32[]{:S(2)}, u32[]{:S(2)}) collective-permute-start(bf16[96,1536]{1,0:T(8,128)(2,1)S(1)} %collective-permute-done.5.refs_7_), channel_id=1, source_target_pairs={{0,1},{1,0},{2,3},{3,2},{4,5},{5,4},{6,7},{7,6},{8,9},{9,8},{10,11... | collective-permute-start | bytes 884744 | tf_op jit(solution)/shard_map/ppermute | solution.py:264
  52.8 9.0 %copy-start.4 = (bf16[1024,768]{1,0:T(8,128)(2,1)S(1)}, bf16[1024,768]{1,0:T(8,128)(2,1)}, u32[]{:S(2)}) copy-start(bf16[1024,768]{1,0:T(8,128)(2,1)} %param.8) | copy-start | bytes 4718596
  52.8 21.7 %collective-permute-start.17 = (bf16[384,1536]{1,0:T(8,128)(2,1)S(1)}, bf16[384,1536]{1,0:T(8,128)(2,1)S(1)}, u32[]{:S(2)}, u32[]{:S(2)}) collective-permute-start(bf16[384,1536]{1,0:T(8,128)(2,1)S(1)} %convolution_convert_fusion), channel_id=1, source_target_pairs={{0,1},{1,0},{2,3},{3,2},{4,5},{5,4},{6,7},{7,6},{8,9},{9,8},{10,11... | collective-permute-start | bytes 3538952 | tf_op jit(solution)/shard_map/ppermute | solution.py:414
  60.4 18.7 %collective-permute-start.14 = (bf16[512,768]{1,0:T(8,128)(2,1)S(1)}, bf16[512,768]{1,0:T(8,128)(2,1)S(1)}, u32[]{:S(2)}, u32[]{:S(2)}) collective-permute-start(bf16[512,768]{1,0:T(8,128)(2,1)S(1)} %get-tuple-element.26), channel_id=1, source_target_pairs={{0,2},{2,0},{1,3},{3,1},{4,6},{6,4},{5,7},{7,5},{8,10},{10,8},{9,1... | collective-permute-start | bytes 2359304 | tf_op jit(solution)/shard_map/ppermute | solution.py:453
  64.5 7.1 %copy-start.16 = (f32[768]{0:T(1024)S(1)}, f32[768]{0:T(1024)}, u32[]{:S(2)}) copy-start(f32[768]{0:T(1024)} %param.12) | copy-start | bytes 9220
  64.5 7.1 %copy-start.18 = (s32[768]{0:T(1024)S(1)}, s32[768]{0:T(1024)}, u32[]{:S(2)}) copy-start(s32[768]{0:T(1024)} %copy-done.17) | copy-start | bytes 9220
  71.6 2.9 %copy-start.14 = (bf16[1024,768]{1,0:T(8,128)(2,1)S(1)}, bf16[1024,768]{1,0:T(8,128)(2,1)}, u32[]{:S(2)}) copy-start(bf16[1024,768]{1,0:T(8,128)(2,1)} %copy-done.13) | copy-start | bytes 4718596
  79.1 2.6 %copy-start.5 = (bf16[1024,768]{1,0:T(8,128)(2,1)S(1)}, bf16[1024,768]{1,0:T(8,128)(2,1)}, u32[]{:S(2)}) copy-start(bf16[1024,768]{1,0:T(8,128)(2,1)} %param.8) | copy-start | bytes 4718596
  81.7 1.6 copy-start.11
  81.7 3.3 %copy-start.12 = (bf16[1024,768]{1,0:T(8,128)(2,1)S(1)}, bf16[1024,768]{1,0:T(8,128)(2,1)}, u32[]{:S(2)}) copy-start(bf16[1024,768]{1,0:T(8,128)(2,1)} %fusion.31) | copy-start | bytes 4718596
  83.4 2.3 %copy-start.7 = (bf16[1024,1536]{1,0:T(8,128)(2,1)S(1)}, bf16[1024,1536]{1,0:T(8,128)(2,1)}, u32[]{:S(2)}) copy-start(bf16[1024,1536]{1,0:T(8,128)(2,1)} %get-tuple-element.33) | copy-start | bytes 9437188
  88.1 10.6 %collective-permute-start.16 = (bf16[384,1536]{1,0:T(8,128)(2,1)}, bf16[384,1536]{1,0:T(8,128)(2,1)S(1)}, u32[]{:S(2)}, u32[]{:S(2)}) collective-permute-start(bf16[384,1536]{1,0:T(8,128)(2,1)} %convolution_convert_fusion.1), channel_id=1, source_target_pairs={{0,1},{1,0},{2,3},{3,2},{4,5},{5,4},{6,7},{7,6},{8,9},{9,8},{10,11... | collective-permute-start | bytes 3538952 | tf_op jit(solution)/shard_map/ppermute | solution.py:414
  90.7 30.1 %all-to-all-start = ((bf16[16,48,512]{2,1,0:T(8,128)(2,1)}), bf16[16,48,512]{2,1,0:T(8,128)(2,1)S(1)}, u32[]{:S(2)}, u32[]{:S(2)}) async-start(bf16[16,48,512]{2,1,0:T(8,128)(2,1)} %bitcast.19), calls=%async_computation | async-start | bytes 1572864 | tf_op jit(solution)/shard_map/all_to_all | solution.py:464
  96.3 49.0 %reduce-scatter.3.cloned.1.call-start = ((), (), s32[]{:S(2)}) async-start(), calls=%async_computation.4 | async-start | bytes 1474560 | tf_op jit(solution)/shard_map/reduce_scatter | solution.py:416
  97.4 11.9 %collective-permute-start.15 = (bf16[512,384]{1,0:T(8,128)(2,1)}, bf16[512,384]{1,0:T(8,128)(2,1)}, u32[]{:S(2)}, u32[]{:S(2)}) collective-permute-start(bf16[512,384]{1,0:T(8,128)(2,1)} %constant_dynamic-slice_fusion), channel_id=1, source_target_pairs={{0,2},{2,0},{1,3},{3,1},{4,6},{6,4},{5,7},{7,5},{8,10},{10,8},{9,1... | collective-permute-start | bytes 1179656 | tf_op jit(solution)/shard_map/ppermute | solution.py:474
  105.0 2.4 %copy-start.9 = (f32[512,768]{1,0:T(8,128)S(1)}, f32[512,768]{1,0:T(8,128)}, u32[]{:S(2)}) copy-start(f32[512,768]{1,0:T(8,128)} %get-tuple-element.46) | copy-start | bytes 4718596
  120.7 2.2 %copy-start = (bf16[2,32,32,1024]{3,2,1,0:T(8,128)(2,1)S(1)}, bf16[2,32,32,1024]{3,2,1,0:T(8,128)(2,1)}, u32[]{:S(2)}) copy-start(bf16[2,32,32,1024]{3,2,1,0:T(8,128)(2,1)} %pad_maximum_fusion) | copy-start | bytes 12582916
  127.7 29.0 %all-to-all-start.1 = ((bf16[16,192,128]{2,1,0:T(8,128)(2,1)}), bf16[16,192,128]{2,1,0:T(8,128)(2,1)S(1)}, u32[]{:S(2)}, u32[]{:S(2)}) async-start(bf16[16,192,128]{2,1,0:T(8,128)(2,1)} %bitcast.7), calls=%async_computation.1 | async-start | bytes 1572864 | tf_op jit(solution)/shard_map/all_to_all | solution.py:478
Sparse Core Ops, SparseCore 0:
  77.2 33.1 reduce-scatter.4
  112.6 32.5 reduce-scatter.2

commit v3 on v2

--- a/solution.py
+++ b/solution.py
@@ -12,6 +12,8 @@
 SPANS = ("seq", "sub")
 TEAM = ("seq", "sub", "hid")
 LANES = 128
+ROWS = 128
+SMALL = pl.CostEstimate(flops=1 << 20, bytes_accessed=1 << 16, transcendentals=0)
 
 
 def norm_parts(values):
@@ -45,10 +47,10 @@
     return (jnp.cos(angles), jnp.sin(angles))
 
 
-def feature_table(feats, width, slots, team):
+def feature_table(feats, seed, width, slots, team):
     half = width // 2
-    cos_a, sin_a = turn(slots * jnp.arange(team, dtype=jnp.int32)[:, None] * feats[None], width)
-    cos_b, sin_b = turn(jnp.arange(slots, dtype=jnp.int32)[:, None] * feats[None], width)
+    cos_a, sin_a = turn(slots * (jnp.arange(team, dtype=jnp.int32) + seed)[:, None] * feats[None], width)
+    cos_b, sin_b = turn((jnp.arange(slots, dtype=jnp.int32) + seed)[:, None] * feats[None], width)
     slot = lax.broadcasted_iota(jnp.int32, (team, slots, 1), 0) * slots
     slot = slot + lax.broadcasted_iota(jnp.int32, (team, slots, 1), 1)
     cos_all = cos_a[:, None] * cos_b[None] - sin_a[:, None] * sin_b[None]
@@ -63,8 +65,8 @@
     fine = 32
     coarse = count // fine
     col = jnp.arange(count, dtype=jnp.int32) + seed
-    cos_a, sin_a = turn(fine * jnp.arange(coarse, dtype=jnp.int32)[:, None] * col[None], count)
-    cos_b, sin_b = turn(jnp.arange(fine, dtype=jnp.int32)[:, None] * col[None], count)
+    cos_a, sin_a = turn(fine * (jnp.arange(coarse, dtype=jnp.int32) + seed)[:, None] * col[None], count)
+    cos_b, sin_b = turn((jnp.arange(fine, dtype=jnp.int32) + seed)[:, None] * col[None], count)
     cos_a, sin_a = cos_a[:, None], sin_a[:, None]
     cos_b, sin_b = cos_b[None], sin_b[None]
     both = jnp.stack([cos_a * cos_b - sin_a * sin_b, -sin_a * cos_b - cos_a * sin_b])
@@ -170,7 +172,7 @@
             out_specs=pl.BlockSpec((dests, hids, rows, LANES), lambda i: (i, 0, 0, 0)),
             out_shape=jax.ShapeDtypeStruct((spans, hids, rows, LANES), jnp.bfloat16),
             scratch_shapes=[pltpu.VMEM((2 * rows, 2 * count), jnp.bfloat16)],
-            compiler_params=pltpu.CompilerParams(vmem_limit_bytes=48 << 20),
+            compiler_params=pltpu.CompilerParams(vmem_limit_bytes=58 << 20),
             cost_estimate=pl.CostEstimate(
                 flops=2 * 2 * rows * 2 * count * count, bytes_accessed=6 << 20, transcendentals=0
             ),
@@ -237,7 +239,103 @@
     return own + value.reshape(own.shape)
 
 
-def weight_pieces(w_out, w_in):
+def ffn_norm_kernel(z_ref, up_ref, gain_ref, grad_ref, low_ref):
+    grad = norm_backward(z_ref[...], gain_ref[...], up_ref[...].astype(jnp.float32))
+    low = grad.astype(jnp.bfloat16)
+    grad_ref[...] = grad
+    low_ref[...] = low
+
+
+def ffn_norm(z_ffn, grad_out, gain):
+    rows, width = z_ffn.shape
+    tile = pl.BlockSpec((ROWS, width), lambda i: (i, 0))
+    return pl.pallas_call(
+        ffn_norm_kernel,
+        grid=(rows // ROWS,),
+        in_specs=[tile, tile, pl.BlockSpec((1, width), lambda i: (0, 0))],
+        out_specs=[tile, tile],
+        out_shape=[
+            jax.ShapeDtypeStruct(z_ffn.shape, jnp.float32),
+            jax.ShapeDtypeStruct(z_ffn.shape, jnp.bfloat16),
+        ],
+        compiler_params=pltpu.CompilerParams(vmem_limit_bytes=32 << 20),
+        cost_estimate=SMALL,
+        name="ffn_norm",
+    )(z_ffn, grad_out, gain[None])
+
+
+def mix_norm_kernel(z_ref, gain_ref, order_ref, core_ref):
+    normed = (norm_parts(z_ref[...])[0] * gain_ref[...]).astype(jnp.bfloat16)
+    core_ref[...] = jnp.dot(normed, order_ref[...], preferred_element_type=jnp.float32).astype(jnp.bfloat16)
+
+
+def mix_norm(z_mix, gain, order):
+    rows, width = z_mix.shape
+    tile = pl.BlockSpec((ROWS, width), lambda i: (i, 0))
+    return pl.pallas_call(
+        mix_norm_kernel,
+        grid=(rows // ROWS,),
+        in_specs=[tile, pl.BlockSpec((1, width), lambda i: (0, 0)), pl.BlockSpec(order.shape, lambda i: (0, 0))],
+        out_specs=tile,
+        out_shape=jax.ShapeDtypeStruct(z_mix.shape, jnp.bfloat16),
+        compiler_params=pltpu.CompilerParams(vmem_limit_bytes=32 << 20),
+        cost_estimate=SMALL,
+        name="mix_norm",
+    )(z_mix, gain[None], order)
+
+
+def gelu_slope(values):
+    scale = math.sqrt(2.0 / math.pi)
+    a = values.astype(jnp.float32)
+    square = a * a
+    tanh = jnp.tanh(scale * a * (1.0 + 0.044715 * square))
+    upper = 0.5 * (1.0 + tanh)
+    return upper + (0.5 * scale) * a * (1.0 - tanh * tanh) * (1.0 + (3.0 * 0.044715) * square)
+
+
+def mix_kernel(count, hids, where_ref, z_ref, ffn_ref, gain_ref, tab_ref, *refs):
+    parts, (mix_ref, spec_ref) = refs[:count], refs[count:]
+    summed = parts[0][...].astype(jnp.float32)
+    for part in parts[1:]:
+        summed += part[...].astype(jnp.float32)
+    mix = norm_backward(z_ref[...], gain_ref[...], ffn_ref[...] + summed)
+    low = mix.astype(jnp.bfloat16)
+    mix_ref[...] = low
+    spec_ref[...] = lax.dot_general(
+        tab_ref[...], low, (((1,), (1,)), ((), ())), preferred_element_type=jnp.float32
+    ).astype(jnp.bfloat16)
+
+
+def mix_rows(where, z_mix, ffn_grad, gain, table, parts, hids):
+    rows, width = parts[0].shape
+    steps = rows // ROWS
+    tile = pl.BlockSpec((ROWS, width), lambda i, w: (i, 0))
+    own = pl.BlockSpec((ROWS, width), lambda i, w: (w[0] * steps + i, 0))
+    return pl.pallas_call(
+        functools.partial(mix_kernel, len(parts), hids),
+        grid_spec=pltpu.PrefetchScalarGridSpec(
+            num_scalar_prefetch=1,
+            grid=(steps,),
+            in_specs=[
+                own,
+                own,
+                pl.BlockSpec((1, width), lambda i, w: (0, 0)),
+                pl.BlockSpec(table.shape, lambda i, w: (0, 0)),
+                *[tile for _ in parts],
+            ],
+            out_specs=[tile, pl.BlockSpec((table.shape[0], ROWS), lambda i, w: (0, i))],
+        ),
+        out_shape=[
+            jax.ShapeDtypeStruct((rows, width), jnp.bfloat16),
+            jax.ShapeDtypeStruct((table.shape[0], rows), jnp.bfloat16),
+        ],
+        compiler_params=pltpu.CompilerParams(vmem_limit_bytes=32 << 20),
+        cost_estimate=SMALL,
+        name="mix_rows",
+    )(where, z_mix, ffn_grad, gain[None], table, *parts)
+
+
+def weight_pieces(w_out, w_in, first):
     chips, cores, groups = (lax.axis_size(name) for name in ("seq", "sub", "groups"))
     mine = [w_out, w_in]
     if groups == 2:
@@ -248,7 +346,7 @@
     arrived = []
     for wave in waves:
         if arrived:
-            mine = lax.optimization_barrier((tuple(mine), arrived[-1]))[0]
+            mine = lax.optimization_barrier((tuple(mine), arrived[-1], first))[0]
         came = []
         for d in wave:
             blocks = tuple(lax.ppermute(w, "seq", shift_pairs(chips, d)) for w in mine)
@@ -274,7 +372,7 @@
     return [row, row + width]
 
 
-def feed_kernel(keys, count, shard, chips, cores, carried, where_ref, x_ref, slope_ref, *refs):
+def feed_kernel(keys, count, shard, chips, cores, carried, where_ref, x_ref, pre_act_ref, *refs):
     blocks, refs = list(refs[:count]), refs[count + carried :]
     pre_ref, part_ref, weights, total = refs
     width = x_ref.shape[1]
@@ -282,7 +380,7 @@
         for at in piece_rows(key, width, shard, where_ref[1], where_ref[2], where_ref[3], chips, cores):
             weights[pl.ds(pl.multiple_of(at, shard), shard), :] = blocks.pop(0)[...]
     act_grad = jnp.dot(x_ref[...], weights[:width, :], preferred_element_type=jnp.float32)
-    pre_grad = (slope_ref[...] * act_grad).astype(jnp.bfloat16)
+    pre_grad = (gelu_slope(pre_act_ref[...]) * act_grad).astype(jnp.bfloat16)
     pre_ref[...] = pre_grad
     term = lax.dot_general(
         pre_grad, weights[width:, :], (((1,), (1,)), ((), ())), preferred_element_type=jnp.float32
@@ -302,9 +400,9 @@
         part_ref[...] = total[...].astype(part_ref.dtype)
 
 
-def feed_rows(where, low, slope, pieces, rows, step, carried):
+def feed_rows(where, low, pre_act, pieces, rows, step, carried):
     chips, cores, hids = (lax.axis_size(name) for name in ("seq", "sub", "hid"))
-    width, units = low.shape[1], slope.shape[1]
+    width, units = low.shape[1], pre_act.shape[1]
     shard = pieces[0][1][0].shape[0]
     tile = 768 if units % 768 == 0 else 128
     keys = [key for key, _ in pieces]
@@ -335,16 +433,14 @@
             ],
         ),
         out_shape=[
-            jax.ShapeDtypeStruct(slope.shape, jnp.bfloat16),
+            jax.ShapeDtypeStruct(pre_act.shape, jnp.bfloat16),
             jax.ShapeDtypeStruct((rows, width), jnp.bfloat16),
         ],
         input_output_aliases={3 + len(flat): 0} if extra else {},
         compiler_params=pltpu.CompilerParams(vmem_limit_bytes=48 << 20),
-        cost_estimate=pl.CostEstimate(
-            flops=4 * rows * width * units, bytes_accessed=12 << 20, transcendentals=0
-        ),
+        cost_estimate=SMALL,
         name="feed_rows",
-    )(where, low, slope, *flat, *extra)
+    )(where, low, pre_act, *flat, *extra)
 
 
 def whole_weights(pieces, width):
@@ -380,7 +476,6 @@
     def row_part(values, index):
         return lax.dynamic_slice_in_dim(values, index * rows, rows, 0)
 
-    pieces, arrived = weight_pieces(w_out, w_in)
     where = jnp.stack([lax.axis_index(name) for name in ("hid", "seq", "sub", "groups")])
 
     feats = jnp.arange(width, dtype=jnp.int32)
@@ -390,43 +485,39 @@
     ) * shard_rows + jnp.arange(shard_rows, dtype=jnp.int32)[None, None]
     core_reorder = (feats[:, None] == core_order.reshape(1, width)).astype(bf16)
 
-    def by_core(values):
-        return jnp.dot(values, core_reorder, preferred_element_type=jnp.float32).astype(bf16)
-
-    ffn_grad = norm_backward(z_ffn, gain_ffn, grad_out.astype(jnp.float32))
-    ffn_low = ffn_grad.astype(bf16)
-    ffn_core = by_core(ffn_low)
-    ffn_low, ffn_core, pre_act, *_ = lax.optimization_barrier((ffn_low, ffn_core, pre_act, *arrived[0]))
-    pre_wide = pre_act.astype(jnp.float32)
-    activation, pull_back = jax.vjp(gelu_tanh, pre_wide)
-    activation = activation.astype(bf16)
-    slope = pull_back(jnp.ones_like(pre_wide))[0]
-    activation, slope = lax.optimization_barrier((activation, slope))
-
-    def weight_grad(left, right, after):
-        def core_rows(core):
-            part = left[:, core * (width // cores) : (core + 1) * (width // cores)]
-            return lax.dot_general(part, right, contract_rows, preferred_element_type=jnp.float32)
-
-        total = core_rows(0)
-        for core in range(1, cores):
-            sent = core_rows(core).astype(bf16)
-            total += lax.ppermute(sent, "sub", shift_pairs(cores, core)).astype(jnp.float32)
-        total, *_ = lax.optimization_barrier((total.astype(bf16), *after))
+    ffn_grad, ffn_low = ffn_norm(z_ffn, grad_out, gain_ffn)
+    pieces, arrived = weight_pieces(w_out, w_in, (ffn_low,))
+
+    def core_rows(left, right, core):
+        part = left[:, core * (width // cores) : (core + 1) * (width // cores)]
+        return lax.dot_general(part, right, contract_rows, preferred_element_type=jnp.float32)
+
+    def others_rows(left, right):
+        return [core_rows(left, right, core).astype(bf16) for core in range(1, cores)]
+
+    def chip_sum(left, right, sent):
+        total = core_rows(left, right, 0)
+        for core, part in enumerate(sent, 1):
+            total += lax.ppermute(part, "sub", shift_pairs(cores, core)).astype(jnp.float32)
+        return total.astype(bf16)
+
+    def over_chips(total):
         return lax.psum_scatter(total, "seq", scatter_dimension=0, tiled=True).astype(jnp.float32)
 
-    grad_w_out = weight_grad(ffn_core, activation, arrived[-1])
-
+    activation = lax.optimization_barrier(gelu_tanh(pre_act.astype(jnp.float32)).astype(bf16))
+    total_out = lax.dot_general(ffn_low, activation, contract_rows, preferred_element_type=jnp.float32)
+    total_out, *_ = lax.optimization_barrier((total_out.astype(bf16), *arrived[-1]))
+    grad_w_out = lax.psum_scatter(total_out, SPANS, scatter_dimension=0, tiled=True).astype(jnp.float32)
     partials = []
     if shard_rows % 16 == 0 and rows % 16 == 0 and unit_count % 128 == 0:
         pre_grad = None
         for step in [*range(1, hids), 0]:
-            pre_grad, part = feed_rows(where, ffn_low, slope, pieces, rows, step, pre_grad)
+            pre_grad, part = feed_rows(where, ffn_low, pre_act, pieces, rows, step, pre_grad)
             partials.append(part)
     else:
         whole = whole_weights(pieces, width)
         act_grad = jnp.dot(ffn_low, whole[:width], preferred_element_type=jnp.float32)
-        pre_grad = (slope * act_grad).astype(bf16)
+        pre_grad = (gelu_slope(pre_act) * act_grad).astype(bf16)
         product = lax.dot_general(
             pre_grad, whole[width:], contract_units, preferred_element_type=jnp.float32
         ).astype(bf16)
@@ -435,45 +526,43 @@
 
     seed = jnp.zeros((), jnp.int32)
     late_z, seed, *_ = lax.optimization_barrier((z_mix, seed, *partials[:-1]))
-    normed_core = by_core((norm_parts(late_z)[0] * gain_mix).astype(bf16))
-    feat_tab = lax.optimization_barrier(feature_table(feats + seed, width, slots, team))
+    normed_core = mix_norm(late_z, gain_mix, core_reorder)
+    feat_tab = lax.optimization_barrier(feature_table(feats + seed, seed, width, slots, team))
+
+    parts = [partials.pop()]
+    for step, part in enumerate(partials, 1):
+        parts.append(lax.ppermute(part, "hid", shift_pairs(hids, step)))
+    sent = others_rows(normed_core, pre_grad)
+    feat_tab, *_ = lax.optimization_barrier((feat_tab, *sent))
+    mix_low, spectral = mix_rows(where, z_mix, ffn_grad, gain_mix, feat_tab, parts, hids)
+
+    pre_grad, seed, spectral = lax.optimization_barrier((pre_grad, seed, spectral))
     pos_tab = lax.optimization_barrier(position_table(tok_rows, seed))
     t_cos, t_sin = turn(
-        jnp.arange(spans, dtype=jnp.int32)[:, None] * jnp.arange(tok_rows, dtype=jnp.int32)[None], seq_length
+        (jnp.arange(spans, dtype=jnp.int32) + seed)[:, None] * (jnp.arange(tok_rows, dtype=jnp.int32) + seed)[None],
+        seq_length,
     )
     twist = jnp.stack([t_cos, t_sin]) * (1.0 / math.sqrt(seq_length * width))
     team_index = lax.axis_index(TEAM)
-    mark = ((team_index * slots + jnp.arange(slots, dtype=jnp.int32)) == 0).astype(jnp.float32)[:, None]
-    own_ids = hid_index * col_count + jnp.arange(col_count, dtype=jnp.int32)
+    mark = ((team_index * slots + jnp.arange(slots, dtype=jnp.int32)) == seed).astype(jnp.float32)[:, None]
+    own_ids = hid_index * col_count + jnp.arange(col_count, dtype=jnp.int32) + seed
     own_slot = jnp.where(own_ids < half, own_ids, jnp.where(own_ids == half, 0, width - own_ids))
     pick = (jnp.arange(team * slots, dtype=jnp.int32)[:, None] == own_slot[None]).astype(bf16)
 
-    summed = partials.pop().astype(jnp.float32)
-    for step, sent in enumerate(partials, 1):
-        summed += lax.ppermute(sent, "hid", shift_pairs(hids, step)).astype(jnp.float32)
-    mix_grad = norm_backward(
-        row_part(z_mix, hid_index), gain_mix, row_part(ffn_grad, hid_index) + summed
-    )
-    mix_low = mix_grad.astype(bf16)
-
-    spectral = lax.dot_general(
-        feat_tab, mix_low, contract_units, preferred_element_type=jnp.float32
-    ).astype(bf16)
-    pre_grad, *_ = lax.optimization_barrier((pre_grad, spectral))
-    grad_w_in = weight_grad(normed_core, pre_grad, ())
+    grad_w_in = over_chips(chip_sum(normed_core, pre_grad, sent))
     got = lax.all_to_all(
         spectral.reshape(team, 2 * slots, rows), TEAM, split_axis=0, concat_axis=0, tiled=True
     )
     def col_part(values, index):
         return lax.dynamic_slice_in_dim(values, index * col_count, col_count, 1)
 
-    own = jnp.zeros((tok_rows, col_count), jnp.float32)
-    own = lax.dynamic_update_slice_in_dim(own, col_part(mix_grad, hid_index), hid_index * rows, 0)
+    own = jnp.zeros((tok_rows, col_count), bf16)
+    own = lax.dynamic_update_slice_in_dim(own, col_part(mix_low, hid_index), hid_index * rows, 0)
     for step in range(1, hids):
         sent = col_part(mix_low, (hid_index + step) % hids)
-        came = lax.ppermute(sent, "hid", shift_pairs(hids, step)).astype(jnp.float32)
+        came = lax.ppermute(sent, "hid", shift_pairs(hids, step))
         own = lax.dynamic_update_slice_in_dim(own, came, (hid_index - step) % hids * rows, 0)
-    got, own = lax.optimization_barrier((got, own))
+    got, own, grad_w_out = lax.optimization_barrier((got, own, grad_w_out))
     sent_back = position_transform(got, mark, twist, pos_tab, spans, hids, slots)
     back = lax.all_to_all(sent_back, TEAM, split_axis=0, concat_axis=0, tiled=True)
     back, grad_w_in, grad_w_out = lax.optimization_barrier((back, grad_w_in, grad_w_out))

time: 167 us -> 162 us (0.970)
  Pallas kernels: 20.9 us -> 35.3 us
  other arithmetic: 34 us -> 23.6 us
  matrix products: 17 us -> 9.84 us
    pallas_call x0 -> x3, Pallas kernels: none -> 11.4 us  [the longest x1 4.67 us: mix_rows(): pl.pallas_call(functools.partial(mix_kernel, len(parts), hids), grid_spec...]
    reduce_scatter x2, waiting for transfers between devices: 10.1 us -> 0.04 us  [the longest x1 0.02 us: over_chips(): lax.psum_scatter(total, 'seq', scatter_dimension=0, tiled=True)]
    reduce_sum x8 -> x0, other arithmetic: 9.8 us -> none  [the longest x2 5.21 us: norm_backward(): jnp.mean(scaled, axis=-1, keepdims=True)]
    all_to_all x1, waiting for transfers between devices: 9.67 us -> 17.7 us  [local(): lax.all_to_all(sent_back, TEAM, split_axis=0, concat_axis=0, tiled=True)]
    ppermute x3, waiting for transfers between devices: 0.01 us -> 6.1 us  [weight_pieces(): lax.ppermute(blocks[0], 'groups', shift_pairs(2, 1))]
    add_any x1 -> x0, other arithmetic: 6.02 us -> none  [gelu_tanh(): return jax.nn.gelu(values, approximate=True)]
    dot_general x4 -> x2, matrix products: 11 us -> 5.87 us  [core_rows(): lax.dot_general(part, right, contract_rows, preferred_element_type=jnp.fl...]
    all_to_all x1, starting transfers between devices: 5.48 us -> 10.5 us  [local(): lax.all_to_all(sent_back, TEAM, split_axis=0, concat_axis=0, tiled=True)]
  transfers between devices with their start and end apart: 22 -> 21, of which waited for: 7 -> 5; matrix products, arithmetic and copies ran while one was open for 31% -> 20% of each run, Pallas kernels for 11% -> 21%
where the time goes in v3:
time: 162 us
  waiting for transfers between devices  45.3 us (28%)
  Pallas kernels  35.3 us (22%)
  starting transfers between devices  28.4 us (18%)
  other arithmetic  23.6 us (15%)
  between operations  14.4 us (9%)
  matrix products  9.84 us (6%)
  local copies, waits for them, and re-layouts  4.79 us (3%)
    all_to_all x1, waiting for transfers between devices, local(): lax.all_to_all(sent_back, TEAM, split_axis=0, concat_axis=0, tiled=True)  17.7 us
    pallas_call x2, Pallas kernels, feed_rows(): pl.pallas_call(functools.partial(feed_kernel, keys, len(flat), shard, chi...  15.3 us
    ppermute x3, waiting for transfers between devices, weight_pieces(): lax.ppermute(w, 'seq', shift_pairs(chips, d))  14 us
    all_to_all x1, starting transfers between devices, local(): lax.all_to_all(sent_back, TEAM, split_axis=0, concat_axis=0, tiled=True)  10.5 us
    all_to_all x1, waiting for transfers between devices, local(): lax.all_to_all(spectral.reshape(team, 2 * slots, rows), TEAM, split_axis=...  6.91 us
    pallas_call x1, Pallas kernels, position_transform(): pl.pallas_call(functools.partial(position_kernel, spans, hids, slots), gr...  6.52 us
    ppermute x3, waiting for transfers between devices, weight_pieces(): lax.ppermute(blocks[0], 'groups', shift_pairs(2, 1))  6.1 us
    dot_general x2, matrix products, core_rows(): lax.dot_general(part, right, contract_rows, preferred_element_type=jnp.fl...  5.87 us
  transfers between devices with their start and end apart: 21, of which 5 were waited for; matrix products, arithmetic and copies ran while one was open for 20% of the time, Pallas kernels for 21%

profile of v3, /device:TPU:1, one launch (start us, length us, event | category | flops | bytes accessed | tf_op | source)
XLA Modules:
  0.0 161.6 jit_solution(1536873333490327761)
XLA Ops:
  7.2 1.7 %broadcast_select_fusion = bf16[96,1536]{1,0:T(8,128)(2,1)} fusion(bf16[96,1536]{1,0:T(8,128)(2,1)} %refs_0_.3, bf16[96,1536]{1,0:T(8,128)(2,1)} %refs_1_.3, pred[]{:T(512)S(6)} %eq.76), kind=kLoop, calls=%fused_computation.29 | loop fusion | flops 147456 | bytes 884737 | tf_op jit(solution)/shard_map/jit(_where)/select_n | solution.py:342
  8.9 2.1 %collective-permute-start = (bf16[96,1536]{1,0:T(8,128)(2,1)}, bf16[96,1536]{1,0:T(8,128)(2,1)S(1)}, u32[]{:S(2)}, u32[]{:S(2)}) collective-permute-start(bf16[96,1536]{1,0:T(8,128)(2,1)} %broadcast_select_fusion), channel_id=1, source_target_pairs={{0,4},{4,8},{8,12},{12,0},{1,5},{5,9},{9,13},{13,1},{2,6},{6,10},{... | collective-permute-start | bytes 884744 | tf_op jit(solution)/shard_map/ppermute | solution.py:352
  11.1 2.0 %collective-permute-start.2 = (bf16[96,1536]{1,0:T(8,128)(2,1)}, bf16[96,1536]{1,0:T(8,128)(2,1)S(1)}, u32[]{:S(2)}, u32[]{:S(2)}) collective-permute-start(bf16[96,1536]{1,0:T(8,128)(2,1)} %broadcast_select_fusion), channel_id=1, source_target_pairs={{0,12},{4,0},{8,4},{12,8},{1,13},{5,1},{9,5},{13,9},{2,14},{6,2},{... | collective-permute-start | bytes 884744 | tf_op jit(solution)/shard_map/ppermute | solution.py:352
  13.1 1.0 collective-permute-start.6
  14.0 0.7 broadcast_in_dim.41.gain_ref
  14.7 3.7 %fusion.5 = bf16[1024,1536]{1,0:T(8,128)(2,1)S(1)} fusion(bf16[1024,1536]{1,0:T(8,128)(2,1)} %pre_act_ref.3), kind=kLoop, calls=%fused_computation.9 | loop fusion | flops 15728640 | bytes 6291456 | tf_op jit(solution)/shard_map/convert_element_type | solution.py:507
  18.5 2.7 %ffn_norm.1 = (f32[1024,768]{1,0:T(8,128)S(1)}, bf16[1024,768]{1,0:T(8,128)(2,1)S(1)}) custom-call(bf16[1024,768]{1,0:T(8,128)(2,1)S(1)} %copy-done.6, bf16[1024,768]{1,0:T(8,128)(2,1)S(1)} %copy-done.7, f32[1,768]{1,0:T(1,128)S(1)} %broadcast_in_dim.41.gain_ref), custom_call_target="tpu_custom_call" | custom-call | flops 1048576 | bytes 65536 | tf_op jit(solution)/shard_map/ffn_norm/pallas_call | solution.py:252
  21.2 1.7 %copy-done.2 = f32[1024,768]{1,0:T(8,128)} copy-done((f32[1024,768]{1,0:T(8,128)}, f32[1024,768]{1,0:T(8,128)S(1)}, u32[]{:S(2)}) %copy-start.2) | copy-done | bytes 3145752
  22.9 4.0 %convolution_convert_fusion = bf16[768,1536]{1,0:T(8,128)(2,1)} fusion(bf16[1024,768]{1,0:T(8,128)(2,1)S(1)} %get-tuple-element.25.x_ref, bf16[1024,1536]{1,0:T(8,128)(2,1)S(1)} %fusion.5), kind=kOutput, calls=%fused_computation.13 | convolution fusion | flops 2417098752 | bytes 7077888 | tf_op jit(solution)/shard_map/dot_general | solution.py:508
  26.9 0.8 collective-permute-start.4
  27.8 1.2 collective-permute-start.3
  29.2 14.0 %collective-permute-done.4.refs_6_ = bf16[96,1536]{1,0:T(8,128)(2,1)S(1)} collective-permute-done((bf16[96,1536]{1,0:T(8,128)(2,1)}, bf16[96,1536]{1,0:T(8,128)(2,1)S(1)}, u32[]{:S(2)}, u32[]{:S(2)}) %collective-permute-start.4) | collective-permute-done | bytes 294944 | tf_op jit(solution)/shard_map/ppermute | solution.py:352
  43.2 0.6 collective-permute-start.10
  43.9 1.4 collective-permute-start.5
  45.4 0.3 collective-permute-start.8
  45.9 0.3 collective-permute-start.11
  46.5 6.1 %collective-permute-done.5.refs_7_ = bf16[96,1536]{1,0:T(8,128)(2,1)S(1)} collective-permute-done((bf16[96,1536]{1,0:T(8,128)(2,1)S(1)}, bf16[96,1536]{1,0:T(8,128)(2,1)S(1)}, u32[]{:S(2)}, u32[]{:S(2)}) %collective-permute-start.5) | collective-permute-done | bytes 294944 | tf_op jit(solution)/shard_map/ppermute | solution.py:356
  52.6 0.8 collective-permute-start.13
  53.6 0.4 fusion.7.order_ref
  54.1 0.6 collective-permute-done.13.refs_15_
  54.7 7.7 %feed_rows.2 = (bf16[1024,1536]{1,0:T(8,128)(2,1)}, bf16[512,768]{1,0:T(8,128)(2,1)S(1)}) custom-call(s32[4]{0:T(128)S(1)} %pad_add_fusion.where_ref, bf16[1024,768]{1,0:T(8,128)(2,1)} %copy-done, bf16[1024,1536]{1,0:T(8,128)(2,1)} %pre_act_ref.3, bf16[96,1536]{1,0:T(8,128)(2,1)S(1)} %copy-done.4, bf16[96,1536]{1,0:T(8,128)(2,1)S(1)} %copy-done.5, ...), custom_call_target="tpu_custom_call" | custom-call | flops 1048576 | bytes 65536 | tf_op jit(solution)/shard_map/feed_rows/pallas_call | solution.py:415
  62.4 1.3 collective-permute-start.14
  63.7 0.3 fusion.34
  64.0 0.4 fusion.23
  64.4 0.4 multiply_subtract_fusion
  64.9 0.3 fusion.6.tab_ref
  65.2 1.0 copy-done.1
  66.2 4.0 %mix_norm.1 = bf16[1024,768]{1,0:T(8,128)(2,1)S(1)} custom-call(bf16[1024,768]{1,0:T(8,128)(2,1)S(1)} %copy-done.1, f32[1,768]{1,0:T(1,128)S(1)} %broadcast_in_dim.42.gain_ref, bf16[768,768]{1,0:T(8,128)(2,1)S(1)} %fusion.7.order_ref), custom_call_target="tpu_custom_call" | custom-call | flops 1048576 | bytes 65536 | tf_op jit(solution)/shard_map/mix_norm/pallas_call | solution.py:275
  70.2 7.7 %feed_rows.3 = (bf16[1024,1536]{1,0:T(8,128)(2,1)}, bf16[512,768]{1,0:T(8,128)(2,1)S(1)}) custom-call(s32[4]{0:T(128)S(1)} %pad_add_fusion.where_ref, bf16[1024,768]{1,0:T(8,128)(2,1)} %copy-done, bf16[1024,1536]{1,0:T(8,128)(2,1)} %pre_act_ref.3, bf16[96,1536]{1,0:T(8,128)(2,1)S(1)} %copy-done.4, ...), custom_call_target="tpu_custom_call", output_to_operand_aliasing={{0}: (19, {})} | custom-call | flops 1048576 | bytes 65536 | tf_op jit(solution)/shard_map/feed_rows/pallas_call | solution.py:415
  77.9 4.5 %convolution_convert_fusion.1 = bf16[384,1536]{1,0:T(8,128)(2,1)} fusion(bf16[1024,1536]{1,0:T(8,128)(2,1)} %get-tuple-element.41, bf16[1024,768]{1,0:T(8,128)(2,1)S(1)} %mix_norm.1), kind=kOutput, calls=%fused_computation.14 | convolution fusion | flops 1208549376 | bytes 5111808 | tf_op jit(solution)/shard_map/dot_general | solution.py:493
  82.4 0.7 collective-permute-start.16
  83.1 4.7 %mix_rows.1 = (bf16[512,768]{1,0:T(8,128)(2,1)S(1)}, bf16[768,512]{1,0:T(8,128)(2,1)}) custom-call(s32[4]{0:T(128)S(1)} %pad_add_fusion.where_ref, bf16[1024,768]{1,0:T(8,128)(2,1)S(1)} %copy-done.1, f32[1024,768]{1,0:T(8,128)S(1)} %copy-done.3, f32[1,768]{1,0:T(1,128)S(1)} %broadcast_in_dim.42.gain_ref, bf16[768,768]{1,0:T(8,128)(2,1)S(1)} %fusion.6.tab_ref, ...), custom_call_target="tpu_custom_call" | custom-call | flops 1048576 | bytes 65536 | tf_op jit(solution)/shard_map/mix_rows/pallas_call | solution.py:314
  88.2 4.4 %all-to-all-start = ((bf16[16,48,512]{2,1,0:T(8,128)(2,1)}), bf16[16,48,512]{2,1,0:T(8,128)(2,1)S(1)}, u32[]{:S(2)}, u32[]{:S(2)}) async-start(bf16[16,48,512]{2,1,0:T(8,128)(2,1)} %bitcast.5), calls=%async_computation | async-start | bytes 1572864 | tf_op jit(solution)/shard_map/all_to_all | solution.py:553
  92.6 1.1 fusion.27
  93.8 3.7 %subtract_convert_fusion.1 = (bf16[1,32,32,1024]{3,2,1,0:T(8,128)(2,1)}, bf16[1,32,32,1024]{3,2,1,0:T(8,128)(2,1)}) fusion(f32[32,1024]{1,0:T(8,128)S(1)} %get-tuple-element.64, f32[32,1024]{1,0:T(8,128)S(1)} %get-tuple-element.53, f32[32,1024]{1,0:T(8,128)S(1)} %get-tuple-element.65, f32[32,1024]{1,0:T(8,128)S(1)} %get-tuple-element.55, ...), kind=kLoop, calls=%fused_computation.12 | loop fusion | flops 8388608 | bytes 4849664 | tf_op jit(solution)/shard_map/convert
  97.4 1.4 fusion.8
  98.9 1.4 add_convert_fusion
  100.3 4.6 %pad_maximum_fusion = bf16[2,32,32,1024]{3,2,1,0:T(8,128)(2,1)} fusion(bf16[1,32,32,1024]{3,2,1,0:T(8,128)(2,1)} %get-tuple-element.50, bf16[1,32,32,1024]{3,2,1,0:T(8,128)(2,1)} %get-tuple-element.49), kind=kLoop, calls=%fused_computation.10 | loop fusion | flops 2097152 | bytes 8388608 | tf_op jit(solution)/shard_map/stack | solution.py:72
  104.9 0.6 fusion.42.mark_ref
  105.7 0.6 maximum_multiply_fusion.twist_ref
  106.4 1.8 %convert_element_type.123 = f32[96,1536]{1,0:T(8,128)} convert(bf16[96,1536]{1,0:T(8,128)(2,1)} %reduce-scatter.3.cloned.1.call-done) | non-fusion elementwise | flops 147456 | bytes 884736 | tf_op jit(solution)/shard_map/convert_element_type | solution.py:510
  108.3 6.9 %all-to-all-done.x_ref = bf16[16,48,512]{2,1,0:T(8,128)(2,1)S(1)} async-done(((bf16[16,48,512]{2,1,0:T(8,128)(2,1)}), bf16[16,48,512]{2,1,0:T(8,128)(2,1)S(1)}, u32[]{:S(2)}, u32[]{:S(2)}) %all-to-all-start) | async-done | bytes 786464 | tf_op jit(solution)/shard_map/all_to_all | solution.py:553
  115.2 0.9 copy-done.11
  116.1 6.5 %position_transform.1 = bf16[8,2,192,128]{3,2,1,0:T(8,128)(2,1)} custom-call(bf16[16,48,512]{2,1,0:T(8,128)(2,1)} %copy-done.11, f32[24,1]{1,0:T(8,128)} %fusion.42.mark_ref, f32[2,8,1024]{2,1,0:T(8,128)} %maximum_multiply_fusion.twist_ref, bf16[2048,1024]{1,0:T(8,128)(2,1)} %bitcast.15), custom_call_target="tpu_custom_call" | custom-call | flops 1610612736 | bytes 6291456 | tf_op jit(solution)/shard_map/position_transform/pallas_call | solution.py:163
  122.6 10.5 %all-to-all-start.1 = ((bf16[16,192,128]{2,1,0:T(8,128)(2,1)}), bf16[16,192,128]{2,1,0:T(8,128)(2,1)S(1)}, u32[]{:S(2)}, u32[]{:S(2)}) async-start(bf16[16,192,128]{2,1,0:T(8,128)(2,1)} %bitcast.16), calls=%async_computation.2 | async-start | bytes 1572864 | tf_op jit(solution)/shard_map/all_to_all | solution.py:567
  133.2 1.8 %convert_element_type.131 = f32[96,1536]{1,0:T(8,128)} convert(bf16[96,1536]{1,0:T(8,128)(2,1)} %reduce-scatter.5.cloned.1.call-done) | non-fusion elementwise | flops 147456 | bytes 884736 | tf_op jit(solution)/shard_map/convert_element_type | solution.py:505
  135.0 17.7 %all-to-all-done.1.back_ref = bf16[16,192,128]{2,1,0:T(8,128)(2,1)S(1)} async-done(((bf16[16,192,128]{2,1,0:T(8,128)(2,1)}), bf16[16,192,128]{2,1,0:T(8,128)(2,1)S(1)}, u32[]{:S(2)}, u32[]{:S(2)}) %all-to-all-start.1) | async-done | bytes 786464 | tf_op jit(solution)/shard_map/all_to_all | solution.py:567
  152.7 2.1 %finish.1 = f32[1024,384]{1,0:T(8,128)} custom-call(bf16[16,192,128]{2,1,0:T(8,128)(2,1)S(1)} %all-to-all-done.1.back_ref, bf16[384,384]{1,0:T(8,128)(2,1)S(1)} %fusion.11.pick_ref, bf16[1024,384]{1,0:T(8,128)(2,1)S(1)} %constant_dynamic-update-slice_fusion.own_ref), custom_call_target="tpu_custom_call" | custom-call | flops 301989888 | bytes 5242880 | tf_op jit(solution)/shard_map/finish/pallas_call | solution.py:223
  (73 shorter events, 2.3 us)
Async XLA Ops:
  7.2 99.3 %reduce-scatter.3.cloned.1.call-start = ((), (), s32[]{:S(2)}) async-start(), calls=%async_computation.4 | async-start | bytes 2654208 | tf_op jit(solution)/shard_map/reduce_scatter | solution.py:510
  8.9 17.9 %collective-permute-start = (bf16[96,1536]{1,0:T(8,128)(2,1)}, bf16[96,1536]{1,0:T(8,128)(2,1)S(1)}, u32[]{:S(2)}, u32[]{:S(2)}) collective-permute-start(bf16[96,1536]{1,0:T(8,128)(2,1)} %broadcast_select_fusion), channel_id=1, source_target_pairs={{0,4},{4,8},{8,12},{12,0},{1,5},{5,9},{9,13},{13,1},{2,6},{6,10},{... | collective-permute-start | bytes 884744 | tf_op jit(solution)/shard_map/ppermute | solution.py:352
  11.1 15.8 %collective-permute-start.2 = (bf16[96,1536]{1,0:T(8,128)(2,1)}, bf16[96,1536]{1,0:T(8,128)(2,1)S(1)}, u32[]{:S(2)}, u32[]{:S(2)}) collective-permute-start(bf16[96,1536]{1,0:T(8,128)(2,1)} %broadcast_select_fusion), channel_id=1, source_target_pairs={{0,12},{4,0},{8,4},{12,8},{1,13},{5,1},{9,5},{13,9},{2,14},{6,2},{... | collective-permute-start | bytes 884744 | tf_op jit(solution)/shard_map/ppermute | solution.py:352
  13.1 30.8 %collective-permute-start.6 = (bf16[96,1536]{1,0:T(8,128)(2,1)}, bf16[96,1536]{1,0:T(8,128)(2,1)S(1)}, u32[]{:S(2)}, u32[]{:S(2)}) collective-permute-start(bf16[96,1536]{1,0:T(8,128)(2,1)} %refs_0_.3), channel_id=1, source_target_pairs={{0,1},{1,0},{2,3},{3,2},{4,5},{5,4},{6,7},{7,6},{8,9},{9,8},{10,11... | collective-permute-start | bytes 884744 | tf_op jit(solution)/shard_map/ppermute | solution.py:362
  14.0 31.4 %collective-permute-start.7 = (bf16[96,1536]{1,0:T(8,128)(2,1)}, bf16[96,1536]{1,0:T(8,128)(2,1)S(1)}, u32[]{:S(2)}, u32[]{:S(2)}) collective-permute-start(bf16[96,1536]{1,0:T(8,128)(2,1)} %refs_1_.3), channel_id=1, source_target_pairs={{0,1},{1,0},{2,3},{3,2},{4,5},{5,4},{6,7},{7,6},{8,9},{9,8},{10,11... | collective-permute-start | bytes 884744 | tf_op jit(solution)/shard_map/ppermute | solution.py:362
  14.7 3.7 %copy-start.6 = (bf16[1024,768]{1,0:T(8,128)(2,1)S(1)}, bf16[1024,768]{1,0:T(8,128)(2,1)}, u32[]{:S(2)}) copy-start(bf16[1024,768]{1,0:T(8,128)(2,1)} %z_ref.2) | copy-start | bytes 4718596
  14.7 3.8 %copy-start.7 = (bf16[1024,768]{1,0:T(8,128)(2,1)S(1)}, bf16[1024,768]{1,0:T(8,128)(2,1)}, u32[]{:S(2)}) copy-start(bf16[1024,768]{1,0:T(8,128)(2,1)} %up_ref.1) | copy-start | bytes 4718596
  21.2 1.7 %copy-start.2 = (f32[1024,768]{1,0:T(8,128)}, f32[1024,768]{1,0:T(8,128)S(1)}, u32[]{:S(2)}) copy-start(f32[1024,768]{1,0:T(8,128)S(1)} %get-tuple-element.31.ffn_ref) | copy-start | bytes 9437188
  22.9 4.0 %copy-start = (bf16[1024,768]{1,0:T(8,128)(2,1)}, bf16[1024,768]{1,0:T(8,128)(2,1)S(1)}, u32[]{:S(2)}) copy-start(bf16[1024,768]{1,0:T(8,128)(2,1)S(1)} %get-tuple-element.25.x_ref) | copy-start | bytes 4718596
  26.8 26.7 %copy-start.12 = (f32[768]{0:T(1024)S(1)}, f32[768]{0:T(1024)}, u32[]{:S(2)}) copy-start(f32[768]{0:T(1024)} %param.12) | copy-start | bytes 9220
  26.8 27.8 %copy-start.4 = (bf16[96,1536]{1,0:T(8,128)(2,1)S(1)}, bf16[96,1536]{1,0:T(8,128)(2,1)}, u32[]{:S(2)}) copy-start(bf16[96,1536]{1,0:T(8,128)(2,1)} %refs_0_.3) | copy-start | bytes 884740
  26.8 27.8 %copy-start.5 = (bf16[96,1536]{1,0:T(8,128)(2,1)S(1)}, bf16[96,1536]{1,0:T(8,128)(2,1)}, u32[]{:S(2)}) copy-start(bf16[96,1536]{1,0:T(8,128)(2,1)} %refs_1_.3) | copy-start | bytes 884740
  26.9 16.3 %collective-permute-start.4 = (bf16[96,1536]{1,0:T(8,128)(2,1)}, bf16[96,1536]{1,0:T(8,128)(2,1)S(1)}, u32[]{:S(2)}, u32[]{:S(2)}) collective-permute-start(bf16[96,1536]{1,0:T(8,128)(2,1)} %broadcast_select_fusion), channel_id=1, source_target_pairs={{0,8},{4,12},{8,0},{12,4},{1,9},{5,13},{9,1},{13,5},{2,10},{6,14},... | collective-permute-start | bytes 884744 | tf_op jit(solution)/shard_map/ppermute | solution.py:352
  27.8 18.0 %collective-permute-start.3 = (bf16[96,1536]{1,0:T(8,128)(2,1)S(1)}, bf16[96,1536]{1,0:T(8,128)(2,1)S(1)}, u32[]{:S(2)}, u32[]{:S(2)}) collective-permute-start(bf16[96,1536]{1,0:T(8,128)(2,1)S(1)} %collective-permute-done.2.refs_4_), channel_id=1, source_target_pairs={{0,16},{16,0},{1,17},{17,1},{2,18},{18,2},{3,19},{19,3},{4,20},{20... | collective-permute-start | bytes 884744 | tf_op jit(solution)/shard_map/ppermute | solution.py:356
  29.0 16.9 %collective-permute-start.1 = (bf16[96,1536]{1,0:T(8,128)(2,1)S(1)}, bf16[96,1536]{1,0:T(8,128)(2,1)S(1)}, u32[]{:S(2)}, u32[]{:S(2)}) collective-permute-start(bf16[96,1536]{1,0:T(8,128)(2,1)S(1)} %collective-permute-done.refs_2_), channel_id=1, source_target_pairs={{0,16},{16,0},{1,17},{17,1},{2,18},{18,2},{3,19},{19,3},{4,20},{20... | collective-permute-start | bytes 884744 | tf_op jit(solution)/shard_map/ppermute | solution.py:356
  43.2 3.1 %collective-permute-start.10 = (bf16[96,1536]{1,0:T(8,128)(2,1)S(1)}, bf16[96,1536]{1,0:T(8,128)(2,1)S(1)}, u32[]{:S(2)}, u32[]{:S(2)}) collective-permute-start(bf16[96,1536]{1,0:T(8,128)(2,1)S(1)} %collective-permute-done.2.refs_4_), channel_id=1, source_target_pairs={{0,1},{1,0},{2,3},{3,2},{4,5},{5,4},{6,7},{7,6},{8,9},{9,8},{10,11... | collective-permute-start | bytes 884744 | tf_op jit(solution)/shard_map/ppermute | solution.py:362
  43.9 8.7 %collective-permute-start.5 = (bf16[96,1536]{1,0:T(8,128)(2,1)S(1)}, bf16[96,1536]{1,0:T(8,128)(2,1)S(1)}, u32[]{:S(2)}, u32[]{:S(2)}) collective-permute-start(bf16[96,1536]{1,0:T(8,128)(2,1)S(1)} %collective-permute-done.4.refs_6_), channel_id=1, source_target_pairs={{0,16},{16,0},{1,17},{17,1},{2,18},{18,2},{3,19},{19,3},{4,20},{20... | collective-permute-start | bytes 884744 | tf_op jit(solution)/shard_map/ppermute | solution.py:356
  45.4 8.6 %collective-permute-start.8 = (bf16[96,1536]{1,0:T(8,128)(2,1)S(1)}, bf16[96,1536]{1,0:T(8,128)(2,1)}, u32[]{:S(2)}, u32[]{:S(2)}) collective-permute-start(bf16[96,1536]{1,0:T(8,128)(2,1)S(1)} %collective-permute-done.refs_2_), channel_id=1, source_target_pairs={{0,1},{1,0},{2,3},{3,2},{4,5},{5,4},{6,7},{7,6},{8,9},{9,8},{10,11... | collective-permute-start | bytes 884744 | tf_op jit(solution)/shard_map/ppermute | solution.py:362
  45.7 8.3 %collective-permute-start.12 = (bf16[96,1536]{1,0:T(8,128)(2,1)S(1)}, bf16[96,1536]{1,0:T(8,128)(2,1)}, u32[]{:S(2)}, u32[]{:S(2)}) collective-permute-start(bf16[96,1536]{1,0:T(8,128)(2,1)S(1)} %collective-permute-done.4.refs_6_), channel_id=1, source_target_pairs={{0,1},{1,0},{2,3},{3,2},{4,5},{5,4},{6,7},{7,6},{8,9},{9,8},{10,11... | collective-permute-start | bytes 884744 | tf_op jit(solution)/shard_map/ppermute | solution.py:362
  45.9 8.1 %collective-permute-start.11 = (bf16[96,1536]{1,0:T(8,128)(2,1)S(1)}, bf16[96,1536]{1,0:T(8,128)(2,1)}, u32[]{:S(2)}, u32[]{:S(2)}) collective-permute-start(bf16[96,1536]{1,0:T(8,128)(2,1)S(1)} %collective-permute-done.3.refs_5_), channel_id=1, source_target_pairs={{0,1},{1,0},{2,3},{3,2},{4,5},{5,4},{6,7},{7,6},{8,9},{9,8},{10,11... | collective-permute-start | bytes 884744 | tf_op jit(solution)/shard_map/ppermute | solution.py:362
  46.3 7.8 %collective-permute-start.9 = (bf16[96,1536]{1,0:T(8,128)(2,1)S(1)}, bf16[96,1536]{1,0:T(8,128)(2,1)}, u32[]{:S(2)}, u32[]{:S(2)}) collective-permute-start(bf16[96,1536]{1,0:T(8,128)(2,1)S(1)} %collective-permute-done.1.refs_3_), channel_id=1, source_target_pairs={{0,1},{1,0},{2,3},{3,2},{4,5},{5,4},{6,7},{7,6},{8,9},{9,8},{10,11... | collective-permute-start | bytes 884744 | tf_op jit(solution)/shard_map/ppermute | solution.py:362
  52.6 2.1 %collective-permute-start.13 = (bf16[96,1536]{1,0:T(8,128)(2,1)S(1)}, bf16[96,1536]{1,0:T(8,128)(2,1)}, u32[]{:S(2)}, u32[]{:S(2)}) collective-permute-start(bf16[96,1536]{1,0:T(8,128)(2,1)S(1)} %collective-permute-done.5.refs_7_), channel_id=1, source_target_pairs={{0,1},{1,0},{2,3},{3,2},{4,5},{5,4},{6,7},{7,6},{8,9},{9,8},{10,11... | collective-permute-start | bytes 884744 | tf_op jit(solution)/shard_map/ppermute | solution.py:362
  62.4 20.7 %collective-permute-start.14 = (bf16[512,768]{1,0:T(8,128)(2,1)S(1)}, bf16[512,768]{1,0:T(8,128)(2,1)S(1)}, u32[]{:S(2)}, u32[]{:S(2)}) collective-permute-start(bf16[512,768]{1,0:T(8,128)(2,1)S(1)} %get-tuple-element.29), channel_id=1, source_target_pairs={{0,2},{2,0},{1,3},{3,1},{4,6},{6,4},{5,7},{7,5},{8,10},{10,8},{9,1... | collective-permute-start | bytes 2359304 | tf_op jit(solution)/shard_map/ppermute | solution.py:534
  64.8 1.4 copy-start.1
  70.2 7.7 %copy-start.8 = (bf16[1024,768]{1,0:T(8,128)(2,1)}, bf16[1024,768]{1,0:T(8,128)(2,1)S(1)}, u32[]{:S(2)}) copy-start(bf16[1024,768]{1,0:T(8,128)(2,1)S(1)} %mix_norm.1) | copy-start | bytes 4718596
  77.9 5.2 %copy-start.3 = (f32[1024,768]{1,0:T(8,128)S(1)}, f32[1024,768]{1,0:T(8,128)}, u32[]{:S(2)}) copy-start(f32[1024,768]{1,0:T(8,128)} %copy-done.2) | copy-start | bytes 9437188
  82.4 16.5 %collective-permute-start.16 = (bf16[384,1536]{1,0:T(8,128)(2,1)}, bf16[384,1536]{1,0:T(8,128)(2,1)S(1)}, u32[]{:S(2)}, u32[]{:S(2)}) collective-permute-start(bf16[384,1536]{1,0:T(8,128)(2,1)} %convolution_convert_fusion.1), channel_id=1, source_target_pairs={{0,1},{1,0},{2,3},{3,2},{4,5},{5,4},{6,7},{7,6},{8,9},{9,8},{10,11... | collective-permute-start | bytes 3538952 | tf_op jit(solution)/shard_map/ppermute | solution.py:501
  88.0 18.4 %collective-permute-start.15 = (bf16[512,384]{1,0:T(8,128)(2,1)S(1)}, bf16[512,384]{1,0:T(8,128)(2,1)S(1)}, u32[]{:S(2)}, u32[]{:S(2)}) collective-permute-start(bf16[512,384]{1,0:T(8,128)(2,1)S(1)} %get-tuple-element.47), channel_id=1, source_target_pairs={{0,2},{2,0},{1,3},{3,1},{4,6},{6,4},{5,7},{7,5},{8,10},{10,8},{9,1... | collective-permute-start | bytes 1179656 | tf_op jit(solution)/shard_map/ppermute | solution.py:563
  88.2 27.0 %all-to-all-start = ((bf16[16,48,512]{2,1,0:T(8,128)(2,1)}), bf16[16,48,512]{2,1,0:T(8,128)(2,1)S(1)}, u32[]{:S(2)}, u32[]{:S(2)}) async-start(bf16[16,48,512]{2,1,0:T(8,128)(2,1)} %bitcast.5), calls=%async_computation | async-start | bytes 1572864 | tf_op jit(solution)/shard_map/all_to_all | solution.py:553
  92.6 40.6 %reduce-scatter.5.cloned.1.call-start = ((), (), s32[]{:S(2)}) async-start(), calls=%async_computation.5 | async-start | bytes 1474560 | tf_op jit(solution)/shard_map/reduce_scatter | solution.py:505
  93.8 3.7 %copy-start.9 = (bf16[1024,768]{1,0:T(8,128)(2,1)S(1)}, bf16[1024,768]{1,0:T(8,128)(2,1)}, u32[]{:S(2)}) copy-start(bf16[1024,768]{1,0:T(8,128)(2,1)} %copy-done.8) | copy-start | bytes 4718596
  93.8 3.7 %copy-start.10 = (bf16[1024,1536]{1,0:T(8,128)(2,1)S(1)}, bf16[1024,1536]{1,0:T(8,128)(2,1)}, u32[]{:S(2)}) copy-start(bf16[1024,1536]{1,0:T(8,128)(2,1)} %get-tuple-element.41) | copy-start | bytes 9437188
  115.2 0.9 copy-start.11
  122.6 30.1 %all-to-all-start.1 = ((bf16[16,192,128]{2,1,0:T(8,128)(2,1)}), bf16[16,192,128]{2,1,0:T(8,128)(2,1)S(1)}, u32[]{:S(2)}, u32[]{:S(2)}) async-start(bf16[16,192,128]{2,1,0:T(8,128)(2,1)} %bitcast.16), calls=%async_computation.2 | async-start | bytes 1572864 | tf_op jit(solution)/shard_map/all_to_all | solution.py:567
Sparse Core Ops, SparseCore 0:
  44.0 33.1 reduce-scatter.2
  100.4 30.5 reduce-scatter.4

commit v4 on v3

--- a/solution.py
+++ b/solution.py
@@ -159,7 +159,7 @@
     team = spans * hids
     rows = spans * slots
     if hids == 2 and share == LANES and slots % 8 == 0 and spans % 2 == 0:
-        dests = 2
+        dests = 4 if spans % 4 == 0 else 2
         out = pl.pallas_call(
             functools.partial(position_kernel, spans, hids, slots),
             grid=(spans // dests,),
@@ -293,6 +293,28 @@
     return upper + (0.5 * scale) * a * (1.0 - tanh * tanh) * (1.0 + (3.0 * 0.044715) * square)
 
 
+def slope_kernel(where_ref, pre_act_ref, slope_ref):
+    slope_ref[...] = gelu_slope(pre_act_ref[...])
+
+
+def slope_rows(where, pre_act, rows, step):
+    hids, units = lax.axis_size("hid"), pre_act.shape[1]
+    steps = rows // ROWS
+    return pl.pallas_call(
+        slope_kernel,
+        grid_spec=pltpu.PrefetchScalarGridSpec(
+            num_scalar_prefetch=1,
+            grid=(steps,),
+            in_specs=[pl.BlockSpec((ROWS, units), lambda i, w: (lax.rem(w[0] + step, hids) * steps + i, 0))],
+            out_specs=pl.BlockSpec((ROWS, units), lambda i, w: (i, 0)),
+        ),
+        out_shape=jax.ShapeDtypeStruct((rows, units), jnp.float32),
+        compiler_params=pltpu.CompilerParams(vmem_limit_bytes=32 << 20),
+        cost_estimate=SMALL,
+        name="slope_rows",
+    )(where, pre_act)
+
+
 def mix_kernel(count, hids, where_ref, z_ref, ffn_ref, gain_ref, tab_ref, *refs):
     parts, (mix_ref, spec_ref) = refs[:count], refs[count:]
     summed = parts[0][...].astype(jnp.float32)
@@ -308,9 +330,10 @@
 
 def mix_rows(where, z_mix, ffn_grad, gain, table, parts, hids):
     rows, width = parts[0].shape
-    steps = rows // ROWS
-    tile = pl.BlockSpec((ROWS, width), lambda i, w: (i, 0))
-    own = pl.BlockSpec((ROWS, width), lambda i, w: (w[0] * steps + i, 0))
+    size = min(rows, 256)
+    steps = rows // size
+    tile = pl.BlockSpec((size, width), lambda i, w: (i, 0))
+    own = pl.BlockSpec((size, width), lambda i, w: (w[0] * steps + i, 0))
     return pl.pallas_call(
         functools.partial(mix_kernel, len(parts), hids),
         grid_spec=pltpu.PrefetchScalarGridSpec(
@@ -323,7 +346,7 @@
                 pl.BlockSpec(table.shape, lambda i, w: (0, 0)),
                 *[tile for _ in parts],
             ],
-            out_specs=[tile, pl.BlockSpec((table.shape[0], ROWS), lambda i, w: (0, i))],
+            out_specs=[tile, pl.BlockSpec((table.shape[0], size), lambda i, w: (0, i))],
         ),
         out_shape=[
             jax.ShapeDtypeStruct((rows, width), jnp.bfloat16),
@@ -335,7 +358,7 @@
     )(where, z_mix, ffn_grad, gain[None], table, *parts)
 
 
-def weight_pieces(w_out, w_in, first):
+def weight_pieces(w_out, w_in, first, during):
     chips, cores, groups = (lax.axis_size(name) for name in ("seq", "sub", "groups"))
     mine = [w_out, w_in]
     if groups == 2:
@@ -347,21 +370,24 @@
     for wave in waves:
         if arrived:
             mine = lax.optimization_barrier((tuple(mine), arrived[-1], first))[0]
-        came = []
-        for d in wave:
-            blocks = tuple(lax.ppermute(w, "seq", shift_pairs(chips, d)) for w in mine)
-            came.extend(blocks)
+        came = [tuple(lax.ppermute(w, "seq", shift_pairs(chips, d)) for w in mine) for d in wave]
+        held = [i for i, ((d, k), _) in enumerate(near) if k == 1]
+        if held:
+            came, ready, during = lax.optimization_barrier((came, [near[i][1] for i in held], during))
+            for i, arrays in zip(held, ready):
+                near[i] = (near[i][0], arrays)
+        arrived.append([x for blocks in came for x in blocks])
+        for d, blocks in zip(wave, came):
             near.append(((d, 0), blocks))
             if groups == 2:
                 near.append(((d, 1), (lax.ppermute(blocks[0], "groups", shift_pairs(2, 1)),)))
-        arrived.append(came)
     pieces = [((0, d, k), arrays) for (d, k), arrays in near]
     for e in range(1, cores):
         for (d, k), arrays in near:
             pieces.append(
                 ((e, d, k), tuple(lax.ppermute(x, "sub", shift_pairs(cores, -e)) for x in arrays))
             )
-    return pieces, arrived
+    return pieces, arrived, during
 
 
 def piece_rows(key, width, shard, seq, sub, group, chips, cores):
@@ -372,7 +398,7 @@
     return [row, row + width]
 
 
-def feed_kernel(keys, count, shard, chips, cores, carried, where_ref, x_ref, pre_act_ref, *refs):
+def feed_kernel(keys, count, shard, chips, cores, carried, ready, where_ref, x_ref, pre_act_ref, *refs):
     blocks, refs = list(refs[:count]), refs[count + carried :]
     pre_ref, part_ref, weights, total = refs
     width = x_ref.shape[1]
@@ -380,7 +406,8 @@
         for at in piece_rows(key, width, shard, where_ref[1], where_ref[2], where_ref[3], chips, cores):
             weights[pl.ds(pl.multiple_of(at, shard), shard), :] = blocks.pop(0)[...]
     act_grad = jnp.dot(x_ref[...], weights[:width, :], preferred_element_type=jnp.float32)
-    pre_grad = (gelu_slope(pre_act_ref[...]) * act_grad).astype(jnp.bfloat16)
+    slope = pre_act_ref[...] if ready else gelu_slope(pre_act_ref[...])
+    pre_grad = (slope * act_grad).astype(jnp.bfloat16)
     pre_ref[...] = pre_grad
     term = lax.dot_general(
         pre_grad, weights[width:, :], (((1,), (1,)), ((), ())), preferred_element_type=jnp.float32
@@ -400,7 +427,7 @@
         part_ref[...] = total[...].astype(part_ref.dtype)
 
 
-def feed_rows(where, low, pre_act, pieces, rows, step, carried):
+def feed_rows(where, low, pre_act, pieces, rows, step, carried, slope=None):
     chips, cores, hids = (lax.axis_size(name) for name in ("seq", "sub", "hid"))
     width, units = low.shape[1], pre_act.shape[1]
     shard = pieces[0][1][0].shape[0]
@@ -413,13 +440,13 @@
 
     extra = [] if carried is None else [carried]
     return pl.pallas_call(
-        functools.partial(feed_kernel, keys, len(flat), shard, chips, cores, len(extra)),
+        functools.partial(feed_kernel, keys, len(flat), shard, chips, cores, len(extra), slope is not None),
         grid_spec=pltpu.PrefetchScalarGridSpec(
             num_scalar_prefetch=1,
             grid=(units // tile,),
             in_specs=[
                 pl.BlockSpec((rows, width), lambda i, w: (lax.rem(w[0] + step, hids), 0)),
-                pl.BlockSpec((rows, tile), row_block),
+                pl.BlockSpec((rows, tile), row_block if slope is None else lambda i, w: (0, i)),
                 *[pl.BlockSpec((x.shape[0], tile), lambda i, w: (0, i)) for x in flat],
                 *[pl.BlockSpec(memory_space=pl.ANY) for _ in extra],
             ],
@@ -437,10 +464,10 @@
             jax.ShapeDtypeStruct((rows, width), jnp.bfloat16),
         ],
         input_output_aliases={3 + len(flat): 0} if extra else {},
-        compiler_params=pltpu.CompilerParams(vmem_limit_bytes=48 << 20),
+        compiler_params=pltpu.CompilerParams(vmem_limit_bytes=60 << 20),
         cost_estimate=SMALL,
         name="feed_rows",
-    )(where, low, pre_act, *flat, *extra)
+    )(where, low, pre_act if slope is None else slope, *flat, *extra)
 
 
 def whole_weights(pieces, width):
@@ -486,7 +513,11 @@
     core_reorder = (feats[:, None] == core_order.reshape(1, width)).astype(bf16)
 
     ffn_grad, ffn_low = ffn_norm(z_ffn, grad_out, gain_ffn)
-    pieces, arrived = weight_pieces(w_out, w_in, (ffn_low,))
+    fast = shard_rows % 16 == 0 and rows % ROWS == 0 and unit_count % 128 == 0
+    slopes = [slope_rows(where, pre_act, rows, step) for step in range(1, hids)] if fast else []
+    pieces, arrived, (normed_core, slopes) = weight_pieces(
+        w_out, w_in, (ffn_low,), (mix_norm(z_mix, gain_mix, core_reorder), slopes)
+    )
 
     def core_rows(left, right, core):
         part = left[:, core * (width // cores) : (core + 1) * (width // cores)]
@@ -509,10 +540,11 @@
     total_out, *_ = lax.optimization_barrier((total_out.astype(bf16), *arrived[-1]))
     grad_w_out = lax.psum_scatter(total_out, SPANS, scatter_dimension=0, tiled=True).astype(jnp.float32)
     partials = []
-    if shard_rows % 16 == 0 and rows % 16 == 0 and unit_count % 128 == 0:
+    if fast:
         pre_grad = None
         for step in [*range(1, hids), 0]:
-            pre_grad, part = feed_rows(where, ffn_low, pre_act, pieces, rows, step, pre_grad)
+            slope = slopes[step - 1] if step else None
+            pre_grad, part = feed_rows(where, ffn_low, pre_act, pieces, rows, step, pre_grad, slope)
             partials.append(part)
     else:
         whole = whole_weights(pieces, width)
@@ -525,8 +557,7 @@
             partials.append(row_part(product, (hid_index + step) % hids))
 
     seed = jnp.zeros((), jnp.int32)
-    late_z, seed, *_ = lax.optimization_barrier((z_mix, seed, *partials[:-1]))
-    normed_core = mix_norm(late_z, gain_mix, core_reorder)
+    seed, *_ = lax.optimization_barrier((seed, *partials[:-1]))
     feat_tab = lax.optimization_barrier(feature_table(feats + seed, seed, width, slots, team))
 
     parts = [partials.pop()]
@@ -537,6 +568,7 @@
     mix_low, spectral = mix_rows(where, z_mix, ffn_grad, gain_mix, feat_tab, parts, hids)
 
     pre_grad, seed, spectral = lax.optimization_barrier((pre_grad, seed, spectral))
+    grad_w_in = over_chips(chip_sum(normed_core, pre_grad, sent))
     pos_tab = lax.optimization_barrier(position_table(tok_rows, seed))
     t_cos, t_sin = turn(
         (jnp.arange(spans, dtype=jnp.int32) + seed)[:, None] * (jnp.arange(tok_rows, dtype=jnp.int32) + seed)[None],
@@ -549,7 +581,6 @@
     own_slot = jnp.where(own_ids < half, own_ids, jnp.where(own_ids == half, 0, width - own_ids))
     pick = (jnp.arange(team * slots, dtype=jnp.int32)[:, None] == own_slot[None]).astype(bf16)
 
-    grad_w_in = over_chips(chip_sum(normed_core, pre_grad, sent))
     got = lax.all_to_all(
         spectral.reshape(team, 2 * slots, rows), TEAM, split_axis=0, concat_axis=0, tiled=True
     )

time: 162 us -> 160 us (0.988)
  waiting for transfers between devices: 45.3 us -> 36 us
  local copies, waits for them, and re-layouts: 4.79 us -> 7.57 us
  matrix products: 9.84 us -> 12 us
  Pallas kernels: 35.3 us -> 37.3 us
    ppermute x3, waiting for transfers between devices: 14 us -> 5.72 us  [weight_pieces(): lax.ppermute(w, 'seq', shift_pairs(chips, d))]
    all_to_all x1, waiting for transfers between devices: 6.91 us -> 2.14 us  [local(): lax.all_to_all(spectral.reshape(team, 2 * slots, rows), TEAM, split_axis=...]
    ppermute x1, waiting for transfers between devices: 0.01 us -> 2.48 us  [local(): parts.append(lax.ppermute(part, 'hid', shift_pairs(hids, step)))]
    pallas_call x0 -> x1, Pallas kernels: none -> 2.39 us  [slope_rows(): pl.pallas_call(slope_kernel, grid_spec=pltpu.PrefetchScalarGridSpec(num_s...]
    dot_general x2, matrix products: 5.87 us -> 8.04 us  [core_rows(): lax.dot_general(part, right, contract_rows, preferred_element_type=jnp.fl...]
    unnamed x26 -> x44, local copies, waits for them, and re-layouts: 3.62 us -> 5.41 us
  transfers between devices with their start and end apart: 21 -> 21, of which waited for: 5 -> 7; matrix products, arithmetic and copies ran while one was open for 20% -> 22% of each run, Pallas kernels for 21% -> 22%
where the time goes in v4:
time: 160 us; the launch traced here: 159 us
  Pallas kernels  37.3 us (23%)
  waiting for transfers between devices  36 us (22%)
  starting transfers between devices  29.6 us (18%)
  other arithmetic  22.2 us (14%)
  between operations  14.4 us (9%)
  matrix products  12 us (8%)
  local copies, waits for them, and re-layouts  7.57 us (5%)
    pallas_call x2, Pallas kernels, feed_rows(): pl.pallas_call(functools.partial(feed_kernel, keys, len(flat), shard, chi...  16.7 us
    all_to_all x1, waiting for transfers between devices, local(): lax.all_to_all(sent_back, TEAM, split_axis=0, concat_axis=0, tiled=True)  16.3 us
    all_to_all x1, starting transfers between devices, local(): lax.all_to_all(sent_back, TEAM, split_axis=0, concat_axis=0, tiled=True)  10.9 us
    dot_general x2, matrix products, core_rows(): lax.dot_general(part, right, contract_rows, preferred_element_type=jnp.fl...  8.04 us
    ppermute x3, waiting for transfers between devices, weight_pieces(): lax.ppermute(blocks[0], 'groups', shift_pairs(2, 1))  6.6 us
    pallas_call x1, Pallas kernels, position_transform(): pl.pallas_call(functools.partial(position_kernel, spans, hids, slots), gr...  5.73 us
    ppermute x3, waiting for transfers between devices, weight_pieces(): lax.ppermute(w, 'seq', shift_pairs(chips, d))  5.72 us
    unnamed x44, local copies, waits for them, and re-layouts  5.41 us
  transfers between devices with their start and end apart: 21, of which 7 were waited for; matrix products, arithmetic and copies ran while one was open for 22% of the time, Pallas kernels for 22%

profile of v4, /device:TPU:1, one launch (start us, length us, event | category | flops | bytes accessed | tf_op | source)
XLA Modules:
  0.0 159.1 jit_solution(10342434869764046644)
XLA Ops:
  7.2 1.7 %broadcast_select_fusion = bf16[96,1536]{1,0:T(8,128)(2,1)} fusion(bf16[96,1536]{1,0:T(8,128)(2,1)} %refs_0_.3, bf16[96,1536]{1,0:T(8,128)(2,1)} %refs_1_.3, pred[]{:T(512)S(6)} %eq.76), kind=kLoop, calls=%fused_computation.29 | loop fusion | flops 147456 | bytes 884737 | tf_op jit(solution)/shard_map/jit(_where)/select_n | solution.py:365
  8.9 2.1 %collective-permute-start = (bf16[96,1536]{1,0:T(8,128)(2,1)}, bf16[96,1536]{1,0:T(8,128)(2,1)S(1)}, u32[]{:S(2)}, u32[]{:S(2)}) collective-permute-start(bf16[96,1536]{1,0:T(8,128)(2,1)} %broadcast_select_fusion), channel_id=1, source_target_pairs={{0,4},{4,8},{8,12},{12,0},{1,5},{5,9},{9,13},{13,1},{2,6},{6,10},{... | collective-permute-start | bytes 884744 | tf_op jit(solution)/shard_map/ppermute | solution.py:373
  11.1 2.0 %collective-permute-start.1 = (bf16[96,1536]{1,0:T(8,128)(2,1)}, bf16[96,1536]{1,0:T(8,128)(2,1)}, u32[]{:S(2)}, u32[]{:S(2)}) collective-permute-start(bf16[96,1536]{1,0:T(8,128)(2,1)} %broadcast_select_fusion), channel_id=1, source_target_pairs={{0,12},{4,0},{8,4},{12,8},{1,13},{5,1},{9,5},{13,9},{2,14},{6,2},{... | collective-permute-start | bytes 884744 | tf_op jit(solution)/shard_map/ppermute | solution.py:373
  13.1 0.7 broadcast_in_dim.41.gain_ref
  13.8 3.7 %fusion.5 = bf16[1024,1536]{1,0:T(8,128)(2,1)S(1)} fusion(bf16[1024,1536]{1,0:T(8,128)(2,1)} %pre_act_ref.3), kind=kLoop, calls=%fused_computation.9 | loop fusion | flops 15728640 | bytes 6291456 | tf_op jit(solution)/shard_map/convert_element_type | solution.py:538
  17.6 2.7 %ffn_norm.1 = (f32[1024,768]{1,0:T(8,128)S(1)}, bf16[1024,768]{1,0:T(8,128)(2,1)S(1)}) custom-call(bf16[1024,768]{1,0:T(8,128)(2,1)S(1)} %copy-done.7, bf16[1024,768]{1,0:T(8,128)(2,1)S(1)} %copy-done.8, f32[1,768]{1,0:T(1,128)S(1)} %broadcast_in_dim.41.gain_ref), custom_call_target="tpu_custom_call" | custom-call | flops 1048576 | bytes 65536 | tf_op jit(solution)/shard_map/ffn_norm/pallas_call | solution.py:252
  20.3 1.7 %copy-done.5 = f32[1024,768]{1,0:T(8,128)} copy-done((f32[1024,768]{1,0:T(8,128)}, f32[1024,768]{1,0:T(8,128)S(1)}, u32[]{:S(2)}) %copy-start.5) | copy-done | bytes 3145752
  21.9 1.1 copy-done.2
  23.1 4.0 %convolution_convert_fusion = bf16[768,1536]{1,0:T(8,128)(2,1)} fusion(bf16[1024,768]{1,0:T(8,128)(2,1)S(1)} %get-tuple-element.29.x_ref, bf16[1024,1536]{1,0:T(8,128)(2,1)S(1)} %fusion.5), kind=kOutput, calls=%fused_computation.13 | convolution fusion | flops 2417098752 | bytes 7077888 | tf_op jit(solution)/shard_map/dot_general | solution.py:539
  27.2 0.5 collective-permute-start.2
  27.8 1.2 collective-permute-start.3
  29.4 2.4 %slope_rows.1.pre_act_ref = f32[512,1536]{1,0:T(8,128)S(1)} custom-call(s32[4]{0:T(128)S(1)} %pad_add_fusion.where_ref, bf16[1024,1536]{1,0:T(8,128)(2,1)S(1)} %copy-done), custom_call_target="tpu_custom_call" | custom-call | flops 1048576 | bytes 65536 | tf_op jit(solution)/shard_map/slope_rows/pallas_call | solution.py:303
  31.8 1.6 %copy-done.1 = f32[512,1536]{1,0:T(8,128)} copy-done((f32[512,1536]{1,0:T(8,128)}, f32[512,1536]{1,0:T(8,128)S(1)}, u32[]{:S(2)}) %copy-start.1) | copy-done | bytes 3145752
  33.5 0.4 fusion.8.order_ref
  33.9 4.0 %mix_norm.1 = bf16[1024,768]{1,0:T(8,128)(2,1)S(1)} custom-call(bf16[1024,768]{1,0:T(8,128)(2,1)S(1)} %copy-done.3, f32[1,768]{1,0:T(1,128)S(1)} %broadcast_in_dim.42.gain_ref, bf16[768,768]{1,0:T(8,128)(2,1)S(1)} %fusion.8.order_ref), custom_call_target="tpu_custom_call" | custom-call | flops 1048576 | bytes 65536 | tf_op jit(solution)/shard_map/mix_norm/pallas_call | solution.py:275
  37.9 5.7 %collective-permute-done.2.refs_6_ = bf16[96,1536]{1,0:T(8,128)(2,1)} collective-permute-done((bf16[96,1536]{1,0:T(8,128)(2,1)}, bf16[96,1536]{1,0:T(8,128)(2,1)}, u32[]{:S(2)}, u32[]{:S(2)}) %collective-permute-start.2) | collective-permute-done | bytes 294944 | tf_op jit(solution)/shard_map/ppermute | solution.py:373
  43.7 0.6 collective-permute-start.6
  44.3 0.4 collective-permute-start.10
  44.8 1.3 collective-permute-start.5
  47.1 6.6 %collective-permute-done.5.refs_7_ = bf16[96,1536]{1,0:T(8,128)(2,1)} collective-permute-done((bf16[96,1536]{1,0:T(8,128)(2,1)}, bf16[96,1536]{1,0:T(8,128)(2,1)}, u32[]{:S(2)}, u32[]{:S(2)}) %collective-permute-start.5) | collective-permute-done | bytes 294944 | tf_op jit(solution)/shard_map/ppermute | solution.py:383
  53.7 0.9 collective-permute-start.13
  54.8 1.3 collective-permute-done.13.refs_15_
  56.1 8.1 %feed_rows.2 = (bf16[1024,1536]{1,0:T(8,128)(2,1)}, bf16[512,768]{1,0:T(8,128)(2,1)}) custom-call(s32[4]{0:T(128)} %copy-done.10, bf16[1024,768]{1,0:T(8,128)(2,1)} %copy-done.2, f32[512,1536]{1,0:T(8,128)} %copy-done.1, bf16[96,1536]{1,0:T(8,128)(2,1)} %refs_0_.3, bf16[96,1536]{1,0:T(8,128)(2,1)} %refs_1_.3, bf16[96,1536]{1,0:T(8,128)(2,1)} %copy-done.15, ...), custom_call_target="tpu_custom_call" | custom-call | flops 1048576 | bytes 65536 | tf_op jit(solution)/shard_map/feed_rows/pallas_call | solution.py:442
  64.2 1.3 collective-permute-start.14
  65.6 8.6 %feed_rows.3 = (bf16[1024,1536]{1,0:T(8,128)(2,1)}, bf16[512,768]{1,0:T(8,128)(2,1)}) custom-call(s32[4]{0:T(128)} %copy-done.10, bf16[1024,768]{1,0:T(8,128)(2,1)} %copy-done.2, bf16[1024,1536]{1,0:T(8,128)(2,1)} %pre_act_ref.3, bf16[96,1536]{1,0:T(8,128)(2,1)} %refs_0_.3, bf16[96,1536]{1,0:T(8,128)(2,1)} %refs_1_.3, ...), custom_call_target="tpu_custom_call", output_to_operand_aliasing={{0}: (19, {})} | custom-call | flops 1048576 | bytes 65536 | tf_op jit(solution)/shard_map/feed_rows/pallas_call | solution.py:442
  74.6 4.3 %convolution_convert_fusion.1 = bf16[384,1536]{1,0:T(8,128)(2,1)} fusion(bf16[1024,1536]{1,0:T(8,128)(2,1)} %get-tuple-element.49, bf16[1024,768]{1,0:T(8,128)(2,1)S(1)} %mix_norm.1), kind=kOutput, calls=%fused_computation.16 | convolution fusion | flops 1208549376 | bytes 5111808 | tf_op jit(solution)/shard_map/dot_general | solution.py:524
  79.2 0.7 collective-permute-start.16
  79.9 0.4 multiply_subtract_fusion
  80.8 2.5 %collective-permute-done.14.refs_1_ = bf16[512,768]{1,0:T(8,128)(2,1)S(1)} collective-permute-done((bf16[512,768]{1,0:T(8,128)(2,1)}, bf16[512,768]{1,0:T(8,128)(2,1)S(1)}, u32[]{:S(2)}, u32[]{:S(2)}) %collective-permute-start.14) | collective-permute-done | bytes 786464 | tf_op jit(solution)/shard_map/ppermute | solution.py:565
  83.3 3.6 %mix_rows.1 = (bf16[512,768]{1,0:T(8,128)(2,1)S(1)}, bf16[768,512]{1,0:T(8,128)(2,1)}) custom-call(s32[4]{0:T(128)S(1)} %copy-done.11, bf16[1024,768]{1,0:T(8,128)(2,1)S(1)} %copy-done.4, f32[1024,768]{1,0:T(8,128)S(1)} %copy-done.6, f32[1,768]{1,0:T(1,128)S(1)} %broadcast_in_dim.42.gain_ref, bf16[768,768]{1,0:T(8,128)(2,1)S(1)} %fusion.7.tab_ref, ...), custom_call_target="tpu_custom_call" | custom-call | flops 1048576 | bytes 65536 | tf_op jit(solution)/shard_map/mix_rows/pallas_call | solution.py:337
  87.1 1.3 collective-permute-start.15
  88.4 4.9 %all-to-all-start = ((bf16[16,48,512]{2,1,0:T(8,128)(2,1)}), bf16[16,48,512]{2,1,0:T(8,128)(2,1)S(1)}, u32[]{:S(2)}, u32[]{:S(2)}) async-start(bf16[16,48,512]{2,1,0:T(8,128)(2,1)} %bitcast.5), calls=%async_computation | async-start | bytes 1572864 | tf_op jit(solution)/shard_map/all_to_all | solution.py:584
  93.4 1.1 fusion.27
  94.5 3.6 %subtract_convert_fusion.1 = (bf16[1,32,32,1024]{3,2,1,0:T(8,128)(2,1)}, bf16[1,32,32,1024]{3,2,1,0:T(8,128)(2,1)}) fusion(f32[32,1024]{1,0:T(8,128)S(1)} %get-tuple-element.72, f32[32,1024]{1,0:T(8,128)S(1)} %get-tuple-element.61, f32[32,1024]{1,0:T(8,128)S(1)} %get-tuple-element.73, f32[32,1024]{1,0:T(8,128)S(1)} %get-tuple-element.63, ...), kind=kLoop, calls=%fused_computation.12 | loop fusion | flops 8388608 | bytes 4849664 | tf_op jit(solution)/shard_map/convert
  98.1 3.7 %fusion.6 = bf16[384,1536]{1,0:T(8,128)(2,1)} fusion(bf16[1024,1536]{1,0:T(8,128)(2,1)S(1)} %copy-done.12, bf16[384,1536]{1,0:T(8,128)(2,1)} %collective-permute-done.16, bf16[1024,768]{1,0:T(8,128)(2,1)S(1)} %mix_norm.1), kind=kOutput, calls=%fused_computation.15 | convolution fusion | flops 1209729024 | bytes 6291456 | tf_op jit(solution)/shard_map/dot_general | solution.py:524
  101.8 4.6 %pad_maximum_fusion = bf16[2,32,32,1024]{3,2,1,0:T(8,128)(2,1)} fusion(bf16[1,32,32,1024]{3,2,1,0:T(8,128)(2,1)} %get-tuple-element.58, bf16[1,32,32,1024]{3,2,1,0:T(8,128)(2,1)} %get-tuple-element.57), kind=kLoop, calls=%fused_computation.10 | loop fusion | flops 2097152 | bytes 8388608 | tf_op jit(solution)/shard_map/stack | solution.py:72
  106.5 0.6 fusion.42.mark_ref
  107.3 0.6 maximum_multiply_fusion.twist_ref
  108.0 1.1 constant_dynamic-update-slice_fusion.own_ref
  109.0 1.8 %convert_element_type.123 = f32[96,1536]{1,0:T(8,128)} convert(bf16[96,1536]{1,0:T(8,128)(2,1)} %reduce-scatter.3.cloned.1.call-done) | non-fusion elementwise | flops 147456 | bytes 884736 | tf_op jit(solution)/shard_map/convert_element_type | solution.py:541
  110.9 2.1 %all-to-all-done.x_ref = bf16[16,48,512]{2,1,0:T(8,128)(2,1)S(1)} async-done(((bf16[16,48,512]{2,1,0:T(8,128)(2,1)}), bf16[16,48,512]{2,1,0:T(8,128)(2,1)S(1)}, u32[]{:S(2)}, u32[]{:S(2)}) %all-to-all-start) | async-done | bytes 786464 | tf_op jit(solution)/shard_map/all_to_all | solution.py:584
  113.0 0.9 copy-done.20
  113.9 5.7 %position_transform.1 = bf16[8,2,192,128]{3,2,1,0:T(8,128)(2,1)} custom-call(bf16[16,48,512]{2,1,0:T(8,128)(2,1)} %copy-done.20, f32[24,1]{1,0:T(8,128)} %fusion.42.mark_ref, f32[2,8,1024]{2,1,0:T(8,128)} %maximum_multiply_fusion.twist_ref, bf16[2048,1024]{1,0:T(8,128)(2,1)} %bitcast.15), custom_call_target="tpu_custom_call" | custom-call | flops 1610612736 | bytes 6291456 | tf_op jit(solution)/shard_map/position_transform/pallas_call | solution.py:163
  119.6 10.9 %all-to-all-start.1 = ((bf16[16,192,128]{2,1,0:T(8,128)(2,1)}), bf16[16,192,128]{2,1,0:T(8,128)(2,1)S(1)}, u32[]{:S(2)}, u32[]{:S(2)}) async-start(bf16[16,192,128]{2,1,0:T(8,128)(2,1)} %bitcast.16), calls=%async_computation.2 | async-start | bytes 1572864 | tf_op jit(solution)/shard_map/all_to_all | solution.py:598
  130.6 1.4 reduce-scatter.5.cloned.1.call-done
  132.1 1.8 %convert_element_type.131 = f32[96,1536]{1,0:T(8,128)} convert(bf16[96,1536]{1,0:T(8,128)(2,1)} %reduce-scatter.5.cloned.1.call-done) | non-fusion elementwise | flops 147456 | bytes 884736 | tf_op jit(solution)/shard_map/convert_element_type | solution.py:536
  133.9 16.3 %all-to-all-done.1.back_ref = bf16[16,192,128]{2,1,0:T(8,128)(2,1)S(1)} async-done(((bf16[16,192,128]{2,1,0:T(8,128)(2,1)}), bf16[16,192,128]{2,1,0:T(8,128)(2,1)S(1)}, u32[]{:S(2)}, u32[]{:S(2)}) %all-to-all-start.1) | async-done | bytes 786464 | tf_op jit(solution)/shard_map/all_to_all | solution.py:598
  150.2 2.1 %finish.1 = f32[1024,384]{1,0:T(8,128)} custom-call(bf16[16,192,128]{2,1,0:T(8,128)(2,1)S(1)} %all-to-all-done.1.back_ref, bf16[384,384]{1,0:T(8,128)(2,1)S(1)} %fusion.11.pick_ref, bf16[1024,384]{1,0:T(8,128)(2,1)S(1)} %constant_dynamic-update-slice_fusion.own_ref), custom_call_target="tpu_custom_call" | custom-call | flops 301989888 | bytes 5242880 | tf_op jit(solution)/shard_map/finish/pallas_call | solution.py:223
  (91 shorter events, 3.7 us)
Async XLA Ops:
  7.2 101.9 %reduce-scatter.3.cloned.1.call-start = ((), (), s32[]{:S(2)}) async-start(), calls=%async_computation.4 | async-start | bytes 2654208 | tf_op jit(solution)/shard_map/reduce_scatter | solution.py:541
  8.9 18.3 %collective-permute-start = (bf16[96,1536]{1,0:T(8,128)(2,1)}, bf16[96,1536]{1,0:T(8,128)(2,1)S(1)}, u32[]{:S(2)}, u32[]{:S(2)}) collective-permute-start(bf16[96,1536]{1,0:T(8,128)(2,1)} %broadcast_select_fusion), channel_id=1, source_target_pairs={{0,4},{4,8},{8,12},{12,0},{1,5},{5,9},{9,13},{13,1},{2,6},{6,10},{... | collective-permute-start | bytes 884744 | tf_op jit(solution)/shard_map/ppermute | solution.py:373
  11.1 16.2 %collective-permute-start.1 = (bf16[96,1536]{1,0:T(8,128)(2,1)}, bf16[96,1536]{1,0:T(8,128)(2,1)}, u32[]{:S(2)}, u32[]{:S(2)}) collective-permute-start(bf16[96,1536]{1,0:T(8,128)(2,1)} %broadcast_select_fusion), channel_id=1, source_target_pairs={{0,12},{4,0},{8,4},{12,8},{1,13},{5,1},{9,5},{13,9},{2,14},{6,2},{... | collective-permute-start | bytes 884744 | tf_op jit(solution)/shard_map/ppermute | solution.py:373
  13.8 3.8 %copy-start.7 = (bf16[1024,768]{1,0:T(8,128)(2,1)S(1)}, bf16[1024,768]{1,0:T(8,128)(2,1)}, u32[]{:S(2)}) copy-start(bf16[1024,768]{1,0:T(8,128)(2,1)} %z_ref.3) | copy-start | bytes 4718596
  13.8 3.8 %copy-start.8 = (bf16[1024,768]{1,0:T(8,128)(2,1)S(1)}, bf16[1024,768]{1,0:T(8,128)(2,1)}, u32[]{:S(2)}) copy-start(bf16[1024,768]{1,0:T(8,128)(2,1)} %up_ref.1) | copy-start | bytes 4718596
  20.3 1.7 %copy-start.5 = (f32[1024,768]{1,0:T(8,128)}, f32[1024,768]{1,0:T(8,128)S(1)}, u32[]{:S(2)}) copy-start(f32[1024,768]{1,0:T(8,128)S(1)} %get-tuple-element.39.ffn_ref) | copy-start | bytes 9437188
  21.9 1.1 copy-start.2
  23.1 6.3 %copy-start.21 = (f32[768]{0:T(1024)S(1)}, f32[768]{0:T(1024)}, u32[]{:S(2)}) copy-start(f32[768]{0:T(1024)} %param.12) | copy-start | bytes 9220
  23.1 6.3 %copy-start = (bf16[1024,1536]{1,0:T(8,128)(2,1)S(1)}, bf16[1024,1536]{1,0:T(8,128)(2,1)}, u32[]{:S(2)}) copy-start(bf16[1024,1536]{1,0:T(8,128)(2,1)} %pre_act_ref.3) | copy-start | bytes 9437188
  27.2 18.8 %copy-start.15 = (bf16[96,1536]{1,0:T(8,128)(2,1)}, bf16[96,1536]{1,0:T(8,128)(2,1)S(1)}, u32[]{:S(2)}) copy-start(bf16[96,1536]{1,0:T(8,128)(2,1)S(1)} %collective-permute-done.refs_2_) | copy-start | bytes 884740
  27.2 16.4 %collective-permute-start.2 = (bf16[96,1536]{1,0:T(8,128)(2,1)}, bf16[96,1536]{1,0:T(8,128)(2,1)}, u32[]{:S(2)}, u32[]{:S(2)}) collective-permute-start(bf16[96,1536]{1,0:T(8,128)(2,1)} %broadcast_select_fusion), channel_id=1, source_target_pairs={{0,8},{4,12},{8,0},{12,4},{1,9},{5,13},{9,1},{13,5},{2,10},{6,14},... | collective-permute-start | bytes 884744 | tf_op jit(solution)/shard_map/ppermute | solution.py:373
  27.8 15.9 %collective-permute-start.3 = (bf16[96,1536]{1,0:T(8,128)(2,1)S(1)}, bf16[96,1536]{1,0:T(8,128)(2,1)}, u32[]{:S(2)}, u32[]{:S(2)}) collective-permute-start(bf16[96,1536]{1,0:T(8,128)(2,1)S(1)} %collective-permute-done.refs_2_), channel_id=1, source_target_pairs={{0,16},{16,0},{1,17},{17,1},{2,18},{18,2},{3,19},{19,3},{4,20},{20... | collective-permute-start | bytes 884744 | tf_op jit(solution)/shard_map/ppermute | solution.py:383
  29.0 14.7 %collective-permute-start.4 = (bf16[96,1536]{1,0:T(8,128)(2,1)}, bf16[96,1536]{1,0:T(8,128)(2,1)}, u32[]{:S(2)}, u32[]{:S(2)}) collective-permute-start(bf16[96,1536]{1,0:T(8,128)(2,1)} %collective-permute-done.1.refs_4_), channel_id=1, source_target_pairs={{0,16},{16,0},{1,17},{17,1},{2,18},{18,2},{3,19},{19,3},{4,20},{20... | collective-permute-start | bytes 884744 | tf_op jit(solution)/shard_map/ppermute | solution.py:383
  29.3 2.5 %copy-start.10 = (s32[4]{0:T(128)}, s32[4]{0:T(128)S(1)}, u32[]{:S(2)}) copy-start(s32[4]{0:T(128)S(1)} %pad_add_fusion.where_ref) | copy-start | bytes 52
  29.4 4.5 %copy-start.3 = (bf16[1024,768]{1,0:T(8,128)(2,1)S(1)}, bf16[1024,768]{1,0:T(8,128)(2,1)}, u32[]{:S(2)}) copy-start(bf16[1024,768]{1,0:T(8,128)(2,1)} %z_ref.5) | copy-start | bytes 4718596
  31.8 1.6 %copy-start.1 = (f32[512,1536]{1,0:T(8,128)}, f32[512,1536]{1,0:T(8,128)S(1)}, u32[]{:S(2)}) copy-start(f32[512,1536]{1,0:T(8,128)S(1)} %slope_rows.1.pre_act_ref) | copy-start | bytes 9437188
  33.9 9.8 %copy-start.13 = (bf16[96,1536]{1,0:T(8,128)(2,1)S(1)}, bf16[96,1536]{1,0:T(8,128)(2,1)}, u32[]{:S(2)}) copy-start(bf16[96,1536]{1,0:T(8,128)(2,1)} %refs_0_.3) | copy-start | bytes 884740
  33.9 10.4 %copy-start.14 = (bf16[96,1536]{1,0:T(8,128)(2,1)S(1)}, bf16[96,1536]{1,0:T(8,128)(2,1)}, u32[]{:S(2)}) copy-start(bf16[96,1536]{1,0:T(8,128)(2,1)} %refs_1_.3) | copy-start | bytes 884740
  43.7 2.7 %collective-permute-start.6 = (bf16[96,1536]{1,0:T(8,128)(2,1)S(1)}, bf16[96,1536]{1,0:T(8,128)(2,1)S(1)}, u32[]{:S(2)}, u32[]{:S(2)}) collective-permute-start(bf16[96,1536]{1,0:T(8,128)(2,1)S(1)} %copy-done.13), channel_id=1, source_target_pairs={{0,1},{1,0},{2,3},{3,2},{4,5},{5,4},{6,7},{7,6},{8,9},{9,8},{10,11... | collective-permute-start | bytes 884744 | tf_op jit(solution)/shard_map/ppermute | solution.py:388
  44.3 2.3 %collective-permute-start.7 = (bf16[96,1536]{1,0:T(8,128)(2,1)S(1)}, bf16[96,1536]{1,0:T(8,128)(2,1)S(1)}, u32[]{:S(2)}, u32[]{:S(2)}) collective-permute-start(bf16[96,1536]{1,0:T(8,128)(2,1)S(1)} %copy-done.14), channel_id=1, source_target_pairs={{0,1},{1,0},{2,3},{3,2},{4,5},{5,4},{6,7},{7,6},{8,9},{9,8},{10,11... | collective-permute-start | bytes 884744 | tf_op jit(solution)/shard_map/ppermute | solution.py:388
  44.3 2.6 %collective-permute-start.10 = (bf16[96,1536]{1,0:T(8,128)(2,1)}, bf16[96,1536]{1,0:T(8,128)(2,1)}, u32[]{:S(2)}, u32[]{:S(2)}) collective-permute-start(bf16[96,1536]{1,0:T(8,128)(2,1)} %collective-permute-done.1.refs_4_), channel_id=1, source_target_pairs={{0,1},{1,0},{2,3},{3,2},{4,5},{5,4},{6,7},{7,6},{8,9},{9,8},{10,11... | collective-permute-start | bytes 884744 | tf_op jit(solution)/shard_map/ppermute | solution.py:388
  44.8 8.9 %collective-permute-start.5 = (bf16[96,1536]{1,0:T(8,128)(2,1)}, bf16[96,1536]{1,0:T(8,128)(2,1)}, u32[]{:S(2)}, u32[]{:S(2)}) collective-permute-start(bf16[96,1536]{1,0:T(8,128)(2,1)} %collective-permute-done.2.refs_6_), channel_id=1, source_target_pairs={{0,16},{16,0},{1,17},{17,1},{2,18},{18,2},{3,19},{19,3},{4,20},{20... | collective-permute-start | bytes 884744 | tf_op jit(solution)/shard_map/ppermute | solution.py:383
  46.0 8.7 %collective-permute-start.8 = (bf16[96,1536]{1,0:T(8,128)(2,1)S(1)}, bf16[96,1536]{1,0:T(8,128)(2,1)}, u32[]{:S(2)}, u32[]{:S(2)}) collective-permute-start(bf16[96,1536]{1,0:T(8,128)(2,1)S(1)} %collective-permute-done.refs_2_), channel_id=1, source_target_pairs={{0,1},{1,0},{2,3},{3,2},{4,5},{5,4},{6,7},{7,6},{8,9},{9,8},{10,11... | collective-permute-start | bytes 884744 | tf_op jit(solution)/shard_map/ppermute | solution.py:388
  46.4 9.7 %copy-start.16 = (bf16[96,1536]{1,0:T(8,128)(2,1)}, bf16[96,1536]{1,0:T(8,128)(2,1)S(1)}, u32[]{:S(2)}) copy-start(bf16[96,1536]{1,0:T(8,128)(2,1)S(1)} %collective-permute-done.6.refs_8_) | copy-start | bytes 884740
  46.4 8.4 %collective-permute-start.12 = (bf16[96,1536]{1,0:T(8,128)(2,1)}, bf16[96,1536]{1,0:T(8,128)(2,1)S(1)}, u32[]{:S(2)}, u32[]{:S(2)}) collective-permute-start(bf16[96,1536]{1,0:T(8,128)(2,1)} %collective-permute-done.2.refs_6_), channel_id=1, source_target_pairs={{0,1},{1,0},{2,3},{3,2},{4,5},{5,4},{6,7},{7,6},{8,9},{9,8},{10,11... | collective-permute-start | bytes 884744 | tf_op jit(solution)/shard_map/ppermute | solution.py:388
  46.5 9.5 %copy-start.17 = (bf16[96,1536]{1,0:T(8,128)(2,1)}, bf16[96,1536]{1,0:T(8,128)(2,1)S(1)}, u32[]{:S(2)}) copy-start(bf16[96,1536]{1,0:T(8,128)(2,1)S(1)} %collective-permute-done.7.refs_9_) | copy-start | bytes 884740
  46.6 8.2 %collective-permute-start.11 = (bf16[96,1536]{1,0:T(8,128)(2,1)}, bf16[96,1536]{1,0:T(8,128)(2,1)S(1)}, u32[]{:S(2)}, u32[]{:S(2)}) collective-permute-start(bf16[96,1536]{1,0:T(8,128)(2,1)} %collective-permute-done.4.refs_5_), channel_id=1, source_target_pairs={{0,1},{1,0},{2,3},{3,2},{4,5},{5,4},{6,7},{7,6},{8,9},{9,8},{10,11... | collective-permute-start | bytes 884744 | tf_op jit(solution)/shard_map/ppermute | solution.py:388
  46.9 7.9 %collective-permute-start.9 = (bf16[96,1536]{1,0:T(8,128)(2,1)}, bf16[96,1536]{1,0:T(8,128)(2,1)}, u32[]{:S(2)}, u32[]{:S(2)}) collective-permute-start(bf16[96,1536]{1,0:T(8,128)(2,1)} %collective-permute-done.3.refs_3_), channel_id=1, source_target_pairs={{0,1},{1,0},{2,3},{3,2},{4,5},{5,4},{6,7},{7,6},{8,9},{9,8},{10,11... | collective-permute-start | bytes 884744 | tf_op jit(solution)/shard_map/ppermute | solution.py:388
  53.7 2.4 %collective-permute-start.13 = (bf16[96,1536]{1,0:T(8,128)(2,1)}, bf16[96,1536]{1,0:T(8,128)(2,1)}, u32[]{:S(2)}, u32[]{:S(2)}) collective-permute-start(bf16[96,1536]{1,0:T(8,128)(2,1)} %collective-permute-done.5.refs_7_), channel_id=1, source_target_pairs={{0,1},{1,0},{2,3},{3,2},{4,5},{5,4},{6,7},{7,6},{8,9},{9,8},{10,11... | collective-permute-start | bytes 884744 | tf_op jit(solution)/shard_map/ppermute | solution.py:388
  54.8 1.3 copy-start.18
  54.8 1.3 copy-start.19
  64.2 19.0 %collective-permute-start.14 = (bf16[512,768]{1,0:T(8,128)(2,1)}, bf16[512,768]{1,0:T(8,128)(2,1)S(1)}, u32[]{:S(2)}, u32[]{:S(2)}) collective-permute-start(bf16[512,768]{1,0:T(8,128)(2,1)} %get-tuple-element.37), channel_id=1, source_target_pairs={{0,2},{2,0},{1,3},{3,1},{4,6},{6,4},{5,7},{7,5},{8,10},{10,8},{9,1... | collective-permute-start | bytes 2359304 | tf_op jit(solution)/shard_map/ppermute | solution.py:565
  79.2 18.9 %collective-permute-start.16 = (bf16[384,1536]{1,0:T(8,128)(2,1)}, bf16[384,1536]{1,0:T(8,128)(2,1)}, u32[]{:S(2)}, u32[]{:S(2)}) collective-permute-start(bf16[384,1536]{1,0:T(8,128)(2,1)} %convolution_convert_fusion.1), channel_id=1, source_target_pairs={{0,1},{1,0},{2,3},{3,2},{4,5},{5,4},{6,7},{7,6},{8,9},{9,8},{10,11... | collective-permute-start | bytes 3538952 | tf_op jit(solution)/shard_map/ppermute | solution.py:532
  79.9 3.3 %copy-start.9 = (bf16[512,768]{1,0:T(8,128)(2,1)S(1)}, bf16[512,768]{1,0:T(8,128)(2,1)}, u32[]{:S(2)}) copy-start(bf16[512,768]{1,0:T(8,128)(2,1)} %get-tuple-element.42.refs_0_) | copy-start | bytes 2359300
  80.3 2.9 %copy-start.4 = (bf16[1024,768]{1,0:T(8,128)(2,1)S(1)}, bf16[1024,768]{1,0:T(8,128)(2,1)}, u32[]{:S(2)}) copy-start(bf16[1024,768]{1,0:T(8,128)(2,1)} %z_ref.5) | copy-start | bytes 4718596
  80.3 2.9 %copy-start.6 = (f32[1024,768]{1,0:T(8,128)S(1)}, f32[1024,768]{1,0:T(8,128)}, u32[]{:S(2)}) copy-start(f32[1024,768]{1,0:T(8,128)} %copy-done.5) | copy-start | bytes 9437188
  80.3 2.9 %copy-start.11 = (s32[4]{0:T(128)S(1)}, s32[4]{0:T(128)}, u32[]{:S(2)}) copy-start(s32[4]{0:T(128)} %copy-done.10) | copy-start | bytes 52
  87.1 20.9 %collective-permute-start.15 = (bf16[512,384]{1,0:T(8,128)(2,1)S(1)}, bf16[512,384]{1,0:T(8,128)(2,1)}, u32[]{:S(2)}, u32[]{:S(2)}) collective-permute-start(bf16[512,384]{1,0:T(8,128)(2,1)S(1)} %get-tuple-element.55), channel_id=1, source_target_pairs={{0,2},{2,0},{1,3},{3,1},{4,6},{6,4},{5,7},{7,5},{8,10},{10,8},{9,1... | collective-permute-start | bytes 1179656 | tf_op jit(solution)/shard_map/ppermute | solution.py:594
  88.4 24.6 %all-to-all-start = ((bf16[16,48,512]{2,1,0:T(8,128)(2,1)}), bf16[16,48,512]{2,1,0:T(8,128)(2,1)S(1)}, u32[]{:S(2)}, u32[]{:S(2)}) async-start(bf16[16,48,512]{2,1,0:T(8,128)(2,1)} %bitcast.5), calls=%async_computation | async-start | bytes 1572864 | tf_op jit(solution)/shard_map/all_to_all | solution.py:584
  93.3 38.8 %reduce-scatter.5.cloned.1.call-start = ((), (), s32[]{:S(2)}) async-start(), calls=%async_computation.5 | async-start | bytes 1474560 | tf_op jit(solution)/shard_map/reduce_scatter | solution.py:536
  94.5 3.6 %copy-start.12 = (bf16[1024,1536]{1,0:T(8,128)(2,1)S(1)}, bf16[1024,1536]{1,0:T(8,128)(2,1)}, u32[]{:S(2)}) copy-start(bf16[1024,1536]{1,0:T(8,128)(2,1)} %get-tuple-element.49) | copy-start | bytes 9437188
  113.0 0.9 copy-start.20
  119.6 30.5 %all-to-all-start.1 = ((bf16[16,192,128]{2,1,0:T(8,128)(2,1)}), bf16[16,192,128]{2,1,0:T(8,128)(2,1)S(1)}, u32[]{:S(2)}, u32[]{:S(2)}) async-start(bf16[16,192,128]{2,1,0:T(8,128)(2,1)} %bitcast.16), calls=%async_computation.2 | async-start | bytes 1572864 | tf_op jit(solution)/shard_map/all_to_all | solution.py:598
Sparse Core Ops, SparseCore 0:
  43.8 33.1 reduce-scatter.2
  102.0 30.0 reduce-scatter.4

commit v5 on v4

--- a/solution.py
+++ b/solution.py
@@ -464,7 +464,7 @@
             jax.ShapeDtypeStruct((rows, width), jnp.bfloat16),
         ],
         input_output_aliases={3 + len(flat): 0} if extra else {},
-        compiler_params=pltpu.CompilerParams(vmem_limit_bytes=60 << 20),
+        compiler_params=pltpu.CompilerParams(vmem_limit_bytes=48 << 20),
         cost_estimate=SMALL,
         name="feed_rows",
     )(where, low, pre_act if slope is None else slope, *flat, *extra)
@@ -514,9 +514,8 @@
 
     ffn_grad, ffn_low = ffn_norm(z_ffn, grad_out, gain_ffn)
     fast = shard_rows % 16 == 0 and rows % ROWS == 0 and unit_count % 128 == 0
-    slopes = [slope_rows(where, pre_act, rows, step) for step in range(1, hids)] if fast else []
-    pieces, arrived, (normed_core, slopes) = weight_pieces(
-        w_out, w_in, (ffn_low,), (mix_norm(z_mix, gain_mix, core_reorder), slopes)
+    pieces, arrived, normed_core = weight_pieces(
+        w_out, w_in, (ffn_low,), mix_norm(z_mix, gain_mix, core_reorder)
     )
 
     def core_rows(left, right, core):
@@ -543,8 +542,7 @@
     if fast:
         pre_grad = None
         for step in [*range(1, hids), 0]:
-            slope = slopes[step - 1] if step else None
-            pre_grad, part = feed_rows(where, ffn_low, pre_act, pieces, rows, step, pre_grad, slope)
+            pre_grad, part = feed_rows(where, ffn_low, pre_act, pieces, rows, step, pre_grad)
             partials.append(part)
     else:
         whole = whole_weights(pieces, width)

time: 160 us -> 159 us (level)
  Pallas kernels: 37.3 us -> 33.5 us
  waiting for transfers between devices: 36 us -> 38.9 us
  starting transfers between devices: 29.6 us -> 31.8 us
  local copies, waits for them, and re-layouts: 7.57 us -> 5.72 us
    ppermute x3, waiting for transfers between devices: 5.72 us -> 8.42 us  [weight_pieces(): lax.ppermute(w, 'seq', shift_pairs(chips, d))]
    pallas_call x1 -> x0, Pallas kernels: 2.39 us -> none  [slope_rows(): pl.pallas_call(slope_kernel, grid_spec=pltpu.PrefetchScalarGridSpec(num_s...]
    unnamed x44 -> x24, local copies, waits for them, and re-layouts: 5.41 us -> 3.55 us
  transfers between devices with their start and end apart: 21 -> 21, of which waited for: 7 -> 7; matrix products, arithmetic and copies ran while one was open for 22% -> 22% of each run, Pallas kernels for 22% -> 20%
where the time goes in v5:
time: 159 us
  waiting for transfers between devices  38.9 us (24%)
  Pallas kernels  33.5 us (21%)
  starting transfers between devices  31.8 us (20%)
  other arithmetic  22.3 us (14%)
  between operations  14.3 us (9%)
  matrix products  12 us (8%)
  local copies, waits for them, and re-layouts  5.72 us (4%)
    all_to_all x1, waiting for transfers between devices, local(): lax.all_to_all(sent_back, TEAM, split_axis=0, concat_axis=0, tiled=True)  16.3 us
    pallas_call x2, Pallas kernels, feed_rows(): pl.pallas_call(functools.partial(feed_kernel, keys, len(flat), shard, chi...  16.1 us
    all_to_all x1, starting transfers between devices, local(): lax.all_to_all(sent_back, TEAM, split_axis=0, concat_axis=0, tiled=True)  10.9 us
    ppermute x3, waiting for transfers between devices, weight_pieces(): lax.ppermute(w, 'seq', shift_pairs(chips, d))  8.42 us
    dot_general x2, matrix products, core_rows(): lax.dot_general(part, right, contract_rows, preferred_element_type=jnp.fl...  8.05 us
    ppermute x3, waiting for transfers between devices, weight_pieces(): lax.ppermute(blocks[0], 'groups', shift_pairs(2, 1))  6.61 us
    pallas_call x1, Pallas kernels, position_transform(): pl.pallas_call(functools.partial(position_kernel, spans, hids, slots), gr...  5.74 us
    all_to_all x1, starting transfers between devices, local(): lax.all_to_all(spectral.reshape(team, 2 * slots, rows), TEAM, split_axis=...  5.73 us
  transfers between devices with their start and end apart: 21, of which 7 were waited for; matrix products, arithmetic and copies ran while one was open for 22% of the time, Pallas kernels for 20%

profile of v5, /device:TPU:1, one launch (start us, length us, event | category | flops | bytes accessed | tf_op | source)
XLA Modules:
  0.0 158.6 jit_solution(5396770873181697714)
XLA Ops:
  7.2 1.7 %broadcast_select_fusion = bf16[96,1536]{1,0:T(8,128)(2,1)} fusion(bf16[96,1536]{1,0:T(8,128)(2,1)} %refs_0_.3, bf16[96,1536]{1,0:T(8,128)(2,1)} %refs_1_.3, pred[]{:T(512)S(6)} %eq.76), kind=kLoop, calls=%fused_computation.29 | loop fusion | flops 147456 | bytes 884737 | tf_op jit(solution)/shard_map/jit(_where)/select_n | solution.py:365
  8.9 2.1 %collective-permute-start = (bf16[96,1536]{1,0:T(8,128)(2,1)}, bf16[96,1536]{1,0:T(8,128)(2,1)}, u32[]{:S(2)}, u32[]{:S(2)}) collective-permute-start(bf16[96,1536]{1,0:T(8,128)(2,1)} %broadcast_select_fusion), channel_id=1, source_target_pairs={{0,4},{4,8},{8,12},{12,0},{1,5},{5,9},{9,13},{13,1},{2,6},{6,10},{... | collective-permute-start | bytes 884744 | tf_op jit(solution)/shard_map/ppermute | solution.py:373
  11.1 2.0 %collective-permute-start.1 = (bf16[96,1536]{1,0:T(8,128)(2,1)}, bf16[96,1536]{1,0:T(8,128)(2,1)}, u32[]{:S(2)}, u32[]{:S(2)}) collective-permute-start(bf16[96,1536]{1,0:T(8,128)(2,1)} %broadcast_select_fusion), channel_id=1, source_target_pairs={{0,12},{4,0},{8,4},{12,8},{1,13},{5,1},{9,5},{13,9},{2,14},{6,2},{... | collective-permute-start | bytes 884744 | tf_op jit(solution)/shard_map/ppermute | solution.py:373
  13.1 0.7 broadcast_in_dim.41.gain_ref
  13.8 3.7 %fusion.5 = bf16[1024,1536]{1,0:T(8,128)(2,1)S(1)} fusion(bf16[1024,1536]{1,0:T(8,128)(2,1)} %pre_act_ref.3), kind=kLoop, calls=%fused_computation.9 | loop fusion | flops 15728640 | bytes 6291456 | tf_op jit(solution)/shard_map/convert_element_type | solution.py:537
  17.5 2.7 %ffn_norm.1 = (f32[1024,768]{1,0:T(8,128)S(1)}, bf16[1024,768]{1,0:T(8,128)(2,1)S(1)}) custom-call(bf16[1024,768]{1,0:T(8,128)(2,1)S(1)} %copy-done.6, bf16[1024,768]{1,0:T(8,128)(2,1)S(1)} %copy-done.7, f32[1,768]{1,0:T(1,128)S(1)} %broadcast_in_dim.41.gain_ref), custom_call_target="tpu_custom_call" | custom-call | flops 1048576 | bytes 65536 | tf_op jit(solution)/shard_map/ffn_norm/pallas_call | solution.py:252
  20.2 1.7 %copy-done.2 = f32[1024,768]{1,0:T(8,128)} copy-done((f32[1024,768]{1,0:T(8,128)}, f32[1024,768]{1,0:T(8,128)S(1)}, u32[]{:S(2)}) %copy-start.2) | copy-done | bytes 3145752
  21.9 4.0 %convolution_convert_fusion = bf16[768,1536]{1,0:T(8,128)(2,1)} fusion(bf16[1024,768]{1,0:T(8,128)(2,1)S(1)} %get-tuple-element.28.x_ref, bf16[1024,1536]{1,0:T(8,128)(2,1)S(1)} %fusion.5), kind=kOutput, calls=%fused_computation.13 | convolution fusion | flops 2417098752 | bytes 7077888 | tf_op jit(solution)/shard_map/dot_general | solution.py:538
  26.0 0.8 collective-permute-start.2
  26.8 1.0 collective-permute-start.3
  27.8 0.5 collective-permute-start.4
  28.4 0.4 fusion.8.order_ref
  28.9 4.0 %mix_norm.1 = bf16[1024,768]{1,0:T(8,128)(2,1)S(1)} custom-call(bf16[1024,768]{1,0:T(8,128)(2,1)S(1)} %copy-done.1, f32[1,768]{1,0:T(1,128)S(1)} %broadcast_in_dim.42.gain_ref, bf16[768,768]{1,0:T(8,128)(2,1)S(1)} %fusion.8.order_ref), custom_call_target="tpu_custom_call" | custom-call | flops 1048576 | bytes 65536 | tf_op jit(solution)/shard_map/mix_norm/pallas_call | solution.py:275
  32.9 8.4 %collective-permute-done.2.refs_6_ = bf16[96,1536]{1,0:T(8,128)(2,1)} collective-permute-done((bf16[96,1536]{1,0:T(8,128)(2,1)}, bf16[96,1536]{1,0:T(8,128)(2,1)}, u32[]{:S(2)}, u32[]{:S(2)}) %collective-permute-start.2) | collective-permute-done | bytes 294944 | tf_op jit(solution)/shard_map/ppermute | solution.py:373
  41.3 1.8 %collective-permute-start.6 = (bf16[96,1536]{1,0:T(8,128)(2,1)S(1)}, bf16[96,1536]{1,0:T(8,128)(2,1)}, u32[]{:S(2)}, u32[]{:S(2)}) collective-permute-start(bf16[96,1536]{1,0:T(8,128)(2,1)S(1)} %copy-done.4), channel_id=1, source_target_pairs={{0,1},{1,0},{2,3},{3,2},{4,5},{5,4},{6,7},{7,6},{8,9},{9,8},{10,11... | collective-permute-start | bytes 884744 | tf_op jit(solution)/shard_map/ppermute | solution.py:388
  43.2 0.4 collective-permute-start.10
  43.6 1.3 collective-permute-start.5
  45.9 6.6 %collective-permute-done.5.refs_7_ = bf16[96,1536]{1,0:T(8,128)(2,1)} collective-permute-done((bf16[96,1536]{1,0:T(8,128)(2,1)}, bf16[96,1536]{1,0:T(8,128)(2,1)}, u32[]{:S(2)}, u32[]{:S(2)}) %collective-permute-start.5) | collective-permute-done | bytes 294944 | tf_op jit(solution)/shard_map/ppermute | solution.py:383
  52.5 0.8 collective-permute-start.13
  53.7 1.2 collective-permute-done.13.refs_15_
  54.9 1.0 copy-done.5
  55.9 8.1 %feed_rows.2 = (bf16[1024,1536]{1,0:T(8,128)(2,1)}, bf16[512,768]{1,0:T(8,128)(2,1)S(1)}) custom-call(s32[4]{0:T(128)S(1)} %pad_add_fusion.where_ref, bf16[1024,768]{1,0:T(8,128)(2,1)} %copy-done, bf16[1024,1536]{1,0:T(8,128)(2,1)} %pre_act_ref.3, bf16[96,1536]{1,0:T(8,128)(2,1)S(1)} %copy-done.4, bf16[96,1536]{1,0:T(8,128)(2,1)S(1)} %copy-done.5, ...), custom_call_target="tpu_custom_call" | custom-call | flops 1048576 | bytes 65536 | tf_op jit(solution)/shard_map/feed_rows/pallas_call | solution.py:442
  64.0 1.3 collective-permute-start.14
  65.2 8.1 %feed_rows.3 = (bf16[1024,1536]{1,0:T(8,128)(2,1)}, bf16[512,768]{1,0:T(8,128)(2,1)S(1)}) custom-call(s32[4]{0:T(128)S(1)} %pad_add_fusion.where_ref, bf16[1024,768]{1,0:T(8,128)(2,1)} %copy-done, bf16[1024,1536]{1,0:T(8,128)(2,1)} %pre_act_ref.3, bf16[96,1536]{1,0:T(8,128)(2,1)S(1)} %copy-done.4, ...), custom_call_target="tpu_custom_call", output_to_operand_aliasing={{0}: (19, {})} | custom-call | flops 1048576 | bytes 65536 | tf_op jit(solution)/shard_map/feed_rows/pallas_call | solution.py:442
  73.3 0.4 fusion.23
  73.7 4.4 %convolution_convert_fusion.1 = bf16[384,1536]{1,0:T(8,128)(2,1)} fusion(bf16[1024,1536]{1,0:T(8,128)(2,1)} %get-tuple-element.47, bf16[1024,768]{1,0:T(8,128)(2,1)S(1)} %mix_norm.1), kind=kOutput, calls=%fused_computation.16 | convolution fusion | flops 1208549376 | bytes 5111808 | tf_op jit(solution)/shard_map/dot_general | solution.py:523
  78.3 0.7 collective-permute-start.16
  79.1 0.4 multiply_subtract_fusion
  79.9 2.9 %collective-permute-done.14.refs_1_ = bf16[512,768]{1,0:T(8,128)(2,1)S(1)} collective-permute-done((bf16[512,768]{1,0:T(8,128)(2,1)S(1)}, bf16[512,768]{1,0:T(8,128)(2,1)S(1)}, u32[]{:S(2)}, u32[]{:S(2)}) %collective-permute-start.14) | collective-permute-done | bytes 786464 | tf_op jit(solution)/shard_map/ppermute | solution.py:563
  82.8 2.9 %mix_rows.1 = (bf16[512,768]{1,0:T(8,128)(2,1)S(1)}, bf16[768,512]{1,0:T(8,128)(2,1)S(1)}) custom-call(s32[4]{0:T(128)S(1)} %pad_add_fusion.where_ref, bf16[1024,768]{1,0:T(8,128)(2,1)S(1)} %copy-done.1, f32[1024,768]{1,0:T(8,128)S(1)} %copy-done.3, f32[1,768]{1,0:T(1,128)S(1)} %broadcast_in_dim.42.gain_ref, bf16[768,768]{1,0:T(8,128)(2,1)S(1)} %fusion.7.tab_ref, ...), custom_call_target="tpu_custom_call" | custom-call | flops 1048576 | bytes 65536 | tf_op jit(solution)/shard_map/mix_rows/pallas_call | solution.py:337
  85.9 1.2 collective-permute-start.15
  87.1 5.7 %all-to-all-start = ((bf16[16,48,512]{2,1,0:T(8,128)(2,1)}), bf16[16,48,512]{2,1,0:T(8,128)(2,1)S(1)}, u32[]{:S(2)}, u32[]{:S(2)}) async-start(bf16[16,48,512]{2,1,0:T(8,128)(2,1)} %bitcast.15), calls=%async_computation | async-start | bytes 1572864 | tf_op jit(solution)/shard_map/all_to_all | solution.py:582
  92.9 1.1 fusion.27
  94.0 3.7 %subtract_convert_fusion.1 = (bf16[1,32,32,1024]{3,2,1,0:T(8,128)(2,1)}, bf16[1,32,32,1024]{3,2,1,0:T(8,128)(2,1)}) fusion(f32[32,1024]{1,0:T(8,128)S(1)} %get-tuple-element.70, f32[32,1024]{1,0:T(8,128)S(1)} %get-tuple-element.59, f32[32,1024]{1,0:T(8,128)S(1)} %get-tuple-element.71, f32[32,1024]{1,0:T(8,128)S(1)} %get-tuple-element.61, ...), kind=kLoop, calls=%fused_computation.12 | loop fusion | flops 8388608 | bytes 4849664 | tf_op jit(solution)/shard_map/convert
  97.8 3.7 %fusion.6 = bf16[384,1536]{1,0:T(8,128)(2,1)} fusion(bf16[1024,1536]{1,0:T(8,128)(2,1)S(1)} %copy-done.9, bf16[384,1536]{1,0:T(8,128)(2,1)} %collective-permute-done.16, bf16[1024,768]{1,0:T(8,128)(2,1)S(1)} %mix_norm.1), kind=kOutput, calls=%fused_computation.15 | convolution fusion | flops 1209729024 | bytes 6291456 | tf_op jit(solution)/shard_map/dot_general | solution.py:523
  101.5 4.6 %pad_maximum_fusion = bf16[2,32,32,1024]{3,2,1,0:T(8,128)(2,1)} fusion(bf16[1,32,32,1024]{3,2,1,0:T(8,128)(2,1)} %get-tuple-element.56, bf16[1,32,32,1024]{3,2,1,0:T(8,128)(2,1)} %get-tuple-element.55), kind=kLoop, calls=%fused_computation.10 | loop fusion | flops 2097152 | bytes 8388608 | tf_op jit(solution)/shard_map/stack | solution.py:72
  106.1 0.6 fusion.42.mark_ref
  106.9 0.6 maximum_multiply_fusion.twist_ref
  107.6 1.1 constant_dynamic-update-slice_fusion.own_ref
  108.6 1.8 %convert_element_type.123 = f32[96,1536]{1,0:T(8,128)} convert(bf16[96,1536]{1,0:T(8,128)(2,1)} %reduce-scatter.3.cloned.1.call-done) | non-fusion elementwise | flops 147456 | bytes 884736 | tf_op jit(solution)/shard_map/convert_element_type | solution.py:540
  110.5 2.0 %all-to-all-done.x_ref = bf16[16,48,512]{2,1,0:T(8,128)(2,1)S(1)} async-done(((bf16[16,48,512]{2,1,0:T(8,128)(2,1)}), bf16[16,48,512]{2,1,0:T(8,128)(2,1)S(1)}, u32[]{:S(2)}, u32[]{:S(2)}) %all-to-all-start) | async-done | bytes 786464 | tf_op jit(solution)/shard_map/all_to_all | solution.py:582
  112.5 0.9 copy-done.10
  113.4 5.7 %position_transform.1 = bf16[8,2,192,128]{3,2,1,0:T(8,128)(2,1)} custom-call(bf16[16,48,512]{2,1,0:T(8,128)(2,1)} %copy-done.10, f32[24,1]{1,0:T(8,128)} %fusion.42.mark_ref, f32[2,8,1024]{2,1,0:T(8,128)} %maximum_multiply_fusion.twist_ref, bf16[2048,1024]{1,0:T(8,128)(2,1)} %bitcast.16), custom_call_target="tpu_custom_call" | custom-call | flops 1610612736 | bytes 6291456 | tf_op jit(solution)/shard_map/position_transform/pallas_call | solution.py:163
  119.1 10.9 %all-to-all-start.1 = ((bf16[16,192,128]{2,1,0:T(8,128)(2,1)}), bf16[16,192,128]{2,1,0:T(8,128)(2,1)S(1)}, u32[]{:S(2)}, u32[]{:S(2)}) async-start(bf16[16,192,128]{2,1,0:T(8,128)(2,1)} %bitcast.17), calls=%async_computation.2 | async-start | bytes 1572864 | tf_op jit(solution)/shard_map/all_to_all | solution.py:596
  130.1 1.4 reduce-scatter.5.cloned.1.call-done
  131.6 1.8 %convert_element_type.131 = f32[96,1536]{1,0:T(8,128)} convert(bf16[96,1536]{1,0:T(8,128)(2,1)} %reduce-scatter.5.cloned.1.call-done) | non-fusion elementwise | flops 147456 | bytes 884736 | tf_op jit(solution)/shard_map/convert_element_type | solution.py:535
  133.4 16.3 %all-to-all-done.1.back_ref = bf16[16,192,128]{2,1,0:T(8,128)(2,1)S(1)} async-done(((bf16[16,192,128]{2,1,0:T(8,128)(2,1)}), bf16[16,192,128]{2,1,0:T(8,128)(2,1)S(1)}, u32[]{:S(2)}, u32[]{:S(2)}) %all-to-all-start.1) | async-done | bytes 786464 | tf_op jit(solution)/shard_map/all_to_all | solution.py:596
  149.7 2.1 %finish.1 = f32[1024,384]{1,0:T(8,128)} custom-call(bf16[16,192,128]{2,1,0:T(8,128)(2,1)S(1)} %all-to-all-done.1.back_ref, bf16[384,384]{1,0:T(8,128)(2,1)S(1)} %fusion.11.pick_ref, bf16[1024,384]{1,0:T(8,128)(2,1)S(1)} %constant_dynamic-update-slice_fusion.own_ref), custom_call_target="tpu_custom_call" | custom-call | flops 301989888 | bytes 5242880 | tf_op jit(solution)/shard_map/finish/pallas_call | solution.py:223
  (70 shorter events, 3.1 us)
Async XLA Ops:
  7.2 101.5 %reduce-scatter.3.cloned.1.call-start = ((), (), s32[]{:S(2)}) async-start(), calls=%async_computation.4 | async-start | bytes 2654208 | tf_op jit(solution)/shard_map/reduce_scatter | solution.py:540
  8.9 17.0 %collective-permute-start = (bf16[96,1536]{1,0:T(8,128)(2,1)}, bf16[96,1536]{1,0:T(8,128)(2,1)}, u32[]{:S(2)}, u32[]{:S(2)}) collective-permute-start(bf16[96,1536]{1,0:T(8,128)(2,1)} %broadcast_select_fusion), channel_id=1, source_target_pairs={{0,4},{4,8},{8,12},{12,0},{1,5},{5,9},{9,13},{13,1},{2,6},{6,10},{... | collective-permute-start | bytes 884744 | tf_op jit(solution)/shard_map/ppermute | solution.py:373
  11.1 14.9 %collective-permute-start.1 = (bf16[96,1536]{1,0:T(8,128)(2,1)}, bf16[96,1536]{1,0:T(8,128)(2,1)}, u32[]{:S(2)}, u32[]{:S(2)}) collective-permute-start(bf16[96,1536]{1,0:T(8,128)(2,1)} %broadcast_select_fusion), channel_id=1, source_target_pairs={{0,12},{4,0},{8,4},{12,8},{1,13},{5,1},{9,5},{13,9},{2,14},{6,2},{... | collective-permute-start | bytes 884744 | tf_op jit(solution)/shard_map/ppermute | solution.py:373
  13.8 3.7 %copy-start.6 = (bf16[1024,768]{1,0:T(8,128)(2,1)S(1)}, bf16[1024,768]{1,0:T(8,128)(2,1)}, u32[]{:S(2)}) copy-start(bf16[1024,768]{1,0:T(8,128)(2,1)} %z_ref.3) | copy-start | bytes 4718596
  13.8 3.8 %copy-start.7 = (bf16[1024,768]{1,0:T(8,128)(2,1)S(1)}, bf16[1024,768]{1,0:T(8,128)(2,1)}, u32[]{:S(2)}) copy-start(bf16[1024,768]{1,0:T(8,128)(2,1)} %up_ref.1) | copy-start | bytes 4718596
  20.2 1.7 %copy-start.2 = (f32[1024,768]{1,0:T(8,128)}, f32[1024,768]{1,0:T(8,128)S(1)}, u32[]{:S(2)}) copy-start(f32[1024,768]{1,0:T(8,128)S(1)} %get-tuple-element.37.ffn_ref) | copy-start | bytes 9437188
  21.9 4.0 %copy-start = (bf16[1024,768]{1,0:T(8,128)(2,1)}, bf16[1024,768]{1,0:T(8,128)(2,1)S(1)}, u32[]{:S(2)}) copy-start(bf16[1024,768]{1,0:T(8,128)(2,1)S(1)} %get-tuple-element.28.x_ref) | copy-start | bytes 4718596
  21.9 6.5 %copy-start.11 = (f32[768]{0:T(1024)S(1)}, f32[768]{0:T(1024)}, u32[]{:S(2)}) copy-start(f32[768]{0:T(1024)} %param.12) | copy-start | bytes 9220
  21.9 6.9 %copy-start.1 = (bf16[1024,768]{1,0:T(8,128)(2,1)S(1)}, bf16[1024,768]{1,0:T(8,128)(2,1)}, u32[]{:S(2)}) copy-start(bf16[1024,768]{1,0:T(8,128)(2,1)} %z_ref.5) | copy-start | bytes 4718596
  26.0 15.2 %collective-permute-start.2 = (bf16[96,1536]{1,0:T(8,128)(2,1)}, bf16[96,1536]{1,0:T(8,128)(2,1)}, u32[]{:S(2)}, u32[]{:S(2)}) collective-permute-start(bf16[96,1536]{1,0:T(8,128)(2,1)} %broadcast_select_fusion), channel_id=1, source_target_pairs={{0,8},{4,12},{8,0},{12,4},{1,9},{5,13},{9,1},{13,5},{2,10},{6,14},... | collective-permute-start | bytes 884744 | tf_op jit(solution)/shard_map/ppermute | solution.py:373
  26.8 14.5 %collective-permute-start.3 = (bf16[96,1536]{1,0:T(8,128)(2,1)}, bf16[96,1536]{1,0:T(8,128)(2,1)}, u32[]{:S(2)}, u32[]{:S(2)}) collective-permute-start(bf16[96,1536]{1,0:T(8,128)(2,1)} %collective-permute-done.refs_2_), channel_id=1, source_target_pairs={{0,16},{16,0},{1,17},{17,1},{2,18},{18,2},{3,19},{19,3},{4,20},{20... | collective-permute-start | bytes 884744 | tf_op jit(solution)/shard_map/ppermute | solution.py:383
  27.8 13.5 %collective-permute-start.4 = (bf16[96,1536]{1,0:T(8,128)(2,1)}, bf16[96,1536]{1,0:T(8,128)(2,1)}, u32[]{:S(2)}, u32[]{:S(2)}) collective-permute-start(bf16[96,1536]{1,0:T(8,128)(2,1)} %collective-permute-done.1.refs_4_), channel_id=1, source_target_pairs={{0,16},{16,0},{1,17},{17,1},{2,18},{18,2},{3,19},{19,3},{4,20},{20... | collective-permute-start | bytes 884744 | tf_op jit(solution)/shard_map/ppermute | solution.py:383
  28.8 12.4 %copy-start.4 = (bf16[96,1536]{1,0:T(8,128)(2,1)S(1)}, bf16[96,1536]{1,0:T(8,128)(2,1)}, u32[]{:S(2)}) copy-start(bf16[96,1536]{1,0:T(8,128)(2,1)} %refs_0_.3) | copy-start | bytes 884740
  41.3 3.9 %collective-permute-start.6 = (bf16[96,1536]{1,0:T(8,128)(2,1)S(1)}, bf16[96,1536]{1,0:T(8,128)(2,1)}, u32[]{:S(2)}, u32[]{:S(2)}) collective-permute-start(bf16[96,1536]{1,0:T(8,128)(2,1)S(1)} %copy-done.4), channel_id=1, source_target_pairs={{0,1},{1,0},{2,3},{3,2},{4,5},{5,4},{6,7},{7,6},{8,9},{9,8},{10,11... | collective-permute-start | bytes 884744 | tf_op jit(solution)/shard_map/ppermute | solution.py:388
  43.1 2.3 %collective-permute-start.7 = (bf16[96,1536]{1,0:T(8,128)(2,1)}, bf16[96,1536]{1,0:T(8,128)(2,1)}, u32[]{:S(2)}, u32[]{:S(2)}) collective-permute-start(bf16[96,1536]{1,0:T(8,128)(2,1)} %refs_1_.3), channel_id=1, source_target_pairs={{0,1},{1,0},{2,3},{3,2},{4,5},{5,4},{6,7},{7,6},{8,9},{9,8},{10,11... | collective-permute-start | bytes 884744 | tf_op jit(solution)/shard_map/ppermute | solution.py:388
  43.2 2.6 %collective-permute-start.10 = (bf16[96,1536]{1,0:T(8,128)(2,1)}, bf16[96,1536]{1,0:T(8,128)(2,1)}, u32[]{:S(2)}, u32[]{:S(2)}) collective-permute-start(bf16[96,1536]{1,0:T(8,128)(2,1)} %collective-permute-done.1.refs_4_), channel_id=1, source_target_pairs={{0,1},{1,0},{2,3},{3,2},{4,5},{5,4},{6,7},{7,6},{8,9},{9,8},{10,11... | collective-permute-start | bytes 884744 | tf_op jit(solution)/shard_map/ppermute | solution.py:388
  43.6 8.9 %collective-permute-start.5 = (bf16[96,1536]{1,0:T(8,128)(2,1)}, bf16[96,1536]{1,0:T(8,128)(2,1)}, u32[]{:S(2)}, u32[]{:S(2)}) collective-permute-start(bf16[96,1536]{1,0:T(8,128)(2,1)} %collective-permute-done.2.refs_6_), channel_id=1, source_target_pairs={{0,16},{16,0},{1,17},{17,1},{2,18},{18,2},{3,19},{19,3},{4,20},{20... | collective-permute-start | bytes 884744 | tf_op jit(solution)/shard_map/ppermute | solution.py:383
  44.9 8.8 %collective-permute-start.8 = (bf16[96,1536]{1,0:T(8,128)(2,1)}, bf16[96,1536]{1,0:T(8,128)(2,1)}, u32[]{:S(2)}, u32[]{:S(2)}) collective-permute-start(bf16[96,1536]{1,0:T(8,128)(2,1)} %collective-permute-done.refs_2_), channel_id=1, source_target_pairs={{0,1},{1,0},{2,3},{3,2},{4,5},{5,4},{6,7},{7,6},{8,9},{9,8},{10,11... | collective-permute-start | bytes 884744 | tf_op jit(solution)/shard_map/ppermute | solution.py:388
  45.2 8.4 %collective-permute-start.12 = (bf16[96,1536]{1,0:T(8,128)(2,1)}, bf16[96,1536]{1,0:T(8,128)(2,1)}, u32[]{:S(2)}, u32[]{:S(2)}) collective-permute-start(bf16[96,1536]{1,0:T(8,128)(2,1)} %collective-permute-done.2.refs_6_), channel_id=1, source_target_pairs={{0,1},{1,0},{2,3},{3,2},{4,5},{5,4},{6,7},{7,6},{8,9},{9,8},{10,11... | collective-permute-start | bytes 884744 | tf_op jit(solution)/shard_map/ppermute | solution.py:388
  45.4 8.3 %collective-permute-start.11 = (bf16[96,1536]{1,0:T(8,128)(2,1)}, bf16[96,1536]{1,0:T(8,128)(2,1)}, u32[]{:S(2)}, u32[]{:S(2)}) collective-permute-start(bf16[96,1536]{1,0:T(8,128)(2,1)} %collective-permute-done.4.refs_5_), channel_id=1, source_target_pairs={{0,1},{1,0},{2,3},{3,2},{4,5},{5,4},{6,7},{7,6},{8,9},{9,8},{10,11... | collective-permute-start | bytes 884744 | tf_op jit(solution)/shard_map/ppermute | solution.py:388
  45.7 7.9 %collective-permute-start.9 = (bf16[96,1536]{1,0:T(8,128)(2,1)}, bf16[96,1536]{1,0:T(8,128)(2,1)}, u32[]{:S(2)}, u32[]{:S(2)}) collective-permute-start(bf16[96,1536]{1,0:T(8,128)(2,1)} %collective-permute-done.3.refs_3_), channel_id=1, source_target_pairs={{0,1},{1,0},{2,3},{3,2},{4,5},{5,4},{6,7},{7,6},{8,9},{9,8},{10,11... | collective-permute-start | bytes 884744 | tf_op jit(solution)/shard_map/ppermute | solution.py:388
  52.5 2.4 %collective-permute-start.13 = (bf16[96,1536]{1,0:T(8,128)(2,1)}, bf16[96,1536]{1,0:T(8,128)(2,1)}, u32[]{:S(2)}, u32[]{:S(2)}) collective-permute-start(bf16[96,1536]{1,0:T(8,128)(2,1)} %collective-permute-done.5.refs_7_), channel_id=1, source_target_pairs={{0,1},{1,0},{2,3},{3,2},{4,5},{5,4},{6,7},{7,6},{8,9},{9,8},{10,11... | collective-permute-start | bytes 884744 | tf_op jit(solution)/shard_map/ppermute | solution.py:388
  54.9 1.0 copy-start.5
  64.0 18.8 %collective-permute-start.14 = (bf16[512,768]{1,0:T(8,128)(2,1)S(1)}, bf16[512,768]{1,0:T(8,128)(2,1)S(1)}, u32[]{:S(2)}, u32[]{:S(2)}) collective-permute-start(bf16[512,768]{1,0:T(8,128)(2,1)S(1)} %get-tuple-element.35), channel_id=1, source_target_pairs={{0,2},{2,0},{1,3},{3,1},{4,6},{6,4},{5,7},{7,5},{8,10},{10,8},{9,1... | collective-permute-start | bytes 2359304 | tf_op jit(solution)/shard_map/ppermute | solution.py:563
  78.3 19.4 %collective-permute-start.16 = (bf16[384,1536]{1,0:T(8,128)(2,1)}, bf16[384,1536]{1,0:T(8,128)(2,1)}, u32[]{:S(2)}, u32[]{:S(2)}) collective-permute-start(bf16[384,1536]{1,0:T(8,128)(2,1)} %convolution_convert_fusion.1), channel_id=1, source_target_pairs={{0,1},{1,0},{2,3},{3,2},{4,5},{5,4},{6,7},{7,6},{8,9},{9,8},{10,11... | collective-permute-start | bytes 3538952 | tf_op jit(solution)/shard_map/ppermute | solution.py:531
  79.5 3.3 %copy-start.3 = (f32[1024,768]{1,0:T(8,128)S(1)}, f32[1024,768]{1,0:T(8,128)}, u32[]{:S(2)}) copy-start(f32[1024,768]{1,0:T(8,128)} %copy-done.2) | copy-start | bytes 9437188
  85.6 1.5 copy-start.8
  85.9 21.7 %collective-permute-start.15 = (bf16[512,384]{1,0:T(8,128)(2,1)S(1)}, bf16[512,384]{1,0:T(8,128)(2,1)}, u32[]{:S(2)}, u32[]{:S(2)}) collective-permute-start(bf16[512,384]{1,0:T(8,128)(2,1)S(1)} %get-tuple-element.53), channel_id=1, source_target_pairs={{0,2},{2,0},{1,3},{3,1},{4,6},{6,4},{5,7},{7,5},{8,10},{10,8},{9,1... | collective-permute-start | bytes 1179656 | tf_op jit(solution)/shard_map/ppermute | solution.py:592
  87.1 25.4 %all-to-all-start = ((bf16[16,48,512]{2,1,0:T(8,128)(2,1)}), bf16[16,48,512]{2,1,0:T(8,128)(2,1)S(1)}, u32[]{:S(2)}, u32[]{:S(2)}) async-start(bf16[16,48,512]{2,1,0:T(8,128)(2,1)} %bitcast.15), calls=%async_computation | async-start | bytes 1572864 | tf_op jit(solution)/shard_map/all_to_all | solution.py:582
  92.9 38.7 %reduce-scatter.5.cloned.1.call-start = ((), (), s32[]{:S(2)}) async-start(), calls=%async_computation.5 | async-start | bytes 1474560 | tf_op jit(solution)/shard_map/reduce_scatter | solution.py:535
  94.0 3.7 %copy-start.9 = (bf16[1024,1536]{1,0:T(8,128)(2,1)S(1)}, bf16[1024,1536]{1,0:T(8,128)(2,1)}, u32[]{:S(2)}) copy-start(bf16[1024,1536]{1,0:T(8,128)(2,1)} %get-tuple-element.47) | copy-start | bytes 9437188
  112.5 0.9 copy-start.10
  119.1 30.5 %all-to-all-start.1 = ((bf16[16,192,128]{2,1,0:T(8,128)(2,1)}), bf16[16,192,128]{2,1,0:T(8,128)(2,1)S(1)}, u32[]{:S(2)}, u32[]{:S(2)}) async-start(bf16[16,192,128]{2,1,0:T(8,128)(2,1)} %bitcast.17), calls=%async_computation.2 | async-start | bytes 1572864 | tf_op jit(solution)/shard_map/all_to_all | solution.py:596
Sparse Core Ops, SparseCore 0:
  41.4 35.6 reduce-scatter.2
  101.6 29.8 reduce-scatter.4

commit v6 on v5

--- a/solution.py
+++ b/solution.py
@@ -330,7 +330,7 @@
 
 def mix_rows(where, z_mix, ffn_grad, gain, table, parts, hids):
     rows, width = parts[0].shape
-    size = min(rows, 256)
+    size = min(rows, 512)
     steps = rows // size
     tile = pl.BlockSpec((size, width), lambda i, w: (i, 0))
     own = pl.BlockSpec((size, width), lambda i, w: (w[0] * steps + i, 0))

time: 159 us -> 159 us (level)
  no operation moved by 1% of the time
where the time goes in v6:
time: 159 us; the launch traced here: 158 us
  waiting for transfers between devices  38.9 us (24%)
  Pallas kernels  33.1 us (21%)
  starting transfers between devices  31.8 us (20%)
  other arithmetic  22.3 us (14%)
  between operations  14.3 us (9%)
  matrix products  12 us (8%)
  local copies, waits for them, and re-layouts  5.72 us (4%)
    all_to_all x1, waiting for transfers between devices, local(): lax.all_to_all(sent_back, TEAM, split_axis=0, concat_axis=0, tiled=True)  16.3 us
    pallas_call x2, Pallas kernels, feed_rows(): pl.pallas_call(functools.partial(feed_kernel, keys, len(flat), shard, chi...  16.1 us
    all_to_all x1, starting transfers between devices, local(): lax.all_to_all(sent_back, TEAM, split_axis=0, concat_axis=0, tiled=True)  10.9 us
    ppermute x3, waiting for transfers between devices, weight_pieces(): lax.ppermute(w, 'seq', shift_pairs(chips, d))  8.42 us
    dot_general x2, matrix products, core_rows(): lax.dot_general(part, right, contract_rows, preferred_element_type=jnp.fl...  8.05 us
    ppermute x3, waiting for transfers between devices, weight_pieces(): lax.ppermute(blocks[0], 'groups', shift_pairs(2, 1))  6.61 us
    pallas_call x1, Pallas kernels, position_transform(): pl.pallas_call(functools.partial(position_kernel, spans, hids, slots), gr...  5.74 us
    all_to_all x1, starting transfers between devices, local(): lax.all_to_all(spectral.reshape(team, 2 * slots, rows), TEAM, split_axis=...  5.73 us
  transfers between devices with their start and end apart: 21, of which 7 were waited for; matrix products, arithmetic and copies ran while one was open for 22% of the time, Pallas kernels for 20%

profile of v6, /device:TPU:1, one launch (start us, length us, event | category | flops | bytes accessed | tf_op | source)
XLA Modules:
  0.0 158.1 jit_solution(856763870938200233)
XLA Ops:
  7.2 1.7 %broadcast_select_fusion = bf16[96,1536]{1,0:T(8,128)(2,1)} fusion(bf16[96,1536]{1,0:T(8,128)(2,1)} %refs_0_.3, bf16[96,1536]{1,0:T(8,128)(2,1)} %refs_1_.3, pred[]{:T(512)S(6)} %eq.76), kind=kLoop, calls=%fused_computation.29 | loop fusion | flops 147456 | bytes 884737 | tf_op jit(solution)/shard_map/jit(_where)/select_n | solution.py:365
  8.9 2.1 %collective-permute-start = (bf16[96,1536]{1,0:T(8,128)(2,1)}, bf16[96,1536]{1,0:T(8,128)(2,1)}, u32[]{:S(2)}, u32[]{:S(2)}) collective-permute-start(bf16[96,1536]{1,0:T(8,128)(2,1)} %broadcast_select_fusion), channel_id=1, source_target_pairs={{0,4},{4,8},{8,12},{12,0},{1,5},{5,9},{9,13},{13,1},{2,6},{6,10},{... | collective-permute-start | bytes 884744 | tf_op jit(solution)/shard_map/ppermute | solution.py:373
  11.1 2.0 %collective-permute-start.1 = (bf16[96,1536]{1,0:T(8,128)(2,1)}, bf16[96,1536]{1,0:T(8,128)(2,1)}, u32[]{:S(2)}, u32[]{:S(2)}) collective-permute-start(bf16[96,1536]{1,0:T(8,128)(2,1)} %broadcast_select_fusion), channel_id=1, source_target_pairs={{0,12},{4,0},{8,4},{12,8},{1,13},{5,1},{9,5},{13,9},{2,14},{6,2},{... | collective-permute-start | bytes 884744 | tf_op jit(solution)/shard_map/ppermute | solution.py:373
  13.1 0.7 broadcast_in_dim.41.gain_ref
  13.8 3.7 %fusion.5 = bf16[1024,1536]{1,0:T(8,128)(2,1)S(1)} fusion(bf16[1024,1536]{1,0:T(8,128)(2,1)} %pre_act_ref.3), kind=kLoop, calls=%fused_computation.9 | loop fusion | flops 15728640 | bytes 6291456 | tf_op jit(solution)/shard_map/convert_element_type | solution.py:537
  17.5 2.7 %ffn_norm.1 = (f32[1024,768]{1,0:T(8,128)S(1)}, bf16[1024,768]{1,0:T(8,128)(2,1)S(1)}) custom-call(bf16[1024,768]{1,0:T(8,128)(2,1)S(1)} %copy-done.6, bf16[1024,768]{1,0:T(8,128)(2,1)S(1)} %copy-done.7, f32[1,768]{1,0:T(1,128)S(1)} %broadcast_in_dim.41.gain_ref), custom_call_target="tpu_custom_call" | custom-call | flops 1048576 | bytes 65536 | tf_op jit(solution)/shard_map/ffn_norm/pallas_call | solution.py:252
  20.2 1.7 %copy-done.2 = f32[1024,768]{1,0:T(8,128)} copy-done((f32[1024,768]{1,0:T(8,128)}, f32[1024,768]{1,0:T(8,128)S(1)}, u32[]{:S(2)}) %copy-start.2) | copy-done | bytes 3145752
  21.9 4.0 %convolution_convert_fusion = bf16[768,1536]{1,0:T(8,128)(2,1)} fusion(bf16[1024,768]{1,0:T(8,128)(2,1)S(1)} %get-tuple-element.28.x_ref, bf16[1024,1536]{1,0:T(8,128)(2,1)S(1)} %fusion.5), kind=kOutput, calls=%fused_computation.13 | convolution fusion | flops 2417098752 | bytes 7077888 | tf_op jit(solution)/shard_map/dot_general | solution.py:538
  26.0 0.8 collective-permute-start.2
  26.8 1.0 collective-permute-start.3
  27.8 0.5 collective-permute-start.4
  28.4 0.4 fusion.8.order_ref
  28.9 4.0 %mix_norm.1 = bf16[1024,768]{1,0:T(8,128)(2,1)S(1)} custom-call(bf16[1024,768]{1,0:T(8,128)(2,1)S(1)} %copy-done.1, f32[1,768]{1,0:T(1,128)S(1)} %broadcast_in_dim.42.gain_ref, bf16[768,768]{1,0:T(8,128)(2,1)S(1)} %fusion.8.order_ref), custom_call_target="tpu_custom_call" | custom-call | flops 1048576 | bytes 65536 | tf_op jit(solution)/shard_map/mix_norm/pallas_call | solution.py:275
  32.9 8.4 %collective-permute-done.2.refs_6_ = bf16[96,1536]{1,0:T(8,128)(2,1)} collective-permute-done((bf16[96,1536]{1,0:T(8,128)(2,1)}, bf16[96,1536]{1,0:T(8,128)(2,1)}, u32[]{:S(2)}, u32[]{:S(2)}) %collective-permute-start.2) | collective-permute-done | bytes 294944 | tf_op jit(solution)/shard_map/ppermute | solution.py:373
  41.3 1.8 %collective-permute-start.6 = (bf16[96,1536]{1,0:T(8,128)(2,1)S(1)}, bf16[96,1536]{1,0:T(8,128)(2,1)}, u32[]{:S(2)}, u32[]{:S(2)}) collective-permute-start(bf16[96,1536]{1,0:T(8,128)(2,1)S(1)} %copy-done.4), channel_id=1, source_target_pairs={{0,1},{1,0},{2,3},{3,2},{4,5},{5,4},{6,7},{7,6},{8,9},{9,8},{10,11... | collective-permute-start | bytes 884744 | tf_op jit(solution)/shard_map/ppermute | solution.py:388
  43.2 0.4 collective-permute-start.10
  43.6 1.3 collective-permute-start.5
  45.9 6.6 %collective-permute-done.5.refs_7_ = bf16[96,1536]{1,0:T(8,128)(2,1)} collective-permute-done((bf16[96,1536]{1,0:T(8,128)(2,1)}, bf16[96,1536]{1,0:T(8,128)(2,1)}, u32[]{:S(2)}, u32[]{:S(2)}) %collective-permute-start.5) | collective-permute-done | bytes 294944 | tf_op jit(solution)/shard_map/ppermute | solution.py:383
  52.5 0.8 collective-permute-start.13
  53.7 1.2 collective-permute-done.13.refs_15_
  54.9 1.0 copy-done.5
  55.9 8.1 %feed_rows.2 = (bf16[1024,1536]{1,0:T(8,128)(2,1)}, bf16[512,768]{1,0:T(8,128)(2,1)S(1)}) custom-call(s32[4]{0:T(128)S(1)} %pad_add_fusion.where_ref, bf16[1024,768]{1,0:T(8,128)(2,1)} %copy-done, bf16[1024,1536]{1,0:T(8,128)(2,1)} %pre_act_ref.3, bf16[96,1536]{1,0:T(8,128)(2,1)S(1)} %copy-done.4, bf16[96,1536]{1,0:T(8,128)(2,1)S(1)} %copy-done.5, ...), custom_call_target="tpu_custom_call" | custom-call | flops 1048576 | bytes 65536 | tf_op jit(solution)/shard_map/feed_rows/pallas_call | solution.py:442
  64.0 1.3 collective-permute-start.14
  65.2 8.1 %feed_rows.3 = (bf16[1024,1536]{1,0:T(8,128)(2,1)}, bf16[512,768]{1,0:T(8,128)(2,1)S(1)}) custom-call(s32[4]{0:T(128)S(1)} %pad_add_fusion.where_ref, bf16[1024,768]{1,0:T(8,128)(2,1)} %copy-done, bf16[1024,1536]{1,0:T(8,128)(2,1)} %pre_act_ref.3, bf16[96,1536]{1,0:T(8,128)(2,1)S(1)} %copy-done.4, ...), custom_call_target="tpu_custom_call", output_to_operand_aliasing={{0}: (19, {})} | custom-call | flops 1048576 | bytes 65536 | tf_op jit(solution)/shard_map/feed_rows/pallas_call | solution.py:442
  73.3 0.4 fusion.23
  73.7 4.4 %convolution_convert_fusion.1 = bf16[384,1536]{1,0:T(8,128)(2,1)} fusion(bf16[1024,1536]{1,0:T(8,128)(2,1)} %get-tuple-element.47, bf16[1024,768]{1,0:T(8,128)(2,1)S(1)} %mix_norm.1), kind=kOutput, calls=%fused_computation.16 | convolution fusion | flops 1208549376 | bytes 5111808 | tf_op jit(solution)/shard_map/dot_general | solution.py:523
  78.3 0.7 collective-permute-start.16
  79.1 0.4 multiply_subtract_fusion
  79.9 2.9 %collective-permute-done.14.refs_1_ = bf16[512,768]{1,0:T(8,128)(2,1)S(1)} collective-permute-done((bf16[512,768]{1,0:T(8,128)(2,1)S(1)}, bf16[512,768]{1,0:T(8,128)(2,1)S(1)}, u32[]{:S(2)}, u32[]{:S(2)}) %collective-permute-start.14) | collective-permute-done | bytes 786464 | tf_op jit(solution)/shard_map/ppermute | solution.py:563
  82.8 2.4 %mix_rows.1 = (bf16[512,768]{1,0:T(8,128)(2,1)S(1)}, bf16[768,512]{1,0:T(8,128)(2,1)S(1)}) custom-call(s32[4]{0:T(128)S(1)} %pad_add_fusion.where_ref, bf16[1024,768]{1,0:T(8,128)(2,1)S(1)} %copy-done.1, f32[1024,768]{1,0:T(8,128)S(1)} %copy-done.3, f32[1,768]{1,0:T(1,128)S(1)} %broadcast_in_dim.42.gain_ref, bf16[768,768]{1,0:T(8,128)(2,1)S(1)} %fusion.7.tab_ref, ...), custom_call_target="tpu_custom_call" | custom-call | flops 1048576 | bytes 65536 | tf_op jit(solution)/shard_map/mix_rows/pallas_call | solution.py:337
  85.4 1.2 collective-permute-start.15
  86.6 5.7 %all-to-all-start = ((bf16[16,48,512]{2,1,0:T(8,128)(2,1)}), bf16[16,48,512]{2,1,0:T(8,128)(2,1)S(1)}, u32[]{:S(2)}, u32[]{:S(2)}) async-start(bf16[16,48,512]{2,1,0:T(8,128)(2,1)} %bitcast.15), calls=%async_computation | async-start | bytes 1572864 | tf_op jit(solution)/shard_map/all_to_all | solution.py:582
  92.5 1.1 fusion.27
  93.6 3.7 %subtract_convert_fusion.1 = (bf16[1,32,32,1024]{3,2,1,0:T(8,128)(2,1)}, bf16[1,32,32,1024]{3,2,1,0:T(8,128)(2,1)}) fusion(f32[32,1024]{1,0:T(8,128)S(1)} %get-tuple-element.70, f32[32,1024]{1,0:T(8,128)S(1)} %get-tuple-element.59, f32[32,1024]{1,0:T(8,128)S(1)} %get-tuple-element.71, f32[32,1024]{1,0:T(8,128)S(1)} %get-tuple-element.61, ...), kind=kLoop, calls=%fused_computation.12 | loop fusion | flops 8388608 | bytes 4849664 | tf_op jit(solution)/shard_map/convert
  97.3 3.7 %fusion.6 = bf16[384,1536]{1,0:T(8,128)(2,1)} fusion(bf16[1024,1536]{1,0:T(8,128)(2,1)S(1)} %copy-done.9, bf16[384,1536]{1,0:T(8,128)(2,1)} %collective-permute-done.16, bf16[1024,768]{1,0:T(8,128)(2,1)S(1)} %mix_norm.1), kind=kOutput, calls=%fused_computation.15 | convolution fusion | flops 1209729024 | bytes 6291456 | tf_op jit(solution)/shard_map/dot_general | solution.py:523
  101.0 4.6 %pad_maximum_fusion = bf16[2,32,32,1024]{3,2,1,0:T(8,128)(2,1)} fusion(bf16[1,32,32,1024]{3,2,1,0:T(8,128)(2,1)} %get-tuple-element.56, bf16[1,32,32,1024]{3,2,1,0:T(8,128)(2,1)} %get-tuple-element.55), kind=kLoop, calls=%fused_computation.10 | loop fusion | flops 2097152 | bytes 8388608 | tf_op jit(solution)/shard_map/stack | solution.py:72
  105.6 0.6 fusion.42.mark_ref
  106.4 0.6 maximum_multiply_fusion.twist_ref
  107.1 1.1 constant_dynamic-update-slice_fusion.own_ref
  108.2 1.8 %convert_element_type.123 = f32[96,1536]{1,0:T(8,128)} convert(bf16[96,1536]{1,0:T(8,128)(2,1)} %reduce-scatter.3.cloned.1.call-done) | non-fusion elementwise | flops 147456 | bytes 884736 | tf_op jit(solution)/shard_map/convert_element_type | solution.py:540
  110.0 2.0 %all-to-all-done.x_ref = bf16[16,48,512]{2,1,0:T(8,128)(2,1)S(1)} async-done(((bf16[16,48,512]{2,1,0:T(8,128)(2,1)}), bf16[16,48,512]{2,1,0:T(8,128)(2,1)S(1)}, u32[]{:S(2)}, u32[]{:S(2)}) %all-to-all-start) | async-done | bytes 786464 | tf_op jit(solution)/shard_map/all_to_all | solution.py:582
  112.0 0.9 copy-done.10
  112.9 5.7 %position_transform.1 = bf16[8,2,192,128]{3,2,1,0:T(8,128)(2,1)} custom-call(bf16[16,48,512]{2,1,0:T(8,128)(2,1)} %copy-done.10, f32[24,1]{1,0:T(8,128)} %fusion.42.mark_ref, f32[2,8,1024]{2,1,0:T(8,128)} %maximum_multiply_fusion.twist_ref, bf16[2048,1024]{1,0:T(8,128)(2,1)} %bitcast.16), custom_call_target="tpu_custom_call" | custom-call | flops 1610612736 | bytes 6291456 | tf_op jit(solution)/shard_map/position_transform/pallas_call | solution.py:163
  118.6 10.9 %all-to-all-start.1 = ((bf16[16,192,128]{2,1,0:T(8,128)(2,1)}), bf16[16,192,128]{2,1,0:T(8,128)(2,1)S(1)}, u32[]{:S(2)}, u32[]{:S(2)}) async-start(bf16[16,192,128]{2,1,0:T(8,128)(2,1)} %bitcast.17), calls=%async_computation.2 | async-start | bytes 1572864 | tf_op jit(solution)/shard_map/all_to_all | solution.py:596
  129.7 1.4 reduce-scatter.5.cloned.1.call-done
  131.1 1.8 %convert_element_type.131 = f32[96,1536]{1,0:T(8,128)} convert(bf16[96,1536]{1,0:T(8,128)(2,1)} %reduce-scatter.5.cloned.1.call-done) | non-fusion elementwise | flops 147456 | bytes 884736 | tf_op jit(solution)/shard_map/convert_element_type | solution.py:535
  132.9 16.3 %all-to-all-done.1.back_ref = bf16[16,192,128]{2,1,0:T(8,128)(2,1)S(1)} async-done(((bf16[16,192,128]{2,1,0:T(8,128)(2,1)}), bf16[16,192,128]{2,1,0:T(8,128)(2,1)S(1)}, u32[]{:S(2)}, u32[]{:S(2)}) %all-to-all-start.1) | async-done | bytes 786464 | tf_op jit(solution)/shard_map/all_to_all | solution.py:596
  149.2 2.1 %finish.1 = f32[1024,384]{1,0:T(8,128)} custom-call(bf16[16,192,128]{2,1,0:T(8,128)(2,1)S(1)} %all-to-all-done.1.back_ref, bf16[384,384]{1,0:T(8,128)(2,1)S(1)} %fusion.11.pick_ref, bf16[1024,384]{1,0:T(8,128)(2,1)S(1)} %constant_dynamic-update-slice_fusion.own_ref), custom_call_target="tpu_custom_call" | custom-call | flops 301989888 | bytes 5242880 | tf_op jit(solution)/shard_map/finish/pallas_call | solution.py:223
  (70 shorter events, 3.1 us)
Async XLA Ops:
  7.2 101.0 %reduce-scatter.3.cloned.1.call-start = ((), (), s32[]{:S(2)}) async-start(), calls=%async_computation.4 | async-start | bytes 2654208 | tf_op jit(solution)/shard_map/reduce_scatter | solution.py:540
  8.9 17.0 %collective-permute-start = (bf16[96,1536]{1,0:T(8,128)(2,1)}, bf16[96,1536]{1,0:T(8,128)(2,1)}, u32[]{:S(2)}, u32[]{:S(2)}) collective-permute-start(bf16[96,1536]{1,0:T(8,128)(2,1)} %broadcast_select_fusion), channel_id=1, source_target_pairs={{0,4},{4,8},{8,12},{12,0},{1,5},{5,9},{9,13},{13,1},{2,6},{6,10},{... | collective-permute-start | bytes 884744 | tf_op jit(solution)/shard_map/ppermute | solution.py:373
  11.1 14.9 %collective-permute-start.1 = (bf16[96,1536]{1,0:T(8,128)(2,1)}, bf16[96,1536]{1,0:T(8,128)(2,1)}, u32[]{:S(2)}, u32[]{:S(2)}) collective-permute-start(bf16[96,1536]{1,0:T(8,128)(2,1)} %broadcast_select_fusion), channel_id=1, source_target_pairs={{0,12},{4,0},{8,4},{12,8},{1,13},{5,1},{9,5},{13,9},{2,14},{6,2},{... | collective-permute-start | bytes 884744 | tf_op jit(solution)/shard_map/ppermute | solution.py:373
  13.8 3.7 %copy-start.6 = (bf16[1024,768]{1,0:T(8,128)(2,1)S(1)}, bf16[1024,768]{1,0:T(8,128)(2,1)}, u32[]{:S(2)}) copy-start(bf16[1024,768]{1,0:T(8,128)(2,1)} %z_ref.3) | copy-start | bytes 4718596
  13.8 3.8 %copy-start.7 = (bf16[1024,768]{1,0:T(8,128)(2,1)S(1)}, bf16[1024,768]{1,0:T(8,128)(2,1)}, u32[]{:S(2)}) copy-start(bf16[1024,768]{1,0:T(8,128)(2,1)} %up_ref.1) | copy-start | bytes 4718596
  20.2 1.7 %copy-start.2 = (f32[1024,768]{1,0:T(8,128)}, f32[1024,768]{1,0:T(8,128)S(1)}, u32[]{:S(2)}) copy-start(f32[1024,768]{1,0:T(8,128)S(1)} %get-tuple-element.37.ffn_ref) | copy-start | bytes 9437188
  21.9 4.0 %copy-start = (bf16[1024,768]{1,0:T(8,128)(2,1)}, bf16[1024,768]{1,0:T(8,128)(2,1)S(1)}, u32[]{:S(2)}) copy-start(bf16[1024,768]{1,0:T(8,128)(2,1)S(1)} %get-tuple-element.28.x_ref) | copy-start | bytes 4718596
  21.9 6.5 %copy-start.11 = (f32[768]{0:T(1024)S(1)}, f32[768]{0:T(1024)}, u32[]{:S(2)}) copy-start(f32[768]{0:T(1024)} %param.12) | copy-start | bytes 9220
  21.9 6.9 %copy-start.1 = (bf16[1024,768]{1,0:T(8,128)(2,1)S(1)}, bf16[1024,768]{1,0:T(8,128)(2,1)}, u32[]{:S(2)}) copy-start(bf16[1024,768]{1,0:T(8,128)(2,1)} %z_ref.5) | copy-start | bytes 4718596
  26.0 15.2 %collective-permute-start.2 = (bf16[96,1536]{1,0:T(8,128)(2,1)}, bf16[96,1536]{1,0:T(8,128)(2,1)}, u32[]{:S(2)}, u32[]{:S(2)}) collective-permute-start(bf16[96,1536]{1,0:T(8,128)(2,1)} %broadcast_select_fusion), channel_id=1, source_target_pairs={{0,8},{4,12},{8,0},{12,4},{1,9},{5,13},{9,1},{13,5},{2,10},{6,14},... | collective-permute-start | bytes 884744 | tf_op jit(solution)/shard_map/ppermute | solution.py:373
  26.8 14.5 %collective-permute-start.3 = (bf16[96,1536]{1,0:T(8,128)(2,1)}, bf16[96,1536]{1,0:T(8,128)(2,1)}, u32[]{:S(2)}, u32[]{:S(2)}) collective-permute-start(bf16[96,1536]{1,0:T(8,128)(2,1)} %collective-permute-done.refs_2_), channel_id=1, source_target_pairs={{0,16},{16,0},{1,17},{17,1},{2,18},{18,2},{3,19},{19,3},{4,20},{20... | collective-permute-start | bytes 884744 | tf_op jit(solution)/shard_map/ppermute | solution.py:383
  27.8 13.5 %collective-permute-start.4 = (bf16[96,1536]{1,0:T(8,128)(2,1)}, bf16[96,1536]{1,0:T(8,128)(2,1)}, u32[]{:S(2)}, u32[]{:S(2)}) collective-permute-start(bf16[96,1536]{1,0:T(8,128)(2,1)} %collective-permute-done.1.refs_4_), channel_id=1, source_target_pairs={{0,16},{16,0},{1,17},{17,1},{2,18},{18,2},{3,19},{19,3},{4,20},{20... | collective-permute-start | bytes 884744 | tf_op jit(solution)/shard_map/ppermute | solution.py:383
  28.8 12.4 %copy-start.4 = (bf16[96,1536]{1,0:T(8,128)(2,1)S(1)}, bf16[96,1536]{1,0:T(8,128)(2,1)}, u32[]{:S(2)}) copy-start(bf16[96,1536]{1,0:T(8,128)(2,1)} %refs_0_.3) | copy-start | bytes 884740
  41.3 3.9 %collective-permute-start.6 = (bf16[96,1536]{1,0:T(8,128)(2,1)S(1)}, bf16[96,1536]{1,0:T(8,128)(2,1)}, u32[]{:S(2)}, u32[]{:S(2)}) collective-permute-start(bf16[96,1536]{1,0:T(8,128)(2,1)S(1)} %copy-done.4), channel_id=1, source_target_pairs={{0,1},{1,0},{2,3},{3,2},{4,5},{5,4},{6,7},{7,6},{8,9},{9,8},{10,11... | collective-permute-start | bytes 884744 | tf_op jit(solution)/shard_map/ppermute | solution.py:388
  43.1 2.3 %collective-permute-start.7 = (bf16[96,1536]{1,0:T(8,128)(2,1)}, bf16[96,1536]{1,0:T(8,128)(2,1)}, u32[]{:S(2)}, u32[]{:S(2)}) collective-permute-start(bf16[96,1536]{1,0:T(8,128)(2,1)} %refs_1_.3), channel_id=1, source_target_pairs={{0,1},{1,0},{2,3},{3,2},{4,5},{5,4},{6,7},{7,6},{8,9},{9,8},{10,11... | collective-permute-start | bytes 884744 | tf_op jit(solution)/shard_map/ppermute | solution.py:388
  43.2 2.6 %collective-permute-start.10 = (bf16[96,1536]{1,0:T(8,128)(2,1)}, bf16[96,1536]{1,0:T(8,128)(2,1)}, u32[]{:S(2)}, u32[]{:S(2)}) collective-permute-start(bf16[96,1536]{1,0:T(8,128)(2,1)} %collective-permute-done.1.refs_4_), channel_id=1, source_target_pairs={{0,1},{1,0},{2,3},{3,2},{4,5},{5,4},{6,7},{7,6},{8,9},{9,8},{10,11... | collective-permute-start | bytes 884744 | tf_op jit(solution)/shard_map/ppermute | solution.py:388
  43.6 8.9 %collective-permute-start.5 = (bf16[96,1536]{1,0:T(8,128)(2,1)}, bf16[96,1536]{1,0:T(8,128)(2,1)}, u32[]{:S(2)}, u32[]{:S(2)}) collective-permute-start(bf16[96,1536]{1,0:T(8,128)(2,1)} %collective-permute-done.2.refs_6_), channel_id=1, source_target_pairs={{0,16},{16,0},{1,17},{17,1},{2,18},{18,2},{3,19},{19,3},{4,20},{20... | collective-permute-start | bytes 884744 | tf_op jit(solution)/shard_map/ppermute | solution.py:383
  44.9 8.8 %collective-permute-start.8 = (bf16[96,1536]{1,0:T(8,128)(2,1)}, bf16[96,1536]{1,0:T(8,128)(2,1)}, u32[]{:S(2)}, u32[]{:S(2)}) collective-permute-start(bf16[96,1536]{1,0:T(8,128)(2,1)} %collective-permute-done.refs_2_), channel_id=1, source_target_pairs={{0,1},{1,0},{2,3},{3,2},{4,5},{5,4},{6,7},{7,6},{8,9},{9,8},{10,11... | collective-permute-start | bytes 884744 | tf_op jit(solution)/shard_map/ppermute | solution.py:388
  45.2 8.4 %collective-permute-start.12 = (bf16[96,1536]{1,0:T(8,128)(2,1)}, bf16[96,1536]{1,0:T(8,128)(2,1)}, u32[]{:S(2)}, u32[]{:S(2)}) collective-permute-start(bf16[96,1536]{1,0:T(8,128)(2,1)} %collective-permute-done.2.refs_6_), channel_id=1, source_target_pairs={{0,1},{1,0},{2,3},{3,2},{4,5},{5,4},{6,7},{7,6},{8,9},{9,8},{10,11... | collective-permute-start | bytes 884744 | tf_op jit(solution)/shard_map/ppermute | solution.py:388
  45.4 8.3 %collective-permute-start.11 = (bf16[96,1536]{1,0:T(8,128)(2,1)}, bf16[96,1536]{1,0:T(8,128)(2,1)}, u32[]{:S(2)}, u32[]{:S(2)}) collective-permute-start(bf16[96,1536]{1,0:T(8,128)(2,1)} %collective-permute-done.4.refs_5_), channel_id=1, source_target_pairs={{0,1},{1,0},{2,3},{3,2},{4,5},{5,4},{6,7},{7,6},{8,9},{9,8},{10,11... | collective-permute-start | bytes 884744 | tf_op jit(solution)/shard_map/ppermute | solution.py:388
  45.7 7.9 %collective-permute-start.9 = (bf16[96,1536]{1,0:T(8,128)(2,1)}, bf16[96,1536]{1,0:T(8,128)(2,1)}, u32[]{:S(2)}, u32[]{:S(2)}) collective-permute-start(bf16[96,1536]{1,0:T(8,128)(2,1)} %collective-permute-done.3.refs_3_), channel_id=1, source_target_pairs={{0,1},{1,0},{2,3},{3,2},{4,5},{5,4},{6,7},{7,6},{8,9},{9,8},{10,11... | collective-permute-start | bytes 884744 | tf_op jit(solution)/shard_map/ppermute | solution.py:388
  52.5 2.4 %collective-permute-start.13 = (bf16[96,1536]{1,0:T(8,128)(2,1)}, bf16[96,1536]{1,0:T(8,128)(2,1)}, u32[]{:S(2)}, u32[]{:S(2)}) collective-permute-start(bf16[96,1536]{1,0:T(8,128)(2,1)} %collective-permute-done.5.refs_7_), channel_id=1, source_target_pairs={{0,1},{1,0},{2,3},{3,2},{4,5},{5,4},{6,7},{7,6},{8,9},{9,8},{10,11... | collective-permute-start | bytes 884744 | tf_op jit(solution)/shard_map/ppermute | solution.py:388
  54.9 1.0 copy-start.5
  64.0 18.8 %collective-permute-start.14 = (bf16[512,768]{1,0:T(8,128)(2,1)S(1)}, bf16[512,768]{1,0:T(8,128)(2,1)S(1)}, u32[]{:S(2)}, u32[]{:S(2)}) collective-permute-start(bf16[512,768]{1,0:T(8,128)(2,1)S(1)} %get-tuple-element.35), channel_id=1, source_target_pairs={{0,2},{2,0},{1,3},{3,1},{4,6},{6,4},{5,7},{7,5},{8,10},{10,8},{9,1... | collective-permute-start | bytes 2359304 | tf_op jit(solution)/shard_map/ppermute | solution.py:563
  78.3 19.0 %collective-permute-start.16 = (bf16[384,1536]{1,0:T(8,128)(2,1)}, bf16[384,1536]{1,0:T(8,128)(2,1)}, u32[]{:S(2)}, u32[]{:S(2)}) collective-permute-start(bf16[384,1536]{1,0:T(8,128)(2,1)} %convolution_convert_fusion.1), channel_id=1, source_target_pairs={{0,1},{1,0},{2,3},{3,2},{4,5},{5,4},{6,7},{7,6},{8,9},{9,8},{10,11... | collective-permute-start | bytes 3538952 | tf_op jit(solution)/shard_map/ppermute | solution.py:531
  79.5 3.3 %copy-start.3 = (f32[1024,768]{1,0:T(8,128)S(1)}, f32[1024,768]{1,0:T(8,128)}, u32[]{:S(2)}) copy-start(f32[1024,768]{1,0:T(8,128)} %copy-done.2) | copy-start | bytes 9437188
  85.2 1.5 copy-start.8
  85.4 21.7 %collective-permute-start.15 = (bf16[512,384]{1,0:T(8,128)(2,1)S(1)}, bf16[512,384]{1,0:T(8,128)(2,1)}, u32[]{:S(2)}, u32[]{:S(2)}) collective-permute-start(bf16[512,384]{1,0:T(8,128)(2,1)S(1)} %get-tuple-element.53), channel_id=1, source_target_pairs={{0,2},{2,0},{1,3},{3,1},{4,6},{6,4},{5,7},{7,5},{8,10},{10,8},{9,1... | collective-permute-start | bytes 1179656 | tf_op jit(solution)/shard_map/ppermute | solution.py:592
  86.6 25.4 %all-to-all-start = ((bf16[16,48,512]{2,1,0:T(8,128)(2,1)}), bf16[16,48,512]{2,1,0:T(8,128)(2,1)S(1)}, u32[]{:S(2)}, u32[]{:S(2)}) async-start(bf16[16,48,512]{2,1,0:T(8,128)(2,1)} %bitcast.15), calls=%async_computation | async-start | bytes 1572864 | tf_op jit(solution)/shard_map/all_to_all | solution.py:582
  92.4 38.7 %reduce-scatter.5.cloned.1.call-start = ((), (), s32[]{:S(2)}) async-start(), calls=%async_computation.5 | async-start | bytes 1474560 | tf_op jit(solution)/shard_map/reduce_scatter | solution.py:535
  93.6 3.7 %copy-start.9 = (bf16[1024,1536]{1,0:T(8,128)(2,1)S(1)}, bf16[1024,1536]{1,0:T(8,128)(2,1)}, u32[]{:S(2)}) copy-start(bf16[1024,1536]{1,0:T(8,128)(2,1)} %get-tuple-element.47) | copy-start | bytes 9437188
  112.0 0.9 copy-start.10
  118.6 30.5 %all-to-all-start.1 = ((bf16[16,192,128]{2,1,0:T(8,128)(2,1)}), bf16[16,192,128]{2,1,0:T(8,128)(2,1)S(1)}, u32[]{:S(2)}, u32[]{:S(2)}) async-start(bf16[16,192,128]{2,1,0:T(8,128)(2,1)} %bitcast.17), calls=%async_computation.2 | async-start | bytes 1572864 | tf_op jit(solution)/shard_map/all_to_all | solution.py:596
Sparse Core Ops, SparseCore 0:
  41.4 35.6 reduce-scatter.2
  101.1 29.8 reduce-scatter.4

commit v7 on v6

--- a/solution.py
+++ b/solution.py
@@ -12,7 +12,7 @@
 SPANS = ("seq", "sub")
 TEAM = ("seq", "sub", "hid")
 LANES = 128
-ROWS = 128
+ROWS = 256
 SMALL = pl.CostEstimate(flops=1 << 20, bytes_accessed=1 << 16, transcendentals=0)
 
 

time: 159 us -> 159 us (level)
  Pallas kernels: 33.1 us -> 31.2 us
  waiting for transfers between devices: 38.9 us -> 40.8 us
    ppermute x3, waiting for transfers between devices: 8.42 us -> 10.3 us  [weight_pieces(): lax.ppermute(w, 'seq', shift_pairs(chips, d))]
  transfers between devices with their start and end apart: 21 -> 21, of which waited for: 7 -> 8; matrix products, arithmetic and copies ran while one was open for 22% -> 22% of each run, Pallas kernels for 20% -> 18%
where the time goes in v7:
time: 159 us; the launch traced here: 158 us
  waiting for transfers between devices  40.8 us (26%)
  starting transfers between devices  31.8 us (20%)
  Pallas kernels  31.2 us (20%)
  other arithmetic  22.3 us (14%)
  between operations  14.3 us (9%)
  matrix products  12 us (8%)
  local copies, waits for them, and re-layouts  5.72 us (4%)
    all_to_all x1, waiting for transfers between devices, local(): lax.all_to_all(sent_back, TEAM, split_axis=0, concat_axis=0, tiled=True)  16.3 us
    pallas_call x2, Pallas kernels, feed_rows(): pl.pallas_call(functools.partial(feed_kernel, keys, len(flat), shard, chi...  16.1 us
    all_to_all x1, starting transfers between devices, local(): lax.all_to_all(sent_back, TEAM, split_axis=0, concat_axis=0, tiled=True)  10.9 us
    ppermute x3, waiting for transfers between devices, weight_pieces(): lax.ppermute(w, 'seq', shift_pairs(chips, d))  10.3 us
    dot_general x2, matrix products, core_rows(): lax.dot_general(part, right, contract_rows, preferred_element_type=jnp.fl...  8.05 us
    ppermute x3, waiting for transfers between devices, weight_pieces(): lax.ppermute(blocks[0], 'groups', shift_pairs(2, 1))  6.62 us
    all_to_all x1, starting transfers between devices, local(): lax.all_to_all(spectral.reshape(team, 2 * slots, rows), TEAM, split_axis=...  5.74 us
    pallas_call x1, Pallas kernels, position_transform(): pl.pallas_call(functools.partial(position_kernel, spans, hids, slots), gr...  5.74 us
  transfers between devices with their start and end apart: 21, of which 8 were waited for; matrix products, arithmetic and copies ran while one was open for 22% of the time, Pallas kernels for 18%

profile of v7, /device:TPU:1, one launch (start us, length us, event | category | flops | bytes accessed | tf_op | source)
XLA Modules:
  0.0 158.1 jit_solution(6046042368698960297)
XLA Ops:
  7.2 1.7 %broadcast_select_fusion = bf16[96,1536]{1,0:T(8,128)(2,1)} fusion(bf16[96,1536]{1,0:T(8,128)(2,1)} %refs_0_.3, bf16[96,1536]{1,0:T(8,128)(2,1)} %refs_1_.3, pred[]{:T(512)S(6)} %eq.76), kind=kLoop, calls=%fused_computation.29 | loop fusion | flops 147456 | bytes 884737 | tf_op jit(solution)/shard_map/jit(_where)/select_n | solution.py:365
  8.9 2.1 %collective-permute-start = (bf16[96,1536]{1,0:T(8,128)(2,1)}, bf16[96,1536]{1,0:T(8,128)(2,1)}, u32[]{:S(2)}, u32[]{:S(2)}) collective-permute-start(bf16[96,1536]{1,0:T(8,128)(2,1)} %broadcast_select_fusion), channel_id=1, source_target_pairs={{0,4},{4,8},{8,12},{12,0},{1,5},{5,9},{9,13},{13,1},{2,6},{6,10},{... | collective-permute-start | bytes 884744 | tf_op jit(solution)/shard_map/ppermute | solution.py:373
  11.1 2.0 %collective-permute-start.1 = (bf16[96,1536]{1,0:T(8,128)(2,1)}, bf16[96,1536]{1,0:T(8,128)(2,1)}, u32[]{:S(2)}, u32[]{:S(2)}) collective-permute-start(bf16[96,1536]{1,0:T(8,128)(2,1)} %broadcast_select_fusion), channel_id=1, source_target_pairs={{0,12},{4,0},{8,4},{12,8},{1,13},{5,1},{9,5},{13,9},{2,14},{6,2},{... | collective-permute-start | bytes 884744 | tf_op jit(solution)/shard_map/ppermute | solution.py:373
  13.1 0.7 broadcast_in_dim.41.gain_ref
  13.8 3.7 %fusion.5 = bf16[1024,1536]{1,0:T(8,128)(2,1)S(1)} fusion(bf16[1024,1536]{1,0:T(8,128)(2,1)} %pre_act_ref.3), kind=kLoop, calls=%fused_computation.9 | loop fusion | flops 15728640 | bytes 6291456 | tf_op jit(solution)/shard_map/convert_element_type | solution.py:537
  17.5 2.0 %ffn_norm.1 = (f32[1024,768]{1,0:T(8,128)S(1)}, bf16[1024,768]{1,0:T(8,128)(2,1)S(1)}) custom-call(bf16[1024,768]{1,0:T(8,128)(2,1)S(1)} %copy-done.6, bf16[1024,768]{1,0:T(8,128)(2,1)S(1)} %copy-done.7, f32[1,768]{1,0:T(1,128)S(1)} %broadcast_in_dim.41.gain_ref), custom_call_target="tpu_custom_call" | custom-call | flops 1048576 | bytes 65536 | tf_op jit(solution)/shard_map/ffn_norm/pallas_call | solution.py:252
  19.6 1.7 %copy-done.2 = f32[1024,768]{1,0:T(8,128)} copy-done((f32[1024,768]{1,0:T(8,128)}, f32[1024,768]{1,0:T(8,128)S(1)}, u32[]{:S(2)}) %copy-start.2) | copy-done | bytes 3145752
  21.3 4.0 %convolution_convert_fusion = bf16[768,1536]{1,0:T(8,128)(2,1)} fusion(bf16[1024,768]{1,0:T(8,128)(2,1)S(1)} %get-tuple-element.28.x_ref, bf16[1024,1536]{1,0:T(8,128)(2,1)S(1)} %fusion.5), kind=kOutput, calls=%fused_computation.13 | convolution fusion | flops 2417098752 | bytes 7077888 | tf_op jit(solution)/shard_map/dot_general | solution.py:538
  25.3 0.7 collective-permute-done.1.refs_4_
  26.0 0.8 collective-permute-start.2
  26.8 1.0 collective-permute-start.3
  27.8 0.5 collective-permute-start.4
  28.4 0.4 fusion.8.order_ref
  28.9 2.8 %mix_norm.1 = bf16[1024,768]{1,0:T(8,128)(2,1)S(1)} custom-call(bf16[1024,768]{1,0:T(8,128)(2,1)S(1)} %copy-done.1, f32[1,768]{1,0:T(1,128)S(1)} %broadcast_in_dim.42.gain_ref, bf16[768,768]{1,0:T(8,128)(2,1)S(1)} %fusion.8.order_ref), custom_call_target="tpu_custom_call" | custom-call | flops 1048576 | bytes 65536 | tf_op jit(solution)/shard_map/mix_norm/pallas_call | solution.py:275
  31.6 9.6 %collective-permute-done.2.refs_6_ = bf16[96,1536]{1,0:T(8,128)(2,1)} collective-permute-done((bf16[96,1536]{1,0:T(8,128)(2,1)}, bf16[96,1536]{1,0:T(8,128)(2,1)}, u32[]{:S(2)}, u32[]{:S(2)}) %collective-permute-start.2) | collective-permute-done | bytes 294944 | tf_op jit(solution)/shard_map/ppermute | solution.py:373
  41.3 1.8 %collective-permute-start.6 = (bf16[96,1536]{1,0:T(8,128)(2,1)S(1)}, bf16[96,1536]{1,0:T(8,128)(2,1)}, u32[]{:S(2)}, u32[]{:S(2)}) collective-permute-start(bf16[96,1536]{1,0:T(8,128)(2,1)S(1)} %copy-done.4), channel_id=1, source_target_pairs={{0,1},{1,0},{2,3},{3,2},{4,5},{5,4},{6,7},{7,6},{8,9},{9,8},{10,11... | collective-permute-start | bytes 884744 | tf_op jit(solution)/shard_map/ppermute | solution.py:388
  43.2 0.4 collective-permute-start.10
  43.6 1.3 collective-permute-start.5
  45.9 6.6 %collective-permute-done.5.refs_7_ = bf16[96,1536]{1,0:T(8,128)(2,1)} collective-permute-done((bf16[96,1536]{1,0:T(8,128)(2,1)}, bf16[96,1536]{1,0:T(8,128)(2,1)}, u32[]{:S(2)}, u32[]{:S(2)}) %collective-permute-start.5) | collective-permute-done | bytes 294944 | tf_op jit(solution)/shard_map/ppermute | solution.py:383
  52.5 0.8 collective-permute-start.13
  53.7 1.2 collective-permute-done.13.refs_15_
  54.9 1.0 copy-done.5
  55.9 8.1 %feed_rows.2 = (bf16[1024,1536]{1,0:T(8,128)(2,1)}, bf16[512,768]{1,0:T(8,128)(2,1)S(1)}) custom-call(s32[4]{0:T(128)S(1)} %pad_add_fusion.where_ref, bf16[1024,768]{1,0:T(8,128)(2,1)} %copy-done, bf16[1024,1536]{1,0:T(8,128)(2,1)} %pre_act_ref.3, bf16[96,1536]{1,0:T(8,128)(2,1)S(1)} %copy-done.4, bf16[96,1536]{1,0:T(8,128)(2,1)S(1)} %copy-done.5, ...), custom_call_target="tpu_custom_call" | custom-call | flops 1048576 | bytes 65536 | tf_op jit(solution)/shard_map/feed_rows/pallas_call | solution.py:442
  63.9 1.3 collective-permute-start.14
  65.2 8.1 %feed_rows.3 = (bf16[1024,1536]{1,0:T(8,128)(2,1)}, bf16[512,768]{1,0:T(8,128)(2,1)S(1)}) custom-call(s32[4]{0:T(128)S(1)} %pad_add_fusion.where_ref, bf16[1024,768]{1,0:T(8,128)(2,1)} %copy-done, bf16[1024,1536]{1,0:T(8,128)(2,1)} %pre_act_ref.3, bf16[96,1536]{1,0:T(8,128)(2,1)S(1)} %copy-done.4, ...), custom_call_target="tpu_custom_call", output_to_operand_aliasing={{0}: (19, {})} | custom-call | flops 1048576 | bytes 65536 | tf_op jit(solution)/shard_map/feed_rows/pallas_call | solution.py:442
  73.7 4.4 %convolution_convert_fusion.1 = bf16[384,1536]{1,0:T(8,128)(2,1)} fusion(bf16[1024,1536]{1,0:T(8,128)(2,1)} %get-tuple-element.47, bf16[1024,768]{1,0:T(8,128)(2,1)S(1)} %mix_norm.1), kind=kOutput, calls=%fused_computation.16 | convolution fusion | flops 1208549376 | bytes 5111808 | tf_op jit(solution)/shard_map/dot_general | solution.py:523
  78.3 0.7 collective-permute-start.16
  79.0 0.4 multiply_subtract_fusion
  79.9 2.9 %collective-permute-done.14.refs_1_ = bf16[512,768]{1,0:T(8,128)(2,1)S(1)} collective-permute-done((bf16[512,768]{1,0:T(8,128)(2,1)S(1)}, bf16[512,768]{1,0:T(8,128)(2,1)S(1)}, u32[]{:S(2)}, u32[]{:S(2)}) %collective-permute-start.14) | collective-permute-done | bytes 786464 | tf_op jit(solution)/shard_map/ppermute | solution.py:563
  82.8 2.4 %mix_rows.1 = (bf16[512,768]{1,0:T(8,128)(2,1)S(1)}, bf16[768,512]{1,0:T(8,128)(2,1)S(1)}) custom-call(s32[4]{0:T(128)S(1)} %pad_add_fusion.where_ref, bf16[1024,768]{1,0:T(8,128)(2,1)S(1)} %copy-done.1, f32[1024,768]{1,0:T(8,128)S(1)} %copy-done.3, f32[1,768]{1,0:T(1,128)S(1)} %broadcast_in_dim.42.gain_ref, bf16[768,768]{1,0:T(8,128)(2,1)S(1)} %fusion.7.tab_ref, ...), custom_call_target="tpu_custom_call" | custom-call | flops 1048576 | bytes 65536 | tf_op jit(solution)/shard_map/mix_rows/pallas_call | solution.py:337
  85.4 1.2 collective-permute-start.15
  86.6 5.7 %all-to-all-start = ((bf16[16,48,512]{2,1,0:T(8,128)(2,1)}), bf16[16,48,512]{2,1,0:T(8,128)(2,1)S(1)}, u32[]{:S(2)}, u32[]{:S(2)}) async-start(bf16[16,48,512]{2,1,0:T(8,128)(2,1)} %bitcast.15), calls=%async_computation | async-start | bytes 1572864 | tf_op jit(solution)/shard_map/all_to_all | solution.py:582
  92.5 1.1 fusion.27
  93.6 3.7 %subtract_convert_fusion.1 = (bf16[1,32,32,1024]{3,2,1,0:T(8,128)(2,1)}, bf16[1,32,32,1024]{3,2,1,0:T(8,128)(2,1)}) fusion(f32[32,1024]{1,0:T(8,128)S(1)} %get-tuple-element.70, f32[32,1024]{1,0:T(8,128)S(1)} %get-tuple-element.59, f32[32,1024]{1,0:T(8,128)S(1)} %get-tuple-element.71, f32[32,1024]{1,0:T(8,128)S(1)} %get-tuple-element.61, ...), kind=kLoop, calls=%fused_computation.12 | loop fusion | flops 8388608 | bytes 4849664 | tf_op jit(solution)/shard_map/convert
  97.3 3.7 %fusion.6 = bf16[384,1536]{1,0:T(8,128)(2,1)} fusion(bf16[1024,1536]{1,0:T(8,128)(2,1)S(1)} %copy-done.9, bf16[384,1536]{1,0:T(8,128)(2,1)} %collective-permute-done.16, bf16[1024,768]{1,0:T(8,128)(2,1)S(1)} %mix_norm.1), kind=kOutput, calls=%fused_computation.15 | convolution fusion | flops 1209729024 | bytes 6291456 | tf_op jit(solution)/shard_map/dot_general | solution.py:523
  101.0 4.6 %pad_maximum_fusion = bf16[2,32,32,1024]{3,2,1,0:T(8,128)(2,1)} fusion(bf16[1,32,32,1024]{3,2,1,0:T(8,128)(2,1)} %get-tuple-element.56, bf16[1,32,32,1024]{3,2,1,0:T(8,128)(2,1)} %get-tuple-element.55), kind=kLoop, calls=%fused_computation.10 | loop fusion | flops 2097152 | bytes 8388608 | tf_op jit(solution)/shard_map/stack | solution.py:72
  105.6 0.6 fusion.42.mark_ref
  106.4 0.6 maximum_multiply_fusion.twist_ref
  107.1 1.1 constant_dynamic-update-slice_fusion.own_ref
  108.2 1.8 %convert_element_type.123 = f32[96,1536]{1,0:T(8,128)} convert(bf16[96,1536]{1,0:T(8,128)(2,1)} %reduce-scatter.3.cloned.1.call-done) | non-fusion elementwise | flops 147456 | bytes 884736 | tf_op jit(solution)/shard_map/convert_element_type | solution.py:540
  110.0 2.0 %all-to-all-done.x_ref = bf16[16,48,512]{2,1,0:T(8,128)(2,1)S(1)} async-done(((bf16[16,48,512]{2,1,0:T(8,128)(2,1)}), bf16[16,48,512]{2,1,0:T(8,128)(2,1)S(1)}, u32[]{:S(2)}, u32[]{:S(2)}) %all-to-all-start) | async-done | bytes 786464 | tf_op jit(solution)/shard_map/all_to_all | solution.py:582
  112.0 0.9 copy-done.10
  112.9 5.7 %position_transform.1 = bf16[8,2,192,128]{3,2,1,0:T(8,128)(2,1)} custom-call(bf16[16,48,512]{2,1,0:T(8,128)(2,1)} %copy-done.10, f32[24,1]{1,0:T(8,128)} %fusion.42.mark_ref, f32[2,8,1024]{2,1,0:T(8,128)} %maximum_multiply_fusion.twist_ref, bf16[2048,1024]{1,0:T(8,128)(2,1)} %bitcast.16), custom_call_target="tpu_custom_call" | custom-call | flops 1610612736 | bytes 6291456 | tf_op jit(solution)/shard_map/position_transform/pallas_call | solution.py:163
  118.6 10.9 %all-to-all-start.1 = ((bf16[16,192,128]{2,1,0:T(8,128)(2,1)}), bf16[16,192,128]{2,1,0:T(8,128)(2,1)S(1)}, u32[]{:S(2)}, u32[]{:S(2)}) async-start(bf16[16,192,128]{2,1,0:T(8,128)(2,1)} %bitcast.17), calls=%async_computation.2 | async-start | bytes 1572864 | tf_op jit(solution)/shard_map/all_to_all | solution.py:596
  129.7 1.4 reduce-scatter.5.cloned.1.call-done
  131.1 1.8 %convert_element_type.131 = f32[96,1536]{1,0:T(8,128)} convert(bf16[96,1536]{1,0:T(8,128)(2,1)} %reduce-scatter.5.cloned.1.call-done) | non-fusion elementwise | flops 147456 | bytes 884736 | tf_op jit(solution)/shard_map/convert_element_type | solution.py:535
  132.9 16.3 %all-to-all-done.1.back_ref = bf16[16,192,128]{2,1,0:T(8,128)(2,1)S(1)} async-done(((bf16[16,192,128]{2,1,0:T(8,128)(2,1)}), bf16[16,192,128]{2,1,0:T(8,128)(2,1)S(1)}, u32[]{:S(2)}, u32[]{:S(2)}) %all-to-all-start.1) | async-done | bytes 786464 | tf_op jit(solution)/shard_map/all_to_all | solution.py:596
  149.2 2.1 %finish.1 = f32[1024,384]{1,0:T(8,128)} custom-call(bf16[16,192,128]{2,1,0:T(8,128)(2,1)S(1)} %all-to-all-done.1.back_ref, bf16[384,384]{1,0:T(8,128)(2,1)S(1)} %fusion.11.pick_ref, bf16[1024,384]{1,0:T(8,128)(2,1)S(1)} %constant_dynamic-update-slice_fusion.own_ref), custom_call_target="tpu_custom_call" | custom-call | flops 301989888 | bytes 5242880 | tf_op jit(solution)/shard_map/finish/pallas_call | solution.py:223
  (70 shorter events, 3.4 us)
Async XLA Ops:
  7.2 101.0 %reduce-scatter.3.cloned.1.call-start = ((), (), s32[]{:S(2)}) async-start(), calls=%async_computation.4 | async-start | bytes 2654208 | tf_op jit(solution)/shard_map/reduce_scatter | solution.py:540
  8.9 16.4 %collective-permute-start = (bf16[96,1536]{1,0:T(8,128)(2,1)}, bf16[96,1536]{1,0:T(8,128)(2,1)}, u32[]{:S(2)}, u32[]{:S(2)}) collective-permute-start(bf16[96,1536]{1,0:T(8,128)(2,1)} %broadcast_select_fusion), channel_id=1, source_target_pairs={{0,4},{4,8},{8,12},{12,0},{1,5},{5,9},{9,13},{13,1},{2,6},{6,10},{... | collective-permute-start | bytes 884744 | tf_op jit(solution)/shard_map/ppermute | solution.py:373
  11.1 14.9 %collective-permute-start.1 = (bf16[96,1536]{1,0:T(8,128)(2,1)}, bf16[96,1536]{1,0:T(8,128)(2,1)}, u32[]{:S(2)}, u32[]{:S(2)}) collective-permute-start(bf16[96,1536]{1,0:T(8,128)(2,1)} %broadcast_select_fusion), channel_id=1, source_target_pairs={{0,12},{4,0},{8,4},{12,8},{1,13},{5,1},{9,5},{13,9},{2,14},{6,2},{... | collective-permute-start | bytes 884744 | tf_op jit(solution)/shard_map/ppermute | solution.py:373
  13.8 3.7 %copy-start.6 = (bf16[1024,768]{1,0:T(8,128)(2,1)S(1)}, bf16[1024,768]{1,0:T(8,128)(2,1)}, u32[]{:S(2)}) copy-start(bf16[1024,768]{1,0:T(8,128)(2,1)} %z_ref.3) | copy-start | bytes 4718596
  13.8 3.8 %copy-start.7 = (bf16[1024,768]{1,0:T(8,128)(2,1)S(1)}, bf16[1024,768]{1,0:T(8,128)(2,1)}, u32[]{:S(2)}) copy-start(bf16[1024,768]{1,0:T(8,128)(2,1)} %up_ref.1) | copy-start | bytes 4718596
  19.6 1.7 %copy-start.2 = (f32[1024,768]{1,0:T(8,128)}, f32[1024,768]{1,0:T(8,128)S(1)}, u32[]{:S(2)}) copy-start(f32[1024,768]{1,0:T(8,128)S(1)} %get-tuple-element.37.ffn_ref) | copy-start | bytes 9437188
  21.3 4.0 %copy-start = (bf16[1024,768]{1,0:T(8,128)(2,1)}, bf16[1024,768]{1,0:T(8,128)(2,1)S(1)}, u32[]{:S(2)}) copy-start(bf16[1024,768]{1,0:T(8,128)(2,1)S(1)} %get-tuple-element.28.x_ref) | copy-start | bytes 4718596
  21.3 7.1 %copy-start.11 = (f32[768]{0:T(1024)S(1)}, f32[768]{0:T(1024)}, u32[]{:S(2)}) copy-start(f32[768]{0:T(1024)} %param.12) | copy-start | bytes 9220
  21.3 7.6 %copy-start.1 = (bf16[1024,768]{1,0:T(8,128)(2,1)S(1)}, bf16[1024,768]{1,0:T(8,128)(2,1)}, u32[]{:S(2)}) copy-start(bf16[1024,768]{1,0:T(8,128)(2,1)} %z_ref.5) | copy-start | bytes 4718596
  26.0 15.2 %collective-permute-start.2 = (bf16[96,1536]{1,0:T(8,128)(2,1)}, bf16[96,1536]{1,0:T(8,128)(2,1)}, u32[]{:S(2)}, u32[]{:S(2)}) collective-permute-start(bf16[96,1536]{1,0:T(8,128)(2,1)} %broadcast_select_fusion), channel_id=1, source_target_pairs={{0,8},{4,12},{8,0},{12,4},{1,9},{5,13},{9,1},{13,5},{2,10},{6,14},... | collective-permute-start | bytes 884744 | tf_op jit(solution)/shard_map/ppermute | solution.py:373
  26.8 14.4 %collective-permute-start.3 = (bf16[96,1536]{1,0:T(8,128)(2,1)}, bf16[96,1536]{1,0:T(8,128)(2,1)}, u32[]{:S(2)}, u32[]{:S(2)}) collective-permute-start(bf16[96,1536]{1,0:T(8,128)(2,1)} %collective-permute-done.refs_2_), channel_id=1, source_target_pairs={{0,16},{16,0},{1,17},{17,1},{2,18},{18,2},{3,19},{19,3},{4,20},{20... | collective-permute-start | bytes 884744 | tf_op jit(solution)/shard_map/ppermute | solution.py:383
  27.8 13.4 %collective-permute-start.4 = (bf16[96,1536]{1,0:T(8,128)(2,1)}, bf16[96,1536]{1,0:T(8,128)(2,1)}, u32[]{:S(2)}, u32[]{:S(2)}) collective-permute-start(bf16[96,1536]{1,0:T(8,128)(2,1)} %collective-permute-done.1.refs_4_), channel_id=1, source_target_pairs={{0,16},{16,0},{1,17},{17,1},{2,18},{18,2},{3,19},{19,3},{4,20},{20... | collective-permute-start | bytes 884744 | tf_op jit(solution)/shard_map/ppermute | solution.py:383
  28.8 12.4 %copy-start.4 = (bf16[96,1536]{1,0:T(8,128)(2,1)S(1)}, bf16[96,1536]{1,0:T(8,128)(2,1)}, u32[]{:S(2)}) copy-start(bf16[96,1536]{1,0:T(8,128)(2,1)} %refs_0_.3) | copy-start | bytes 884740
  41.3 3.9 %collective-permute-start.6 = (bf16[96,1536]{1,0:T(8,128)(2,1)S(1)}, bf16[96,1536]{1,0:T(8,128)(2,1)}, u32[]{:S(2)}, u32[]{:S(2)}) collective-permute-start(bf16[96,1536]{1,0:T(8,128)(2,1)S(1)} %copy-done.4), channel_id=1, source_target_pairs={{0,1},{1,0},{2,3},{3,2},{4,5},{5,4},{6,7},{7,6},{8,9},{9,8},{10,11... | collective-permute-start | bytes 884744 | tf_op jit(solution)/shard_map/ppermute | solution.py:388
  43.1 2.3 %collective-permute-start.7 = (bf16[96,1536]{1,0:T(8,128)(2,1)}, bf16[96,1536]{1,0:T(8,128)(2,1)}, u32[]{:S(2)}, u32[]{:S(2)}) collective-permute-start(bf16[96,1536]{1,0:T(8,128)(2,1)} %refs_1_.3), channel_id=1, source_target_pairs={{0,1},{1,0},{2,3},{3,2},{4,5},{5,4},{6,7},{7,6},{8,9},{9,8},{10,11... | collective-permute-start | bytes 884744 | tf_op jit(solution)/shard_map/ppermute | solution.py:388
  43.2 2.6 %collective-permute-start.10 = (bf16[96,1536]{1,0:T(8,128)(2,1)}, bf16[96,1536]{1,0:T(8,128)(2,1)}, u32[]{:S(2)}, u32[]{:S(2)}) collective-permute-start(bf16[96,1536]{1,0:T(8,128)(2,1)} %collective-permute-done.1.refs_4_), channel_id=1, source_target_pairs={{0,1},{1,0},{2,3},{3,2},{4,5},{5,4},{6,7},{7,6},{8,9},{9,8},{10,11... | collective-permute-start | bytes 884744 | tf_op jit(solution)/shard_map/ppermute | solution.py:388
  43.6 8.9 %collective-permute-start.5 = (bf16[96,1536]{1,0:T(8,128)(2,1)}, bf16[96,1536]{1,0:T(8,128)(2,1)}, u32[]{:S(2)}, u32[]{:S(2)}) collective-permute-start(bf16[96,1536]{1,0:T(8,128)(2,1)} %collective-permute-done.2.refs_6_), channel_id=1, source_target_pairs={{0,16},{16,0},{1,17},{17,1},{2,18},{18,2},{3,19},{19,3},{4,20},{20... | collective-permute-start | bytes 884744 | tf_op jit(solution)/shard_map/ppermute | solution.py:383
  44.8 8.8 %collective-permute-start.8 = (bf16[96,1536]{1,0:T(8,128)(2,1)}, bf16[96,1536]{1,0:T(8,128)(2,1)}, u32[]{:S(2)}, u32[]{:S(2)}) collective-permute-start(bf16[96,1536]{1,0:T(8,128)(2,1)} %collective-permute-done.refs_2_), channel_id=1, source_target_pairs={{0,1},{1,0},{2,3},{3,2},{4,5},{5,4},{6,7},{7,6},{8,9},{9,8},{10,11... | collective-permute-start | bytes 884744 | tf_op jit(solution)/shard_map/ppermute | solution.py:388
  45.2 8.4 %collective-permute-start.12 = (bf16[96,1536]{1,0:T(8,128)(2,1)}, bf16[96,1536]{1,0:T(8,128)(2,1)}, u32[]{:S(2)}, u32[]{:S(2)}) collective-permute-start(bf16[96,1536]{1,0:T(8,128)(2,1)} %collective-permute-done.2.refs_6_), channel_id=1, source_target_pairs={{0,1},{1,0},{2,3},{3,2},{4,5},{5,4},{6,7},{7,6},{8,9},{9,8},{10,11... | collective-permute-start | bytes 884744 | tf_op jit(solution)/shard_map/ppermute | solution.py:388
  45.4 8.3 %collective-permute-start.11 = (bf16[96,1536]{1,0:T(8,128)(2,1)}, bf16[96,1536]{1,0:T(8,128)(2,1)}, u32[]{:S(2)}, u32[]{:S(2)}) collective-permute-start(bf16[96,1536]{1,0:T(8,128)(2,1)} %collective-permute-done.4.refs_5_), channel_id=1, source_target_pairs={{0,1},{1,0},{2,3},{3,2},{4,5},{5,4},{6,7},{7,6},{8,9},{9,8},{10,11... | collective-permute-start | bytes 884744 | tf_op jit(solution)/shard_map/ppermute | solution.py:388
  45.7 7.9 %collective-permute-start.9 = (bf16[96,1536]{1,0:T(8,128)(2,1)}, bf16[96,1536]{1,0:T(8,128)(2,1)}, u32[]{:S(2)}, u32[]{:S(2)}) collective-permute-start(bf16[96,1536]{1,0:T(8,128)(2,1)} %collective-permute-done.3.refs_3_), channel_id=1, source_target_pairs={{0,1},{1,0},{2,3},{3,2},{4,5},{5,4},{6,7},{7,6},{8,9},{9,8},{10,11... | collective-permute-start | bytes 884744 | tf_op jit(solution)/shard_map/ppermute | solution.py:388
  52.5 2.4 %collective-permute-start.13 = (bf16[96,1536]{1,0:T(8,128)(2,1)}, bf16[96,1536]{1,0:T(8,128)(2,1)}, u32[]{:S(2)}, u32[]{:S(2)}) collective-permute-start(bf16[96,1536]{1,0:T(8,128)(2,1)} %collective-permute-done.5.refs_7_), channel_id=1, source_target_pairs={{0,1},{1,0},{2,3},{3,2},{4,5},{5,4},{6,7},{7,6},{8,9},{9,8},{10,11... | collective-permute-start | bytes 884744 | tf_op jit(solution)/shard_map/ppermute | solution.py:388
  54.9 1.0 copy-start.5
  63.9 18.8 %collective-permute-start.14 = (bf16[512,768]{1,0:T(8,128)(2,1)S(1)}, bf16[512,768]{1,0:T(8,128)(2,1)S(1)}, u32[]{:S(2)}, u32[]{:S(2)}) collective-permute-start(bf16[512,768]{1,0:T(8,128)(2,1)S(1)} %get-tuple-element.35), channel_id=1, source_target_pairs={{0,2},{2,0},{1,3},{3,1},{4,6},{6,4},{5,7},{7,5},{8,10},{10,8},{9,1... | collective-permute-start | bytes 2359304 | tf_op jit(solution)/shard_map/ppermute | solution.py:563
  78.3 19.0 %collective-permute-start.16 = (bf16[384,1536]{1,0:T(8,128)(2,1)}, bf16[384,1536]{1,0:T(8,128)(2,1)}, u32[]{:S(2)}, u32[]{:S(2)}) collective-permute-start(bf16[384,1536]{1,0:T(8,128)(2,1)} %convolution_convert_fusion.1), channel_id=1, source_target_pairs={{0,1},{1,0},{2,3},{3,2},{4,5},{5,4},{6,7},{7,6},{8,9},{9,8},{10,11... | collective-permute-start | bytes 3538952 | tf_op jit(solution)/shard_map/ppermute | solution.py:531
  79.4 3.3 %copy-start.3 = (f32[1024,768]{1,0:T(8,128)S(1)}, f32[1024,768]{1,0:T(8,128)}, u32[]{:S(2)}) copy-start(f32[1024,768]{1,0:T(8,128)} %copy-done.2) | copy-start | bytes 9437188
  85.1 1.5 copy-start.8
  85.4 21.7 %collective-permute-start.15 = (bf16[512,384]{1,0:T(8,128)(2,1)S(1)}, bf16[512,384]{1,0:T(8,128)(2,1)}, u32[]{:S(2)}, u32[]{:S(2)}) collective-permute-start(bf16[512,384]{1,0:T(8,128)(2,1)S(1)} %get-tuple-element.53), channel_id=1, source_target_pairs={{0,2},{2,0},{1,3},{3,1},{4,6},{6,4},{5,7},{7,5},{8,10},{10,8},{9,1... | collective-permute-start | bytes 1179656 | tf_op jit(solution)/shard_map/ppermute | solution.py:592
  86.6 25.4 %all-to-all-start = ((bf16[16,48,512]{2,1,0:T(8,128)(2,1)}), bf16[16,48,512]{2,1,0:T(8,128)(2,1)S(1)}, u32[]{:S(2)}, u32[]{:S(2)}) async-start(bf16[16,48,512]{2,1,0:T(8,128)(2,1)} %bitcast.15), calls=%async_computation | async-start | bytes 1572864 | tf_op jit(solution)/shard_map/all_to_all | solution.py:582
  92.4 38.7 %reduce-scatter.5.cloned.1.call-start = ((), (), s32[]{:S(2)}) async-start(), calls=%async_computation.5 | async-start | bytes 1474560 | tf_op jit(solution)/shard_map/reduce_scatter | solution.py:535
  93.6 3.7 %copy-start.9 = (bf16[1024,1536]{1,0:T(8,128)(2,1)S(1)}, bf16[1024,1536]{1,0:T(8,128)(2,1)}, u32[]{:S(2)}) copy-start(bf16[1024,1536]{1,0:T(8,128)(2,1)} %get-tuple-element.47) | copy-start | bytes 9437188
  112.0 0.9 copy-start.10
  118.6 30.5 %all-to-all-start.1 = ((bf16[16,192,128]{2,1,0:T(8,128)(2,1)}), bf16[16,192,128]{2,1,0:T(8,128)(2,1)S(1)}, u32[]{:S(2)}, u32[]{:S(2)}) async-start(bf16[16,192,128]{2,1,0:T(8,128)(2,1)} %bitcast.17), calls=%async_computation.2 | async-start | bytes 1572864 | tf_op jit(solution)/shard_map/all_to_all | solution.py:596
Sparse Core Ops, SparseCore 0:
  41.4 35.7 reduce-scatter.2
  101.1 29.8 reduce-scatter.4
